TPU v7x, 512 devices: a whole 4x8x8 slice. The times are simulated.
512 devices in a mesh: vec: 32 (over y_lo, x, core), row: 16 (over y_hi, z).
Axes of the slice: x: 4, y: 8 (y_hi: 2, y_lo: 4; y = y_hi * 4 + y_lo), z: 8, core: 2. Of those that a mesh axis runs over, the one named last changes fastest.
Arguments:
- diag_blocks: float32 [128, 256, 256], P('row'), may hold values from -0.475 to 0.475, as said below
- coupling: float32 [128, 256, 256], P('row'), may hold values from -0.078125 to 0.078125
- vectors: float32 [1024, 32768], P('vec', 'row'), may hold values from -3600 to 3600
Outputs:
- filtered: float32 [1024, 32768], P('vec', 'row')
Inputs may be any that keep to these rules, and one draw needn't show every extreme that they name: `diag_blocks`: each block is symmetric.
All inputs are finite; a program needn't handle non-finite values.
Results may differ from a plain program's by a relative error of at most 0.0001.
Values sent between devices are 32-bit elements; how exact they have to be, the bound alone decides.
No kernel may reach another device: no remote copies, remote signals or barrier semaphores. Data moves between devices by JAX's collectives and lax.ppermute only.
A program may use at most 64 MiB of HBM per device.

v0:
```python
import jax
import jax.numpy as jnp
from jax import lax
from jax.sharding import PartitionSpec as P

DEGREE = 4


filter_center = 0.1
filter_half = 1.0
epsilon = 1e-06
highest = lax.Precision.HIGHEST


def with_halo(block, sides, width):
    for axis, dim in sides:
        count = lax.axis_size(axis)
        forward = [(i, i + 1) for i in range(count - 1)]
        backward = [(target, source) for source, target in forward]
        low = lax.ppermute(
            lax.slice_in_dim(block, block.shape[dim] - width, None, axis=dim), axis, forward
        )
        high = lax.ppermute(lax.slice_in_dim(block, 0, width, axis=dim), axis, backward)
        block = jnp.concatenate([low, block, high], axis=dim)
    return block


def apply_operator(panel, diag_blocks, coupling):
    vec_count = panel.shape[0]
    block_size = diag_blocks.shape[1]
    block_count = diag_blocks.shape[0]
    last_term = jnp.dot(panel[:, -block_size:], coupling[-1], precision=highest)
    edge_pieces = jnp.concatenate([panel[:, :block_size], last_term], axis=1)
    ghosts = with_halo(edge_pieces, (("row", 1),), block_size)
    from_below = ghosts[:, :block_size]
    from_above = ghosts[:, -block_size:]
    blocks = panel.reshape(vec_count, block_count, block_size)
    result = jnp.einsum("vnk,njk->vnj", blocks, diag_blocks, precision=highest)
    upper_next = jnp.concatenate([blocks[:, 1:], from_above[:, None, :]], axis=1)
    result = result + jnp.einsum("vnk,njk->vnj", upper_next, coupling, precision=highest)
    lower_local = jnp.einsum("vnk,nkj->vnj", blocks[:, :-1], coupling[:-1], precision=highest)
    lower_all = jnp.concatenate([from_below[:, None, :], lower_local], axis=1)
    result = result + lower_all
    return result.reshape(panel.shape)


def scaled_apply(panel, diag_blocks, coupling):
    return (apply_operator(panel, diag_blocks, coupling) - filter_center * panel) / filter_half


def local(diag_blocks, coupling, vectors):
    previous = vectors
    current = scaled_apply(vectors, diag_blocks, coupling)
    for turn_index in range(DEGREE - 1):
        following = 2.0 * scaled_apply(current, diag_blocks, coupling) - previous
        previous = current
        current = following
    total_rows = current.shape[1] * lax.axis_size("row")
    stacked = lax.all_to_all(current, "vec", split_axis=1, concat_axis=0, tiled=True)
    partial_value = lax.dot_general(stacked, stacked, (((1,), (1,)), ((), ())), precision=highest)
    gram_sum = lax.psum(partial_value, ("vec", "row"))
    scales = 1.0 / jnp.sqrt(jnp.diagonal(gram_sum) / total_rows + epsilon)
    normalized = gram_sum * scales[:, None] * scales[None, :] / total_rows
    mixing = (1.5 * jnp.eye(gram_sum.shape[0], dtype=jnp.float32) - 0.5 * normalized) * scales[
        None, :
    ]
    renewed = jnp.dot(mixing, stacked, precision=highest)
    return lax.all_to_all(renewed, "vec", split_axis=0, concat_axis=1, tiled=True)


def solution(mesh):
    placed = (P("row", None, None), P("row", None, None), P("vec", "row"))
    return jax.shard_map(
        local, mesh=mesh, in_specs=placed, out_specs=P("vec", "row"), check_vma=False
    )
```

profile of v0, /device:TPU:1, one launch (start us, length us, event | category | flops | bytes accessed | tf_op | source)
XLA Modules:
  0.0 452.5 jit_solution(7985964633548466365)
XLA Ops:
  6.5 0.0 copy-start
  6.5 0.0 all-reduce.2.cloned.1.call-start
  6.5 0.0 copy-start.1
  6.5 0.9 slice.61
  7.5 1.4 collective-permute-start
  8.9 1.2 fusion.45
  10.1 5.4 %collective-permute-start.1 = (f32[32,256]{1,0:T(8,128)S(1)}, f32[32,256]{1,0:T(8,128)S(1)}, u32[]{:S(2)}, u32[]{:S(2)}) collective-permute-start(f32[32,256]{1,0:T(8,128)S(1)} %fusion.45), channel_id=1, source_target_pairs={{0,1},{1,2},{2,3},{3,4},{4,5},{5,6},{6,7},{7,8},{8,9},{9,10},{10,1... | collective-permute-start | bytes 98312 | tf_op jit(solution)/shard_map/ppermute | solution.py:20
  15.5 1.0 copy.60
  16.5 0.0 copy-done
  16.5 3.0 convolution_bitcast_fusion.1
  19.5 0.0 copy-done.1
  19.5 1.2 convolution_bitcast_fusion.2
  20.7 0.0 copy-start.2
  20.8 0.0 collective-permute-done
  20.8 0.0 collective-permute-done.1
  20.8 2.0 fusion.17
  22.9 0.0 copy-done.2
  22.9 0.2 fusion.43
  23.2 2.0 fusion.60
  25.2 1.3 collective-permute-start.2
  26.5 4.6 %collective-permute-start.3 = (f32[32,256]{1,0:T(8,128)S(1)}, f32[32,256]{1,0:T(8,128)S(1)}, u32[]{:S(2)}, u32[]{:S(2)}) collective-permute-start(f32[32,256]{1,0:T(8,128)S(1)} %fusion.43), channel_id=1, source_target_pairs={{0,1},{1,2},{2,3},{3,4},{4,5},{5,6},{6,7},{7,8},{8,9},{9,10},{10,1... | collective-permute-start | bytes 98312 | tf_op jit(solution)/shard_map/ppermute | solution.py:20
  31.1 1.1 fusion.21
  32.3 0.0 collective-permute-done.2
  32.3 0.0 collective-permute-done.3
  32.3 2.0 fusion.14
  34.4 0.2 fusion.41
  34.7 2.0 fusion.61
  36.7 1.3 collective-permute-start.4
  38.0 4.8 %collective-permute-start.5 = (f32[32,256]{1,0:T(8,128)S(1)}, f32[32,256]{1,0:T(8,128)S(1)}, u32[]{:S(2)}, u32[]{:S(2)}) collective-permute-start(f32[32,256]{1,0:T(8,128)S(1)} %fusion.41), channel_id=1, source_target_pairs={{0,1},{1,2},{2,3},{3,4},{4,5},{5,6},{6,7},{7,8},{8,9},{9,10},{10,1... | collective-permute-start | bytes 98312 | tf_op jit(solution)/shard_map/ppermute | solution.py:20
  42.8 1.1 fusion.24
  44.0 0.0 collective-permute-done.4
  44.0 0.0 collective-permute-done.5
  44.0 2.0 fusion.11
  46.1 0.2 fusion.39
  46.4 2.0 fusion.62
  48.4 1.3 collective-permute-start.6
  49.7 5.8 %collective-permute-start.7 = (f32[32,256]{1,0:T(8,128)S(1)}, f32[32,256]{1,0:T(8,128)S(1)}, u32[]{:S(2)}, u32[]{:S(2)}) collective-permute-start(f32[32,256]{1,0:T(8,128)S(1)} %fusion.39), channel_id=1, source_target_pairs={{0,1},{1,2},{2,3},{3,4},{4,5},{5,6},{6,7},{7,8},{8,9},{9,10},{10,1... | collective-permute-start | bytes 98312 | tf_op jit(solution)/shard_map/ppermute | solution.py:20
  55.5 1.1 fusion.18
  56.7 0.0 collective-permute-done.6
  56.7 0.0 collective-permute-done.7
  56.7 2.0 fusion.8
  58.8 0.2 all_to_all.26
  59.1 0.3 copy.61
  59.4 0.3 reshape.56
  59.7 21.1 %all_to_all.35 = f32[32,1,2048]{2,1,0:T(1,128)S(1)} all-to-all(f32[32,1,2048]{2,1,0:T(1,128)S(1)} %reshape.56), channel_id=1, replica_groups=mesh['vec'=32,'row'=16] {'vec'}, dimensions={0} | all-to-all | bytes 524288 | tf_op jit(solution)/shard_map/all_to_all | solution.py:59
  80.8 0.5 broadcast.61
  81.3 1.3 reduce
  82.6 0.2 reshape.57
  82.8 5.0 %fusion.63 = f32[1024,1024]{1,0:T(8,128)} fusion(f32[1024,64]{1,0:T(8,128)S(1)} %bitcast.121), kind=kOutput, calls=%fused_computation.77 | convolution fusion | flops 805306368 | bytes 4456448 | tf_op jit(solution)/shard_map/dot_general | solution.py:60
  87.8 0.0 all-reduce.2.cloned.1.call-update
  87.9 311.7 %all-reduce.2.cloned.1.call-done = f32[1024,1024]{1,0:T(8,128)} async-done(((f32[1024,1024]{1,0:T(8,128)}), f32[1024,1024]{1,0:T(8,128)}) %all-reduce.2.cloned.1.call-update) | async-done | bytes 4194320 | tf_op jit(solution)/shard_map/psum | solution.py:61
  399.5 17.1 %gather_fusion = f32[1024]{0:T(1024)S(1)} fusion(f32[1024,1024]{1,0:T(8,128)} %all-reduce.2.cloned.1.call-done, s32[1024]{0:T(1024)S(1)} %bitcast.113), kind=kCustom, calls=%fused_computation | custom fusion | bytes 16384 | tf_op jit(solution)/shard_map/jit(diagonal)/cond/branch_0_fun/gather | solution.py:62
  416.7 3.0 subtract_multiply_fusion
  419.7 3.4 fusion.64
  423.1 0.3 reshape.58
  423.5 19.5 %all_to_all.36 = f32[32,1,2048]{2,1,0:T(1,128)S(1)} all-to-all(f32[32,1,2048]{2,1,0:T(1,128)S(1)} %reshape.58), channel_id=1, replica_groups=mesh['vec'=32,'row'=16] {'vec'}, dimensions={0} | all-to-all | bytes 524288 | tf_op jit(solution)/shard_map/all_to_all | solution.py:68
  442.9 1.3 reduce.1
  444.2 0.2 reshape.59
  444.4 0.3 copy.34
  444.7 0.9 all_to_all.32
  (20 shorter events, 0.4 us)
Async XLA Ops:
  6.5 10.0 %copy-start = (f32[8,256,256]{2,1,0:T(8,128)S(1)}, f32[8,256,256]{2,1,0:T(8,128)}, u32[]{:S(2)}) copy-start(f32[8,256,256]{2,1,0:T(8,128)} %param.3) | copy-start | bytes 6291460
  6.5 393.0 %all-reduce.2.cloned.1.call-start = ((), (), s32[]{:S(2)}) async-start(), calls=%async_computation.2 | async-start | bytes 8388608 | tf_op jit(solution)/shard_map/psum | solution.py:61
  6.5 13.0 %copy-start.1 = (f32[8,256,256]{2,1,0:T(8,128)S(1)}, f32[8,256,256]{2,1,0:T(8,128)}, u32[]{:S(2)}) copy-start(f32[8,256,256]{2,1,0:T(8,128)} %param.4) | copy-start | bytes 6291460
  7.5 13.3 %collective-permute-start = (f32[32,256]{1,0:T(8,128)S(1)}, f32[32,256]{1,0:T(8,128)S(1)}, u32[]{:S(2)}, u32[]{:S(2)}) collective-permute-start(f32[32,256]{1,0:T(8,128)S(1)} %slice.61), channel_id=1, source_target_pairs={{1,0},{2,1},{3,2},{4,3},{5,4},{6,5},{7,6},{8,7},{9,8},{10,9},{11,1... | collective-permute-start | bytes 98312 | tf_op jit(solution)/shard_map/ppermute | solution.py:23
  10.1 10.7 %collective-permute-start.1 = (f32[32,256]{1,0:T(8,128)S(1)}, f32[32,256]{1,0:T(8,128)S(1)}, u32[]{:S(2)}, u32[]{:S(2)}) collective-permute-start(f32[32,256]{1,0:T(8,128)S(1)} %fusion.45), channel_id=1, source_target_pairs={{0,1},{1,2},{2,3},{3,4},{4,5},{5,6},{6,7},{7,8},{8,9},{9,10},{10,1... | collective-permute-start | bytes 98312 | tf_op jit(solution)/shard_map/ppermute | solution.py:20
  20.7 2.1 copy-start.2
  25.2 7.1 %collective-permute-start.2 = (f32[32,256]{1,0:T(8,128)S(1)}, f32[32,256]{1,0:T(8,128)S(1)}, u32[]{:S(2)}, u32[]{:S(2)}) collective-permute-start(f32[32,256]{1,0:T(8,128)S(1)} %slice.83), channel_id=1, source_target_pairs={{1,0},{2,1},{3,2},{4,3},{5,4},{6,5},{7,6},{8,7},{9,8},{10,9},{11,1... | collective-permute-start | bytes 98312 | tf_op jit(solution)/shard_map/ppermute | solution.py:23
  26.5 5.8 %collective-permute-start.3 = (f32[32,256]{1,0:T(8,128)S(1)}, f32[32,256]{1,0:T(8,128)S(1)}, u32[]{:S(2)}, u32[]{:S(2)}) collective-permute-start(f32[32,256]{1,0:T(8,128)S(1)} %fusion.43), channel_id=1, source_target_pairs={{0,1},{1,2},{2,3},{3,4},{4,5},{5,6},{6,7},{7,8},{8,9},{9,10},{10,1... | collective-permute-start | bytes 98312 | tf_op jit(solution)/shard_map/ppermute | solution.py:20
  36.7 7.3 %collective-permute-start.4 = (f32[32,256]{1,0:T(8,128)S(1)}, f32[32,256]{1,0:T(8,128)S(1)}, u32[]{:S(2)}, u32[]{:S(2)}) collective-permute-start(f32[32,256]{1,0:T(8,128)S(1)} %slice.86), channel_id=1, source_target_pairs={{1,0},{2,1},{3,2},{4,3},{5,4},{6,5},{7,6},{8,7},{9,8},{10,9},{11,1... | collective-permute-start | bytes 98312 | tf_op jit(solution)/shard_map/ppermute | solution.py:23
  38.0 6.0 %collective-permute-start.5 = (f32[32,256]{1,0:T(8,128)S(1)}, f32[32,256]{1,0:T(8,128)S(1)}, u32[]{:S(2)}, u32[]{:S(2)}) collective-permute-start(f32[32,256]{1,0:T(8,128)S(1)} %fusion.41), channel_id=1, source_target_pairs={{0,1},{1,2},{2,3},{3,4},{4,5},{5,6},{6,7},{7,8},{8,9},{9,10},{10,1... | collective-permute-start | bytes 98312 | tf_op jit(solution)/shard_map/ppermute | solution.py:20
  48.4 8.3 %collective-permute-start.6 = (f32[32,256]{1,0:T(8,128)S(1)}, f32[32,256]{1,0:T(8,128)S(1)}, u32[]{:S(2)}, u32[]{:S(2)}) collective-permute-start(f32[32,256]{1,0:T(8,128)S(1)} %slice.89), channel_id=1, source_target_pairs={{1,0},{2,1},{3,2},{4,3},{5,4},{6,5},{7,6},{8,7},{9,8},{10,9},{11,1... | collective-permute-start | bytes 98312 | tf_op jit(solution)/shard_map/ppermute | solution.py:23
  49.7 7.0 %collective-permute-start.7 = (f32[32,256]{1,0:T(8,128)S(1)}, f32[32,256]{1,0:T(8,128)S(1)}, u32[]{:S(2)}, u32[]{:S(2)}) collective-permute-start(f32[32,256]{1,0:T(8,128)S(1)} %fusion.39), channel_id=1, source_target_pairs={{0,1},{1,2},{2,3},{3,4},{4,5},{5,6},{6,7},{7,8},{8,9},{9,10},{10,1... | collective-permute-start | bytes 98312 | tf_op jit(solution)/shard_map/ppermute | solution.py:20
Sparse Core Ops, SparseCore 0:
  88.0 311.5 all-reduce.1
where the time goes:
time: 454 us; the launch traced here: 452 us
  waiting for transfers between devices  312 us (69%)
  blocking collectives  40.6 us (9%)
  matrix products  32 us (7%)
  starting transfers between devices  26 us (6%)
  local copies, waits for them, and re-layouts  22.6 us (5%)
  between operations  13.9 us (3%)
  other arithmetic  5.72 us (1%)
    psum x1, waiting for transfers between devices, local(): gram_sum = lax.psum(partial_value, ('vec', 'row'))  312 us
    all_to_all x1, blocking collectives, local(): lax.all_to_all(current, 'vec', split_axis=1, concat_axis=0, tiled=True)  21.1 us
    ppermute x4, starting transfers between devices, with_halo(): lax.ppermute(lax.slice_in_dim(block, block.shape[dim] - width, None, axis...  20.7 us
    all_to_all x1, blocking collectives, local(): lax.all_to_all(renewed, 'vec', split_axis=0, concat_axis=1, tiled=True)  19.5 us
    gather x1, local copies, waits for them, and re-layouts, local(): scales = 1.0 / jnp.sqrt(jnp.diagonal(gram_sum) / total_rows + epsilon)  17.1 us
  transfers between devices with their start and end apart: 9, of which 1 were waited for; matrix products, arithmetic and copies ran while one was open for 2% of the time, Pallas kernels for 0%

commit v1 on v0

v1 whole, which is shorter than its diff:
```python
import jax
import jax.numpy as jnp
from jax import lax
from jax.sharding import Mesh, PartitionSpec as P

DEGREE = 4

filter_center = 0.1
filter_half = 1.0
epsilon = 1e-06
precision = lax.Precision.HIGH

SPLIT = (("yl", 4), ("x", 4), ("c", 2), ("yh", 2), ("z", 8))
VEC = ("yl", "x", "c")
ROW = ("yh", "z")
SUM = ("yl", "yh", "z")


def dot(a, b, contract, batch=((), ())):
    return lax.dot_general(a, b, (contract, batch), precision=precision)


def local_terms(y, diag_blocks, coupling):
    batch = ((0,), (0,))
    result = dot(y, diag_blocks, ((2,), (2,)), batch) - filter_center * y
    upper = dot(y[1:], coupling[:-1], ((2,), (2,)), batch)
    lower = dot(y[:-1], coupling[:-1], ((2,), (1,)), batch)
    none = jnp.zeros_like(y[:1])
    return result + jnp.concatenate([upper, none]) + jnp.concatenate([none, lower])


def chebyshev(vectors, diag_blocks, coupling):
    count = vectors.shape[0]
    blocks, size = diag_blocks.shape[0], diag_blocks.shape[1]
    rows = lax.axis_size(ROW)
    forward = [(i, i + 1) for i in range(rows - 1)]
    backward = [(target, source) for source, target in forward]
    y = vectors.reshape(count, blocks, size).transpose(1, 0, 2)
    last_coupling = coupling[-1]
    first, last = y[0], y[-1]
    previous = None
    for turn in range(DEGREE):
        from_above = lax.ppermute(first, ROW, backward)
        last_term = dot(last, last_coupling, ((1,), (0,)))
        from_below = lax.ppermute(last_term, ROW, forward)
        scale = (1.0 if turn == 0 else 2.0) / filter_half
        inner = scale * local_terms(y, diag_blocks, coupling)
        if previous is not None:
            inner = inner - previous
        last = inner[-1] + scale * dot(from_above, last_coupling, ((1,), (1,)))
        first = inner[0] + scale * from_below
        previous = y
        y = jnp.concatenate([first[None], inner[1:-1], last[None]])
    return y


def local(diag_blocks, coupling, vectors):
    count = vectors.shape[0]
    y = chebyshev(vectors, diag_blocks, coupling)
    blocks, _, size = y.shape
    nyl, nx, nc = (lax.axis_size(a) for a in VEC)
    total_rows = blocks * size * lax.axis_size(ROW)
    swapped = lax.all_to_all(y, "yl", split_axis=0, concat_axis=0, tiled=True)
    part = blocks // nyl
    own = swapped.reshape(nyl, part, count, size).transpose(0, 2, 1, 3)
    own = own.reshape(nyl * count, part * size)
    group, depth = own.shape
    copies = jnp.broadcast_to(own[None], (nx, group, depth))
    near = lax.all_to_all(copies, "x", split_axis=0, concat_axis=0, tiled=True)
    near = near.reshape(nx * group, depth)
    far = lax.ppermute(near, "c", [(0, 1), (1, 0)])
    half = nx * group
    members = lax.axis_size(SUM)
    gram_near = dot(own, near, ((1,), (1,)))
    gram_far = dot(own, far, ((1,), (1,)))
    squares = jnp.concatenate([jnp.sum(near * near, axis=1), jnp.sum(far * far, axis=1)])
    lanes = 2 * half // 8
    payload = jnp.concatenate(
        [
            gram_near.reshape(members, -1),
            gram_far.reshape(members, -1),
            jnp.tile(squares.reshape(8, lanes), (members // 8, 1)),
        ],
        axis=1,
    )
    pieces = lax.all_to_all(payload, SUM, split_axis=0, concat_axis=0, tiled=True)
    piece = jnp.sum(pieces, axis=0)
    spread = jnp.broadcast_to(piece[None], pieces.shape)
    summed = lax.all_to_all(spread, SUM, split_axis=0, concat_axis=0, tiled=True)
    width = group // members * half
    gram_near = summed[:, :width].reshape(group, half)
    gram_far = summed[:, width : 2 * width].reshape(group, half)
    scales = 1.0 / jnp.sqrt(summed[:8, 2 * width :].reshape(2 * half) / total_rows + epsilon)
    scales_near, scales_far = scales[:half], scales[half:]
    at = lax.axis_index("x") * group
    mine = lax.dynamic_slice(scales_near, (at,), (group,))
    same = lax.broadcasted_iota(jnp.int32, (group, half), 1) == (
        lax.broadcasted_iota(jnp.int32, (group, half), 0) + at
    )
    delta = jnp.where(same, 1.5, 0.0)
    mixing_near = (
        delta - (0.5 / total_rows) * (gram_near * mine[:, None] * scales_near[None, :])
    ) * scales_near[None, :]
    mixing_far = (
        (-0.5 / total_rows) * (gram_far * mine[:, None] * scales_far[None, :])
    ) * scales_far[None, :]
    renewed = dot(mixing_near, near, ((1,), (0,))) + dot(mixing_far, far, ((1,), (0,)))
    return lax.all_to_all(renewed, "yl", split_axis=0, concat_axis=1, tiled=True)


def solution(mesh):
    sizes = tuple(size for _, size in SPLIT)
    fine = Mesh(mesh.devices.reshape(sizes), tuple(name for name, _ in SPLIT))
    placed = (P(ROW, None, None), P(ROW, None, None), P(VEC, ROW))
    return jax.shard_map(
        local, mesh=fine, in_specs=placed, out_specs=P(VEC, ROW), check_vma=False
    )
```

time: 454 us -> 179 us (0.39)
  waiting for transfers between devices: 312 us -> 21 us
  blocking collectives: 40.6 us -> 74.3 us
  starting transfers between devices: 26 us -> 40.1 us
  between operations: 13.9 us -> 0.51 us
  local copies, waits for them, and re-layouts: 22.6 us -> 11.7 us
  matrix products: 32 us -> 22.3 us
    psum x1 -> x0, waiting for transfers between devices: 312 us -> none  [local(): gram_sum = lax.psum(partial_value, ('vec', 'row'))]
    all_to_all x2 -> x4, blocking collectives: 40.6 us -> 74.3 us  [the longest x1 41.7 us: local(): lax.all_to_all(payload, SUM, split_axis=0, concat_axis=0, tiled=True)]
    all_to_all x0 -> x1, waiting for transfers between devices: none -> 17.9 us  [local(): lax.all_to_all(spread, SUM, split_axis=0, concat_axis=0, tiled=True)]
    gather x1 -> x0, local copies, waits for them, and re-layouts: 17.1 us -> none  [local(): scales = 1.0 / jnp.sqrt(jnp.diagonal(gram_sum) / total_rows + epsilon)]
    dot_general x18 -> x24, matrix products: 32 us -> 22.3 us  [dot(): return lax.dot_general(a, b, (contract, batch), precision=precision)]
    all_to_all x0 -> x1, starting transfers between devices: none -> 7.3 us  [local(): lax.all_to_all(spread, SUM, split_axis=0, concat_axis=0, tiled=True)]
    ppermute x8 -> x9, starting transfers between devices: 26 us -> 32.8 us  [the longest x4 18.6 us: chebyshev(): from_below = lax.ppermute(last_term, ROW, forward)]
  transfers between devices with their start and end apart: 9 -> 10, of which waited for: 1 -> 3; matrix products, arithmetic and copies ran while one was open for 2% -> 10% of each run, Pallas kernels for 0% -> 0%
where the time goes in v1:
time: 179 us; the launch traced here: 176 us
  blocking collectives  74.3 us (42%)
  starting transfers between devices  40.1 us (22%)
  matrix products  22.3 us (12%)
  waiting for transfers between devices  21 us (12%)
  local copies, waits for them, and re-layouts  11.7 us (7%)
  other arithmetic  5.87 us (3%)
    all_to_all x1, blocking collectives, local(): lax.all_to_all(payload, SUM, split_axis=0, concat_axis=0, tiled=True)  41.7 us
    dot_general x24, matrix products, dot(): return lax.dot_general(a, b, (contract, batch), precision=precision)  22.3 us
    ppermute x4, starting transfers between devices, chebyshev(): from_below = lax.ppermute(last_term, ROW, forward)  18.6 us
    all_to_all x1, waiting for transfers between devices, local(): lax.all_to_all(spread, SUM, split_axis=0, concat_axis=0, tiled=True)  17.9 us
    all_to_all x1, blocking collectives, local(): near = lax.all_to_all(copies, 'x', split_axis=0, concat_axis=0, tiled=True)  13.6 us
    all_to_all x1, blocking collectives, local(): swapped = lax.all_to_all(y, 'yl', split_axis=0, concat_axis=0, tiled=True)  10.4 us
    ppermute x1, starting transfers between devices, local(): far = lax.ppermute(near, 'c', [(0, 1), (1, 0)])  9.01 us
    all_to_all x1, blocking collectives, local(): lax.all_to_all(renewed, 'yl', split_axis=0, concat_axis=1, tiled=True)  8.62 us
  transfers between devices with their start and end apart: 10, of which 3 were waited for; matrix products, arithmetic and copies ran while one was open for 10% of the time, Pallas kernels for 0%

profile of v1, /device:TPU:1, one launch (start us, length us, event | category | flops | bytes accessed | tf_op | source)
XLA Modules:
  0.0 175.8 jit_solution(3880325752760300105)
XLA Ops:
  0.0 1.1 copy.33
  1.1 1.2 fusion.48
  2.4 4.8 %collective-permute-start = (f32[32,256]{1,0:T(8,128)S(1)}, f32[32,256]{1,0:T(8,128)S(1)}, u32[]{:S(2)}, u32[]{:S(2)}) collective-permute-start(f32[32,256]{1,0:T(8,128)S(1)} %fusion.48), channel_id=1, source_target_pairs={{0,1},{1,2},{2,3},{3,4},{4,5},{5,6},{6,7},{7,8},{8,9},{9,10},{10,1... | collective-permute-start | bytes 98312 | tf_op jit(solution)/shard_map/ppermute | solution.py:45
  7.2 1.3 collective-permute-start.1
  8.5 2.6 %fusion.32 = f32[7,32,256]{2,1,0:T(8,128)S(1)} fusion(f32[8,256,256]{2,1,0:T(8,128)} %param.4, f32[4,8,8,256]{3,2,1,0:T(8,128)} %bitcast.143), kind=kOutput, calls=%fused_computation.41 | convolution fusion | flops 88080384 | bytes 2326528 | tf_op jit(solution)/shard_map/dot_general | solution.py:20
  11.1 0.0 copy-done.2
  11.1 0.7 fusion.30
  11.8 1.0 fusion.4
  12.9 0.0 collective-permute-done
  12.9 1.3 collective-permute-start.3
  14.2 0.3 convolution_add_fusion.1
  14.5 0.2 fusion.45
  14.7 5.3 %collective-permute-start.2 = (f32[32,256]{1,0:T(8,128)S(1)}, f32[32,256]{1,0:T(8,128)S(1)}, u32[]{:S(2)}, u32[]{:S(2)}) collective-permute-start(f32[32,256]{1,0:T(8,128)S(1)} %fusion.45), channel_id=1, source_target_pairs={{0,1},{1,2},{2,3},{3,4},{4,5},{5,6},{6,7},{7,8},{8,9},{9,10},{10,1... | collective-permute-start | bytes 98312 | tf_op jit(solution)/shard_map/ppermute | solution.py:45
  19.9 1.0 fusion.28
  20.9 0.7 fusion.26
  21.6 1.0 fusion.13
  22.7 0.3 fusion.17
  23.0 0.2 fusion.42
  23.2 4.0 %collective-permute-start.4 = (f32[32,256]{1,0:T(8,128)S(1)}, f32[32,256]{1,0:T(8,128)S(1)}, u32[]{:S(2)}, u32[]{:S(2)}) collective-permute-start(f32[32,256]{1,0:T(8,128)S(1)} %fusion.42), channel_id=1, source_target_pairs={{0,1},{1,2},{2,3},{3,4},{4,5},{5,6},{6,7},{7,8},{8,9},{9,10},{10,1... | collective-permute-start | bytes 98312 | tf_op jit(solution)/shard_map/ppermute | solution.py:45
  27.2 1.3 collective-permute-start.5
  28.5 0.7 fusion.22
  29.2 1.0 fusion.24
  30.2 1.0 fusion.11
  31.3 2.5 %collective-permute-done.5 = f32[32,256]{1,0:T(8,128)S(1)} collective-permute-done((f32[32,256]{1,0:T(8,128)S(1)}, f32[32,256]{1,0:T(8,128)S(1)}, u32[]{:S(2)}, u32[]{:S(2)}) %collective-permute-start.5) | collective-permute-done | bytes 32800 | tf_op jit(solution)/shard_map/ppermute | solution.py:43
  33.7 0.3 fusion.16
  34.0 0.2 fusion.39
  34.2 4.6 %collective-permute-start.6 = (f32[32,256]{1,0:T(8,128)S(1)}, f32[32,256]{1,0:T(8,128)S(1)}, u32[]{:S(2)}, u32[]{:S(2)}) collective-permute-start(f32[32,256]{1,0:T(8,128)S(1)} %fusion.39), channel_id=1, source_target_pairs={{0,1},{1,2},{2,3},{3,4},{4,5},{5,6},{6,7},{7,8},{8,9},{9,10},{10,1... | collective-permute-start | bytes 98312 | tf_op jit(solution)/shard_map/ppermute | solution.py:45
  38.8 1.3 collective-permute-start.7
  40.1 0.7 fusion.18
  40.8 1.0 fusion.20
  41.8 1.0 fusion.9
  42.9 0.6 collective-permute-done.7
  43.5 0.3 fusion.15
  43.8 10.4 %all_to_all.47 = f32[8,32,256]{2,1,0:T(8,128)S(1)} all-to-all(f32[8,32,256]{2,1,0:T(8,128)S(1)} %pad_maximum_fusion.4), channel_id=1, replica_groups=mesh['yl'=4,'x'=4,'c'=2,'yh'=2,'z'=8] {'yl'}, dimensions={0} | all-to-all | bytes 524288 | tf_op jit(solution)/shard_map/all_to_all | solution.py:63
  54.2 0.2 copy.12
  54.4 0.1 broadcast_in_dim.59
  54.6 13.6 %all_to_all.48 = f32[4,128,512]{2,1,0:T(8,128)S(1)} all-to-all(f32[4,128,512]{2,1,0:T(8,128)S(1)} %broadcast_in_dim.59), channel_id=1, replica_groups=mesh['yl'=4,'x'=4,'c'=2,'yh'=2,'z'=8] {'x'}, dimensions={0} | all-to-all | bytes 2097152 | tf_op jit(solution)/shard_map/all_to_all | solution.py:69
  68.1 9.0 %collective-permute-start.8 = (f32[512,512]{1,0:T(8,128)S(1)}, f32[512,512]{1,0:T(8,128)}, u32[]{:S(2)}, u32[]{:S(2)}) collective-permute-start(f32[512,512]{1,0:T(8,128)S(1)} %bitcast.139), channel_id=1, source_target_pairs={{0,16},{16,0},{1,17},{17,1},{2,18},{18,2},{3,19},{19,3},{4,20},{20... | collective-permute-start | bytes 3145736 | tf_op jit(solution)/shard_map/ppermute | solution.py:71
  77.1 1.4 fusion.99
  78.5 1.7 reshape.67
  80.2 0.1 multiply_reduce_fusion.1
  80.4 2.6 %fusion.100 = f32[128,512]{1,0:T(8,128)} fusion(f32[128,512]{1,0:T(8,128)S(1)} %bitcast.149, f32[512,512]{1,0:T(8,128)} %collective-permute-done.8), kind=kOutput, calls=%fused_computation.138 | convolution fusion | flops 201326592 | bytes 1572864 | tf_op jit(solution)/shard_map/dot_general | solution.py:20
  83.0 1.0 reshape.68
  84.0 1.4 multiply_reduce_fusion
  85.4 1.0 pad_maximum_fusion
  86.4 0.4 all_to_all.34
  86.8 41.7 %all_to_all.49 = f32[64,1,2176]{2,1,0:T(1,128)} all-to-all(f32[64,1,2176]{2,1,0:T(1,128)S(1)} %all_to_all.34), channel_id=1, replica_groups=mesh['yl'=4,'x'=4,'c'=2,'yh'=2,'z'=8] {'yl','yh','z'}, dimensions={0} | all-to-all | bytes 1114112 | tf_op jit(solution)/shard_map/all_to_all | solution.py:86
  128.5 1.4 reduce_sum.29
  129.9 1.1 broadcast_in_dim.60
  131.0 7.3 %all-to-all-start.3 = ((f32[64,1,2176]{2,1,0:T(1,128)}), f32[64,1,2176]{2,1,0:T(1,128)}, u32[]{:S(2)}, u32[]{:S(2)}) async-start(f32[64,1,2176]{2,1,0:T(1,128)} %broadcast_in_dim.60), calls=%async_computation.3 | async-start | bytes 1114112 | tf_op jit(solution)/shard_map/all_to_all | solution.py:89
  138.4 0.1 iota.38
  138.6 17.9 %all-to-all-done.3 = f32[64,1,2176]{2,1,0:T(1,128)} async-done(((f32[64,1,2176]{2,1,0:T(1,128)}), f32[64,1,2176]{2,1,0:T(1,128)}, u32[]{:S(2)}, u32[]{:S(2)}) %all-to-all-start.3) | async-done | bytes 557088 | tf_op jit(solution)/shard_map/all_to_all | solution.py:89
  156.5 1.1 copy.32
  157.6 0.8 copy-done.3
  158.4 0.1 dynamic_slice.3
  158.5 0.1 mul.137
  158.7 0.1 mul.138
  158.9 1.9 %fusion.98 = (f32[64,1024]{1,0:T(8,128)}, f32[64,1024]{1,0:T(8,128)}) fusion(f32[64,2176]{1,0:T(8,128)} %bitcast.151, f32[1024]{0:T(1024)S(1)} %bitcast.179, f32[64,1024]{1,0:T(8,128)S(1)} %bitcast.164, s32[64,1024]{1,0:T(8,128)S(1)} %bitcast.163, s32[1024]{0:T(1024)S(1)} %bitcast.178), kind=kLoop, calls=%fused_computation.136 | loop fusion | flops 458752 | bytes 1581056 | tf_op jit(solution)/shard_map/slice | solution.py:92
  160.7 1.0 reshape.69
  161.7 1.7 mul.148
  163.4 1.4 fusion.101
  164.8 1.7 convolution_add_fusion
  166.5 8.6 %all_to_all.50 = f32[4,32,512]{2,1,0:T(8,128)S(1)} all-to-all(f32[4,32,512]{2,1,0:T(8,128)S(1)} %bitcast.165), channel_id=1, replica_groups=mesh['yl'=4,'x'=4,'c'=2,'yh'=2,'z'=8] {'yl'}, dimensions={0} | all-to-all | bytes 524288 | tf_op jit(solution)/shard_map/all_to_all | solution.py:108
  175.1 0.7 copy.16
  (35 shorter events, 0.3 us)
Async XLA Ops:
  0.0 11.8 %copy-start = (f32[8,256,256]{2,1,0:T(8,128)S(1)}, f32[8,256,256]{2,1,0:T(8,128)}, u32[]{:S(2)}) copy-start(f32[8,256,256]{2,1,0:T(8,128)} %param.3) | copy-start | bytes 6291460
  0.0 11.1 %copy-start.2 = (f32[32,2048]{1,0:T(8,128)S(1)}, f32[32,2048]{1,0:T(8,128)}, u32[]{:S(2)}) copy-start(f32[32,2048]{1,0:T(8,128)} %param.5) | copy-start | bytes 786436
  0.0 11.1 %copy-start.1 = (f32[8,256,256]{2,1,0:T(8,128)S(1)}, f32[8,256,256]{2,1,0:T(8,128)}, u32[]{:S(2)}) copy-start(f32[8,256,256]{2,1,0:T(8,128)} %param.4) | copy-start | bytes 6291460
  2.4 10.5 %collective-permute-start = (f32[32,256]{1,0:T(8,128)S(1)}, f32[32,256]{1,0:T(8,128)S(1)}, u32[]{:S(2)}, u32[]{:S(2)}) collective-permute-start(f32[32,256]{1,0:T(8,128)S(1)} %fusion.48), channel_id=1, source_target_pairs={{0,1},{1,2},{2,3},{3,4},{4,5},{5,6},{6,7},{7,8},{8,9},{9,10},{10,1... | collective-permute-start | bytes 98312 | tf_op jit(solution)/shard_map/ppermute | solution.py:45
  7.2 7.0 %collective-permute-start.1 = (f32[32,256]{1,0:T(8,128)S(1)}, f32[32,256]{1,0:T(8,128)S(1)}, u32[]{:S(2)}, u32[]{:S(2)}) collective-permute-start(f32[32,256]{1,0:T(8,128)S(1)} %slice_bitcast_fusion.6), channel_id=1, source_target_pairs={{1,0},{2,1},{3,2},{4,3},{5,4},{6,5},{7,6},{8,7},{9,8},{10,9},{11,1... | collective-permute-start | bytes 98312 | tf_op jit(solution)/shard_map/ppermute | solution.py:43
  12.9 9.8 %collective-permute-start.3 = (f32[32,256]{1,0:T(8,128)S(1)}, f32[32,256]{1,0:T(8,128)S(1)}, u32[]{:S(2)}, u32[]{:S(2)}) collective-permute-start(f32[32,256]{1,0:T(8,128)S(1)} %fusion.86), channel_id=1, source_target_pairs={{1,0},{2,1},{3,2},{4,3},{5,4},{6,5},{7,6},{8,7},{9,8},{10,9},{11,1... | collective-permute-start | bytes 98312 | tf_op jit(solution)/shard_map/ppermute | solution.py:43
  14.7 12.5 %collective-permute-start.2 = (f32[32,256]{1,0:T(8,128)S(1)}, f32[32,256]{1,0:T(8,128)S(1)}, u32[]{:S(2)}, u32[]{:S(2)}) collective-permute-start(f32[32,256]{1,0:T(8,128)S(1)} %fusion.45), channel_id=1, source_target_pairs={{0,1},{1,2},{2,3},{3,4},{4,5},{5,6},{6,7},{7,8},{8,9},{9,10},{10,1... | collective-permute-start | bytes 98312 | tf_op jit(solution)/shard_map/ppermute | solution.py:45
  23.2 15.6 %collective-permute-start.4 = (f32[32,256]{1,0:T(8,128)S(1)}, f32[32,256]{1,0:T(8,128)S(1)}, u32[]{:S(2)}, u32[]{:S(2)}) collective-permute-start(f32[32,256]{1,0:T(8,128)S(1)} %fusion.42), channel_id=1, source_target_pairs={{0,1},{1,2},{2,3},{3,4},{4,5},{5,6},{6,7},{7,8},{8,9},{9,10},{10,1... | collective-permute-start | bytes 98312 | tf_op jit(solution)/shard_map/ppermute | solution.py:45
  27.2 6.5 %collective-permute-start.5 = (f32[32,256]{1,0:T(8,128)S(1)}, f32[32,256]{1,0:T(8,128)S(1)}, u32[]{:S(2)}, u32[]{:S(2)}) collective-permute-start(f32[32,256]{1,0:T(8,128)S(1)} %fusion.85), channel_id=1, source_target_pairs={{1,0},{2,1},{3,2},{4,3},{5,4},{6,5},{7,6},{8,7},{9,8},{10,9},{11,1... | collective-permute-start | bytes 98312 | tf_op jit(solution)/shard_map/ppermute | solution.py:43
  34.2 9.6 %collective-permute-start.6 = (f32[32,256]{1,0:T(8,128)S(1)}, f32[32,256]{1,0:T(8,128)S(1)}, u32[]{:S(2)}, u32[]{:S(2)}) collective-permute-start(f32[32,256]{1,0:T(8,128)S(1)} %fusion.39), channel_id=1, source_target_pairs={{0,1},{1,2},{2,3},{3,4},{4,5},{5,6},{6,7},{7,8},{8,9},{9,10},{10,1... | collective-permute-start | bytes 98312 | tf_op jit(solution)/shard_map/ppermute | solution.py:45
  38.8 4.7 %collective-permute-start.7 = (f32[32,256]{1,0:T(8,128)S(1)}, f32[32,256]{1,0:T(8,128)S(1)}, u32[]{:S(2)}, u32[]{:S(2)}) collective-permute-start(f32[32,256]{1,0:T(8,128)S(1)} %fusion.84), channel_id=1, source_target_pairs={{1,0},{2,1},{3,2},{4,3},{5,4},{6,5},{7,6},{8,7},{9,8},{10,9},{11,1... | collective-permute-start | bytes 98312 | tf_op jit(solution)/shard_map/ppermute | solution.py:43
  68.1 12.3 %collective-permute-start.8 = (f32[512,512]{1,0:T(8,128)S(1)}, f32[512,512]{1,0:T(8,128)}, u32[]{:S(2)}, u32[]{:S(2)}) collective-permute-start(f32[512,512]{1,0:T(8,128)S(1)} %bitcast.139), channel_id=1, source_target_pairs={{0,16},{16,0},{1,17},{17,1},{2,18},{18,2},{3,19},{19,3},{4,20},{20... | collective-permute-start | bytes 3145736 | tf_op jit(solution)/shard_map/ppermute | solution.py:71
  131.0 25.4 %all-to-all-start.3 = ((f32[64,1,2176]{2,1,0:T(1,128)}), f32[64,1,2176]{2,1,0:T(1,128)}, u32[]{:S(2)}, u32[]{:S(2)}) async-start(f32[64,1,2176]{2,1,0:T(1,128)} %broadcast_in_dim.60), calls=%async_computation.3 | async-start | bytes 1114112 | tf_op jit(solution)/shard_map/all_to_all | solution.py:89
  157.6 0.8 copy-start.3

commit v2 on v1

--- a/solution.py
+++ b/solution.py
@@ -1,6 +1,10 @@
+import functools
+
 import jax
 import jax.numpy as jnp
 from jax import lax
+from jax.experimental import pallas as pl
+from jax.experimental.pallas import tpu as pltpu
 from jax.sharding import Mesh, PartitionSpec as P
 
 DEGREE = 4
@@ -14,6 +18,9 @@
 VEC = ("yl", "x", "c")
 ROW = ("yh", "z")
 SUM = ("yl", "yh", "z")
+
+TILE, LANES = 8, 128
+INTERPRET = False
 
 
 def dot(a, b, contract, batch=((), ())):
@@ -54,6 +61,104 @@
     return y
 
 
+def split(a):
+    high = a.astype(jnp.bfloat16)
+    return high, (a - high.astype(jnp.float32)).astype(jnp.bfloat16)
+
+
+def product(a, b, contract):
+    def one(x, y):
+        return lax.dot_general(x, y, (contract, ((), ())), preferred_element_type=jnp.float32)
+
+    return one(a[0], b[0]) + (one(a[0], b[1]) + one(a[1], b[0]))
+
+
+def gram_kernel(own_ref, near_ref, far_ref, out_ref):
+    own = split(own_ref[...])
+    ones = jnp.ones((TILE, own_ref.shape[1]), jnp.bfloat16)
+    tiles, squares = [], []
+    for ref in (near_ref, far_ref):
+        tiles.append(product(own, split(ref[...]), ((1,), (1,))))
+        square = split(ref[...] * ref[...])
+        sums = [
+            lax.dot_general(ones, part, (((1,), (1,)), ((), ())), preferred_element_type=jnp.float32)
+            for part in square
+        ]
+        squares.append(sums[0] + sums[1])
+    across = near_ref.shape[0] // LANES
+    step = 2 * TILE + 1
+    for m in range(out_ref.shape[0] // step):
+        i, j = m // across * TILE, m % across * LANES
+        for side in range(2):
+            out_ref[step * m + TILE * side : step * m + TILE * (side + 1), :] = tiles[side][
+                i : i + TILE, j : j + LANES
+            ]
+        side, j = m % (2 * across) // across, m % across * LANES
+        out_ref[step * m + 2 * TILE : step * (m + 1), :] = squares[side][:1, j : j + LANES]
+
+
+def sum_kernel(in_ref, out_ref):
+    step = 2 * TILE + 1
+    group = TILE * step
+    count = in_ref.shape[0] // group
+    total = in_ref[:group, :]
+    for g in range(1, count):
+        total = total + in_ref[group * g : group * (g + 1), :]
+    out_ref[:group, :] = total
+    piece = out_ref[:step, :]
+    for m in range(1, TILE):
+        piece = piece + out_ref[step * m : step * (m + 1), :]
+    for m in range(TILE):
+        out_ref[step * m : step * (m + 1), :] = piece
+    total = out_ref[:group, :]
+    for g in range(1, count):
+        out_ref[group * g : group * (g + 1), :] = total
+
+
+def mixing_kernel(total_rows, at_ref, summed_ref, own_ref, near_ref, far_ref, out_ref):
+    step = 2 * TILE + 1
+    across = near_ref.shape[0] // LANES
+    group = own_ref.shape[0]
+
+    def scales_of(m):
+        row = summed_ref[pl.ds(step * m + 2 * TILE, 1), :]
+        return 1.0 / jnp.sqrt(row / total_rows + epsilon)
+
+    on_diagonal = lax.broadcasted_iota(jnp.int32, (group, LANES), 0) == (
+        lax.broadcasted_iota(jnp.int32, (group, LANES), 1)
+    )
+    mine = jnp.sum(jnp.where(on_diagonal, scales_of(at_ref[0]), 0.0), axis=1, keepdims=True)
+    result = 1.5 * mine * own_ref[...]
+    for side, ref in enumerate((near_ref, far_ref)):
+        columns = []
+        for j in range(across):
+            column = jnp.concatenate(
+                [
+                    summed_ref[step * m + TILE * side : step * m + TILE * (side + 1), :]
+                    for m in range(j, group // TILE * across, across)
+                ]
+            )
+            scale = scales_of(side * across + j)
+            columns.append((0.5 / total_rows) * (column * mine * scale) * scale)
+        mixing = jnp.concatenate(columns, axis=1)
+        result = result - product(split(mixing), split(ref[...]), ((1,), (0,)))
+    out_ref[...] = result
+
+
+def call(kernel, out_shape, name, scalars, *arrays):
+    vmem = pl.BlockSpec(memory_space=pltpu.VMEM)
+    smem = pl.BlockSpec(memory_space=pltpu.SMEM)
+    return pl.pallas_call(
+        kernel,
+        out_shape=jax.ShapeDtypeStruct(out_shape, jnp.float32),
+        in_specs=[smem] * len(scalars) + [vmem] * len(arrays),
+        out_specs=vmem,
+        name=name,
+        compiler_params=pltpu.CompilerParams(vmem_limit_bytes=24 * 2**20),
+        interpret=INTERPRET,
+    )(*scalars, *arrays)
+
+
 def local(diag_blocks, coupling, vectors):
     count = vectors.shape[0]
     y = chebyshev(vectors, diag_blocks, coupling)
@@ -69,42 +174,25 @@
     near = lax.all_to_all(copies, "x", split_axis=0, concat_axis=0, tiled=True)
     near = near.reshape(nx * group, depth)
     far = lax.ppermute(near, "c", [(0, 1), (1, 0)])
-    half = nx * group
-    members = lax.axis_size(SUM)
-    gram_near = dot(own, near, ((1,), (1,)))
-    gram_far = dot(own, far, ((1,), (1,)))
-    squares = jnp.concatenate([jnp.sum(near * near, axis=1), jnp.sum(far * far, axis=1)])
-    lanes = 2 * half // 8
-    payload = jnp.concatenate(
-        [
-            gram_near.reshape(members, -1),
-            gram_far.reshape(members, -1),
-            jnp.tile(squares.reshape(8, lanes), (members // 8, 1)),
-        ],
-        axis=1,
+    members = group // TILE * nx
+    packed = (members * (2 * TILE + 1), LANES)
+
+    def exchange(a):
+        a = a.reshape(lax.axis_size(SUM), -1)
+        return lax.all_to_all(a, SUM, split_axis=0, concat_axis=0, tiled=True).reshape(packed)
+
+    pieces = exchange(call(gram_kernel, packed, "gram", (), own, near, far))
+    summed = exchange(call(sum_kernel, packed, "sum", (), pieces))
+    renewed = call(
+        functools.partial(mixing_kernel, total_rows),
+        (group, depth),
+        "mixing",
+        (lax.axis_index("x").reshape(1),),
+        summed,
+        own,
+        near,
+        far,
     )
-    pieces = lax.all_to_all(payload, SUM, split_axis=0, concat_axis=0, tiled=True)
-    piece = jnp.sum(pieces, axis=0)
-    spread = jnp.broadcast_to(piece[None], pieces.shape)
-    summed = lax.all_to_all(spread, SUM, split_axis=0, concat_axis=0, tiled=True)
-    width = group // members * half
-    gram_near = summed[:, :width].reshape(group, half)
-    gram_far = summed[:, width : 2 * width].reshape(group, half)
-    scales = 1.0 / jnp.sqrt(summed[:8, 2 * width :].reshape(2 * half) / total_rows + epsilon)
-    scales_near, scales_far = scales[:half], scales[half:]
-    at = lax.axis_index("x") * group
-    mine = lax.dynamic_slice(scales_near, (at,), (group,))
-    same = lax.broadcasted_iota(jnp.int32, (group, half), 1) == (
-        lax.broadcasted_iota(jnp.int32, (group, half), 0) + at
-    )
-    delta = jnp.where(same, 1.5, 0.0)
-    mixing_near = (
-        delta - (0.5 / total_rows) * (gram_near * mine[:, None] * scales_near[None, :])
-    ) * scales_near[None, :]
-    mixing_far = (
-        (-0.5 / total_rows) * (gram_far * mine[:, None] * scales_far[None, :])
-    ) * scales_far[None, :]
-    renewed = dot(mixing_near, near, ((1,), (0,))) + dot(mixing_far, far, ((1,), (0,)))
     return lax.all_to_all(renewed, "yl", split_axis=0, concat_axis=1, tiled=True)
 
 

time: 179 us -> 179 us (level)
  blocking collectives: 74.3 us -> 90.6 us
  matrix products: 22.3 us -> 15.2 us
  local copies, waits for them, and re-layouts: 11.7 us -> 5.29 us
  other arithmetic: 5.87 us -> 0.05 us
  Pallas kernels: 0 us -> 3.54 us
    all_to_all x1, blocking collectives: 41.7 us -> 56.3 us  [exchange(): lax.all_to_all(a, SUM, split_axis=0, concat_axis=0, tiled=True)]
    dot_general x24 -> x20, matrix products: 22.3 us -> 15.2 us  [dot(): return lax.dot_general(a, b, (contract, batch), precision=precision)]
    reshape x3 -> x0, local copies, waits for them, and re-layouts: 3.78 us -> none  [the longest x1 1.75 us: local(): gram_near.reshape(members, -1)]
    pallas_call x0 -> x3, Pallas kernels: none -> 3.54 us  [call(): pl.pallas_call(kernel, out_shape=jax.ShapeDtypeStruct(out_shape, jnp.floa...]
    ppermute x4, waiting for transfers between devices: 3.12 us -> 0.01 us  [chebyshev(): from_above = lax.ppermute(first, ROW, backward)]
    reduce_sum x3 -> x0, other arithmetic: 2.91 us -> none  [the longest x1 1.39 us: local(): piece = jnp.sum(pieces, axis=0)]
    ppermute x1, waiting for transfers between devices: 0.01 us -> 2.26 us  [local(): far = lax.ppermute(near, 'c', [(0, 1), (1, 0)])]
    mul x3 -> x0, local copies, waits for them, and re-layouts: 1.96 us -> none  [the longest x1 1.69 us: local(): (delta - 0.5 / total_rows * (gram_near * mine[:, None] * scales_near[None...]
  transfers between devices with their start and end apart: 10 -> 10, of which waited for: 3 -> 3; matrix products, arithmetic and copies ran while one was open for 10% -> 9% of each run, Pallas kernels for 0% -> 0%
where the time goes in v2:
time: 179 us; the launch traced here: 176 us
  blocking collectives  90.6 us (51%)
  starting transfers between devices  40.4 us (23%)
  waiting for transfers between devices  20.7 us (12%)
  matrix products  15.2 us (8%)
  local copies, waits for them, and re-layouts  5.29 us (3%)
  Pallas kernels  3.54 us (2%)
    all_to_all x1, blocking collectives, exchange(): lax.all_to_all(a, SUM, split_axis=0, concat_axis=0, tiled=True)  56.3 us
    ppermute x4, starting transfers between devices, chebyshev(): from_below = lax.ppermute(last_term, ROW, forward)  20.5 us
    all_to_all x1, waiting for transfers between devices, exchange(): lax.all_to_all(a, SUM, split_axis=0, concat_axis=0, tiled=True)  17.9 us
    dot_general x20, matrix products, dot(): return lax.dot_general(a, b, (contract, batch), precision=precision)  15.2 us
    all_to_all x1, blocking collectives, local(): near = lax.all_to_all(copies, 'x', split_axis=0, concat_axis=0, tiled=True)  14.4 us
    all_to_all x1, blocking collectives, local(): swapped = lax.all_to_all(y, 'yl', split_axis=0, concat_axis=0, tiled=True)  11.1 us
    all_to_all x1, blocking collectives, local(): lax.all_to_all(renewed, 'yl', split_axis=0, concat_axis=1, tiled=True)  8.81 us
    ppermute x1, starting transfers between devices, local(): far = lax.ppermute(near, 'c', [(0, 1), (1, 0)])  7.34 us
  transfers between devices with their start and end apart: 10, of which 3 were waited for; matrix products, arithmetic and copies ran while one was open for 9% of the time, Pallas kernels for 0%

profile of v2, /device:TPU:1, one launch (start us, length us, event | category | flops | bytes accessed | tf_op | source)
XLA Modules:
  0.0 176.1 jit_solution(7786197213205440450)
XLA Ops:
  0.0 0.0 copy-start
  0.0 0.0 copy-start.5
  0.0 0.0 copy-start.4
  0.0 1.1 copy.26
  1.1 1.4 collective-permute-start.1
  2.6 1.2 fusion.44
  3.7 5.4 %collective-permute-start = (f32[32,256]{1,0:T(8,128)S(1)}, f32[32,256]{1,0:T(8,128)S(1)}, u32[]{:S(2)}, u32[]{:S(2)}) collective-permute-start(f32[32,256]{1,0:T(8,128)S(1)} %fusion.44), channel_id=1, source_target_pairs={{0,1},{1,2},{2,3},{3,4},{4,5},{5,6},{6,7},{7,8},{8,9},{9,10},{10,1... | collective-permute-start | bytes 98312 | tf_op jit(solution)/shard_map/ppermute | solution.py:52
  9.2 2.3 %fusion.30 = f32[7,32,256]{2,1,0:T(8,128)S(1)} fusion(f32[8,256,256]{2,1,0:T(8,128)} %param.4, f32[4,8,8,256]{3,2,1,0:T(8,128)} %bitcast.126), kind=kOutput, calls=%fused_computation.38 | convolution fusion | flops 88080384 | bytes 2326528 | tf_op jit(solution)/shard_map/dot_general | solution.py:27
  11.4 0.0 copy-done.5
  11.4 0.0 copy-done.4
  11.5 1.0 fusion.32
  12.4 0.0 copy-done
  12.4 1.1 fusion.4
  13.5 0.0 collective-permute-done
  13.5 1.3 collective-permute-start.3
  14.8 0.0 collective-permute-done.1
  14.8 0.3 convolution_add_fusion
  15.1 0.2 fusion.41
  15.3 1.0 fusion.28
  16.3 0.7 fusion.26
  17.0 4.6 %collective-permute-start.2 = (f32[32,256]{1,0:T(8,128)S(1)}, f32[32,256]{1,0:T(8,128)S(1)}, u32[]{:S(2)}, u32[]{:S(2)}) collective-permute-start(f32[32,256]{1,0:T(8,128)S(1)} %fusion.41), channel_id=1, source_target_pairs={{0,1},{1,2},{2,3},{3,4},{4,5},{5,6},{6,7},{7,8},{8,9},{9,10},{10,1... | collective-permute-start | bytes 98312 | tf_op jit(solution)/shard_map/ppermute | solution.py:52
  21.6 1.0 fusion.13
  22.7 0.0 collective-permute-done.2
  22.7 1.3 collective-permute-start.5
  24.0 0.0 collective-permute-done.3
  24.0 0.3 fusion.17
  24.3 1.0 fusion.24
  25.3 0.7 fusion.22
  26.0 1.0 fusion.11
  27.0 0.2 fusion.38
  27.3 4.6 %collective-permute-start.4 = (f32[32,256]{1,0:T(8,128)S(1)}, f32[32,256]{1,0:T(8,128)S(1)}, u32[]{:S(2)}, u32[]{:S(2)}) collective-permute-start(f32[32,256]{1,0:T(8,128)S(1)} %fusion.38), channel_id=1, source_target_pairs={{0,1},{1,2},{2,3},{3,4},{4,5},{5,6},{6,7},{7,8},{8,9},{9,10},{10,1... | collective-permute-start | bytes 98312 | tf_op jit(solution)/shard_map/ppermute | solution.py:52
  31.9 0.0 collective-permute-done.5
  31.9 0.3 fusion.16
  32.2 0.2 fusion.35
  32.4 0.5 collective-permute-done.4
  32.9 1.3 collective-permute-start.7
  34.2 1.0 fusion.20
  35.2 0.7 fusion.18
  35.9 5.8 %collective-permute-start.6 = (f32[32,256]{1,0:T(8,128)S(1)}, f32[32,256]{1,0:T(8,128)S(1)}, u32[]{:S(2)}, u32[]{:S(2)}) collective-permute-start(f32[32,256]{1,0:T(8,128)S(1)} %fusion.35), channel_id=1, source_target_pairs={{0,1},{1,2},{2,3},{3,4},{4,5},{5,6},{6,7},{7,8},{8,9},{9,10},{10,1... | collective-permute-start | bytes 98312 | tf_op jit(solution)/shard_map/ppermute | solution.py:52
  41.7 1.0 fusion.9
  42.8 0.0 collective-permute-done.6
  42.8 0.0 collective-permute-done.7
  42.8 0.3 fusion.15
  43.1 11.1 %all_to_all.47 = f32[8,32,256]{2,1,0:T(8,128)S(1)} all-to-all(f32[8,32,256]{2,1,0:T(8,128)S(1)} %pad_maximum_fusion.3), channel_id=1, replica_groups=mesh['yl'=4,'x'=4,'c'=2,'yh'=2,'z'=8] {'yl'}, dimensions={0} | all-to-all | bytes 524288 | tf_op jit(solution)/shard_map/all_to_all | solution.py:168
  54.2 0.2 copy.10
  54.4 0.1 broadcast_in_dim.37
  54.5 14.4 %all_to_all.48 = f32[4,128,512]{2,1,0:T(8,128)S(1)} all-to-all(f32[4,128,512]{2,1,0:T(8,128)S(1)} %broadcast_in_dim.37), channel_id=1, replica_groups=mesh['yl'=4,'x'=4,'c'=2,'yh'=2,'z'=8] {'x'}, dimensions={0} | all-to-all | bytes 2097152 | tf_op jit(solution)/shard_map/all_to_all | solution.py:174
  69.0 7.3 %collective-permute-start.8 = (f32[512,512]{1,0:T(8,128)S(1)}, f32[512,512]{1,0:T(8,128)S(1)}, u32[]{:S(2)}, u32[]{:S(2)}) collective-permute-start(f32[512,512]{1,0:T(8,128)S(1)} %bitcast.115), channel_id=1, source_target_pairs={{0,16},{16,0},{1,17},{17,1},{2,18},{18,2},{3,19},{19,3},{4,20},{20... | collective-permute-start | bytes 3145736 | tf_op jit(solution)/shard_map/ppermute | solution.py:176
  76.3 2.3 %collective-permute-done.8.far_ref = f32[512,512]{1,0:T(8,128)S(1)} collective-permute-done((f32[512,512]{1,0:T(8,128)S(1)}, f32[512,512]{1,0:T(8,128)S(1)}, u32[]{:S(2)}, u32[]{:S(2)}) %collective-permute-start.8) | collective-permute-done | bytes 1048608 | tf_op jit(solution)/shard_map/ppermute | solution.py:176
  78.6 1.7 gram.1
  80.3 0.0 copy-start.1
  80.3 1.0 copy-done.1
  81.3 56.3 %all_to_all.49 = f32[64,1,2176]{2,1,0:T(1,128)S(1)} all-to-all(f32[64,1,2176]{2,1,0:T(1,128)S(1)} %bitcast.123), channel_id=1, replica_groups=mesh['yl'=4,'x'=4,'c'=2,'yh'=2,'z'=8] {'yl','yh','z'}, dimensions={0} | all-to-all | bytes 1114112 | tf_op jit(solution)/shard_map/all_to_all | solution.py:182
  137.5 0.1 sum.1
  137.6 0.0 copy-start.3
  137.6 0.8 copy-done.3
  138.4 7.2 %all-to-all-start.3 = ((f32[64,1,2176]{2,1,0:T(1,128)}), f32[64,1,2176]{2,1,0:T(1,128)}, u32[]{:S(2)}, u32[]{:S(2)}) async-start(f32[64,1,2176]{2,1,0:T(1,128)} %bitcast.121), calls=%async_computation.3 | async-start | bytes 1114112 | tf_op jit(solution)/shard_map/all_to_all | solution.py:182
  145.7 17.9 %all-to-all-done.3 = f32[64,1,2176]{2,1,0:T(1,128)} async-done(((f32[64,1,2176]{2,1,0:T(1,128)}), f32[64,1,2176]{2,1,0:T(1,128)}, u32[]{:S(2)}, u32[]{:S(2)}) %all-to-all-start.3) | async-done | bytes 557088 | tf_op jit(solution)/shard_map/all_to_all | solution.py:182
  163.5 0.0 copy-start.2
  163.5 1.2 copy-done.2
  164.8 1.8 %mixing.1 = f32[128,512]{1,0:T(8,128)S(1)} custom-call(s32[1]{0:T(128)} %bitcast.at_ref, f32[1088,128]{1,0:T(8,128)} %bitcast.27.summed_ref, f32[128,512]{1,0:T(8,128)S(1)} %bitcast.120, f32[512,512]{1,0:T(8,128)S(1)} %bitcast.117, f32[512,512]{1,0:T(8,128)S(1)} %copy-done.2), custom_call_target="tpu_custom_call" | custom-call | tf_op jit(solution)/shard_map/mixing/pallas_call | solution.py:151
  166.5 8.8 %all_to_all.50 = f32[4,32,512]{2,1,0:T(8,128)S(1)} all-to-all(f32[4,32,512]{2,1,0:T(8,128)S(1)} %bitcast.124), channel_id=1, replica_groups=mesh['yl'=4,'x'=4,'c'=2,'yh'=2,'z'=8] {'yl'}, dimensions={0} | all-to-all | bytes 524288 | tf_op jit(solution)/shard_map/all_to_all | solution.py:196
  175.4 0.7 copy.15
  (11 shorter events, 0.1 us)
Async XLA Ops:
  0.0 12.4 %copy-start = (f32[8,256,256]{2,1,0:T(8,128)S(1)}, f32[8,256,256]{2,1,0:T(8,128)}, u32[]{:S(2)}) copy-start(f32[8,256,256]{2,1,0:T(8,128)} %param.3) | copy-start | bytes 6291460
  0.0 11.4 %copy-start.5 = (f32[32,2048]{1,0:T(8,128)S(1)}, f32[32,2048]{1,0:T(8,128)}, u32[]{:S(2)}) copy-start(f32[32,2048]{1,0:T(8,128)} %param.5) | copy-start | bytes 786436
  0.0 11.4 %copy-start.4 = (f32[8,256,256]{2,1,0:T(8,128)S(1)}, f32[8,256,256]{2,1,0:T(8,128)}, u32[]{:S(2)}) copy-start(f32[8,256,256]{2,1,0:T(8,128)} %param.4) | copy-start | bytes 6291460
  1.1 13.7 %collective-permute-start.1 = (f32[32,256]{1,0:T(8,128)S(1)}, f32[32,256]{1,0:T(8,128)S(1)}, u32[]{:S(2)}, u32[]{:S(2)}) collective-permute-start(f32[32,256]{1,0:T(8,128)S(1)} %slice_bitcast_fusion.6), channel_id=1, source_target_pairs={{1,0},{2,1},{3,2},{4,3},{5,4},{6,5},{7,6},{8,7},{9,8},{10,9},{11,1... | collective-permute-start | bytes 98312 | tf_op jit(solution)/shard_map/ppermute | solution.py:50
  3.7 9.8 %collective-permute-start = (f32[32,256]{1,0:T(8,128)S(1)}, f32[32,256]{1,0:T(8,128)S(1)}, u32[]{:S(2)}, u32[]{:S(2)}) collective-permute-start(f32[32,256]{1,0:T(8,128)S(1)} %fusion.44), channel_id=1, source_target_pairs={{0,1},{1,2},{2,3},{3,4},{4,5},{5,6},{6,7},{7,8},{8,9},{9,10},{10,1... | collective-permute-start | bytes 98312 | tf_op jit(solution)/shard_map/ppermute | solution.py:52
  13.5 10.5 %collective-permute-start.3 = (f32[32,256]{1,0:T(8,128)S(1)}, f32[32,256]{1,0:T(8,128)S(1)}, u32[]{:S(2)}, u32[]{:S(2)}) collective-permute-start(f32[32,256]{1,0:T(8,128)S(1)} %fusion.76), channel_id=1, source_target_pairs={{1,0},{2,1},{3,2},{4,3},{5,4},{6,5},{7,6},{8,7},{9,8},{10,9},{11,1... | collective-permute-start | bytes 98312 | tf_op jit(solution)/shard_map/ppermute | solution.py:50
  17.0 5.7 %collective-permute-start.2 = (f32[32,256]{1,0:T(8,128)S(1)}, f32[32,256]{1,0:T(8,128)S(1)}, u32[]{:S(2)}, u32[]{:S(2)}) collective-permute-start(f32[32,256]{1,0:T(8,128)S(1)} %fusion.41), channel_id=1, source_target_pairs={{0,1},{1,2},{2,3},{3,4},{4,5},{5,6},{6,7},{7,8},{8,9},{9,10},{10,1... | collective-permute-start | bytes 98312 | tf_op jit(solution)/shard_map/ppermute | solution.py:52
  22.7 9.2 %collective-permute-start.5 = (f32[32,256]{1,0:T(8,128)S(1)}, f32[32,256]{1,0:T(8,128)S(1)}, u32[]{:S(2)}, u32[]{:S(2)}) collective-permute-start(f32[32,256]{1,0:T(8,128)S(1)} %fusion.75), channel_id=1, source_target_pairs={{1,0},{2,1},{3,2},{4,3},{5,4},{6,5},{7,6},{8,7},{9,8},{10,9},{11,1... | collective-permute-start | bytes 98312 | tf_op jit(solution)/shard_map/ppermute | solution.py:50
  27.3 5.6 %collective-permute-start.4 = (f32[32,256]{1,0:T(8,128)S(1)}, f32[32,256]{1,0:T(8,128)S(1)}, u32[]{:S(2)}, u32[]{:S(2)}) collective-permute-start(f32[32,256]{1,0:T(8,128)S(1)} %fusion.38), channel_id=1, source_target_pairs={{0,1},{1,2},{2,3},{3,4},{4,5},{5,6},{6,7},{7,8},{8,9},{9,10},{10,1... | collective-permute-start | bytes 98312 | tf_op jit(solution)/shard_map/ppermute | solution.py:52
  32.9 9.9 %collective-permute-start.7 = (f32[32,256]{1,0:T(8,128)S(1)}, f32[32,256]{1,0:T(8,128)S(1)}, u32[]{:S(2)}, u32[]{:S(2)}) collective-permute-start(f32[32,256]{1,0:T(8,128)S(1)} %fusion.74), channel_id=1, source_target_pairs={{1,0},{2,1},{3,2},{4,3},{5,4},{6,5},{7,6},{8,7},{9,8},{10,9},{11,1... | collective-permute-start | bytes 98312 | tf_op jit(solution)/shard_map/ppermute | solution.py:50
  35.9 6.9 %collective-permute-start.6 = (f32[32,256]{1,0:T(8,128)S(1)}, f32[32,256]{1,0:T(8,128)S(1)}, u32[]{:S(2)}, u32[]{:S(2)}) collective-permute-start(f32[32,256]{1,0:T(8,128)S(1)} %fusion.35), channel_id=1, source_target_pairs={{0,1},{1,2},{2,3},{3,4},{4,5},{5,6},{6,7},{7,8},{8,9},{9,10},{10,1... | collective-permute-start | bytes 98312 | tf_op jit(solution)/shard_map/ppermute | solution.py:52
  69.0 9.6 %collective-permute-start.8 = (f32[512,512]{1,0:T(8,128)S(1)}, f32[512,512]{1,0:T(8,128)S(1)}, u32[]{:S(2)}, u32[]{:S(2)}) collective-permute-start(f32[512,512]{1,0:T(8,128)S(1)} %bitcast.115), channel_id=1, source_target_pairs={{0,16},{16,0},{1,17},{17,1},{2,18},{18,2},{3,19},{19,3},{4,20},{20... | collective-permute-start | bytes 3145736 | tf_op jit(solution)/shard_map/ppermute | solution.py:176
  80.3 1.0 copy-start.1
  137.6 0.8 copy-start.3
  138.4 25.1 %all-to-all-start.3 = ((f32[64,1,2176]{2,1,0:T(1,128)}), f32[64,1,2176]{2,1,0:T(1,128)}, u32[]{:S(2)}, u32[]{:S(2)}) async-start(f32[64,1,2176]{2,1,0:T(1,128)} %bitcast.121), calls=%async_computation.3 | async-start | bytes 1114112 | tf_op jit(solution)/shard_map/all_to_all | solution.py:182
  163.5 1.2 copy-start.2

commit v3 on v2

--- a/solution.py
+++ b/solution.py
@@ -6,6 +6,7 @@
 from jax.experimental import pallas as pl
 from jax.experimental.pallas import tpu as pltpu
 from jax.sharding import Mesh, PartitionSpec as P
+
 
 DEGREE = 4
 
@@ -40,20 +41,25 @@
     count = vectors.shape[0]
     blocks, size = diag_blocks.shape[0], diag_blocks.shape[1]
     rows = lax.axis_size(ROW)
-    forward = [(i, i + 1) for i in range(rows - 1)]
-    backward = [(target, source) for source, target in forward]
+    swaps = []
+    for start in (1, 0):
+        ups = [(i, i + 1) for i in range(start, rows - 1, 2)]
+        swaps.append(ups + [(above, below) for below, above in ups])
+    is_odd = lax.axis_index(ROW) % 2 == 1
     y = vectors.reshape(count, blocks, size).transpose(1, 0, 2)
     last_coupling = coupling[-1]
     first, last = y[0], y[-1]
     previous = None
     for turn in range(DEGREE):
-        from_above = lax.ppermute(first, ROW, backward)
         last_term = dot(last, last_coupling, ((1,), (0,)))
-        from_below = lax.ppermute(last_term, ROW, forward)
+        odd = lax.ppermute(jnp.where(is_odd, last_term, first), ROW, swaps[0])
+        even = lax.ppermute(jnp.where(is_odd, first, last_term), ROW, swaps[1])
         scale = (1.0 if turn == 0 else 2.0) / filter_half
         inner = scale * local_terms(y, diag_blocks, coupling)
         if previous is not None:
             inner = inner - previous
+        from_above = jnp.where(is_odd, odd, even)
+        from_below = jnp.where(is_odd, even, odd)
         last = inner[-1] + scale * dot(from_above, last_coupling, ((1,), (1,)))
         first = inner[0] + scale * from_below
         previous = y
@@ -145,7 +151,7 @@
     out_ref[...] = result
 
 
-def call(kernel, out_shape, name, scalars, *arrays):
+def call(kernel, out_shape, scalars, *arrays):
     vmem = pl.BlockSpec(memory_space=pltpu.VMEM)
     smem = pl.BlockSpec(memory_space=pltpu.SMEM)
     return pl.pallas_call(
@@ -153,7 +159,6 @@
         out_shape=jax.ShapeDtypeStruct(out_shape, jnp.float32),
         in_specs=[smem] * len(scalars) + [vmem] * len(arrays),
         out_specs=vmem,
-        name=name,
         compiler_params=pltpu.CompilerParams(vmem_limit_bytes=24 * 2**20),
         interpret=INTERPRET,
     )(*scalars, *arrays)
@@ -161,9 +166,10 @@
 
 def local(diag_blocks, coupling, vectors):
     count = vectors.shape[0]
+    at, vectors = lax.optimization_barrier((lax.axis_index("x").reshape(1), vectors))
     y = chebyshev(vectors, diag_blocks, coupling)
     blocks, _, size = y.shape
-    nyl, nx, nc = (lax.axis_size(a) for a in VEC)
+    nyl, nx, _ = (lax.axis_size(a) for a in VEC)
     total_rows = blocks * size * lax.axis_size(ROW)
     swapped = lax.all_to_all(y, "yl", split_axis=0, concat_axis=0, tiled=True)
     part = blocks // nyl
@@ -181,17 +187,10 @@
         a = a.reshape(lax.axis_size(SUM), -1)
         return lax.all_to_all(a, SUM, split_axis=0, concat_axis=0, tiled=True).reshape(packed)
 
-    pieces = exchange(call(gram_kernel, packed, "gram", (), own, near, far))
-    summed = exchange(call(sum_kernel, packed, "sum", (), pieces))
+    pieces = exchange(call(gram_kernel, packed, (), own, near, far))
+    summed = exchange(call(sum_kernel, packed, (), pieces))
     renewed = call(
-        functools.partial(mixing_kernel, total_rows),
-        (group, depth),
-        "mixing",
-        (lax.axis_index("x").reshape(1),),
-        summed,
-        own,
-        near,
-        far,
+        functools.partial(mixing_kernel, total_rows), (group, depth), (at,), summed, own, near, far
     )
     return lax.all_to_all(renewed, "yl", split_axis=0, concat_axis=1, tiled=True)
 

time: 179 us -> 161 us (0.90)
  waiting for transfers between devices: 20.7 us -> 2.29 us
  blocking collectives: 90.6 us -> 97.5 us
  local copies, waits for them, and re-layouts: 5.29 us -> 2.26 us
  starting transfers between devices: 40.4 us -> 38.1 us
    all_to_all x1 -> x0, waiting for transfers between devices: 17.9 us -> none  [exchange(): lax.all_to_all(a, SUM, split_axis=0, concat_axis=0, tiled=True)]
    all_to_all x1 -> x2, blocking collectives: 56.3 us -> 64.8 us  [exchange(): lax.all_to_all(a, SUM, split_axis=0, concat_axis=0, tiled=True)]
    all_to_all x1 -> x0, starting transfers between devices: 7.22 us -> none  [exchange(): lax.all_to_all(a, SUM, split_axis=0, concat_axis=0, tiled=True)]
    ppermute x8, starting transfers between devices: 25.8 us -> 29.3 us  [the longest x4 26.6 us: chebyshev(): even = lax.ppermute(jnp.where(is_odd, first, last_term), ROW, swaps[1])]
    unnamed x13 -> x7, local copies, waits for them, and re-layouts: 3.07 us -> 0.04 us
  transfers between devices with their start and end apart: 10 -> 9, of which waited for: 3 -> 1; matrix products, arithmetic and copies ran while one was open for 9% -> 8% of each run, Pallas kernels for 0% -> 0%
where the time goes in v3:
time: 161 us; the launch traced here: 158 us
  blocking collectives  97.5 us (61%)
  starting transfers between devices  38.1 us (24%)
  matrix products  15.3 us (10%)
  Pallas kernels  2.48 us (2%)
  waiting for transfers between devices  2.29 us (1%)
  local copies, waits for them, and re-layouts  2.26 us (1%)
    all_to_all x2, blocking collectives, exchange(): lax.all_to_all(a, SUM, split_axis=0, concat_axis=0, tiled=True)  64.8 us
    ppermute x4, starting transfers between devices, chebyshev(): even = lax.ppermute(jnp.where(is_odd, first, last_term), ROW, swaps[1])  26.6 us
    dot_general x20, matrix products, dot(): return lax.dot_general(a, b, (contract, batch), precision=precision)  15.3 us
    all_to_all x1, blocking collectives, local(): near = lax.all_to_all(copies, 'x', split_axis=0, concat_axis=0, tiled=True)  13.6 us
    all_to_all x1, blocking collectives, local(): swapped = lax.all_to_all(y, 'yl', split_axis=0, concat_axis=0, tiled=True)  10.4 us
    ppermute x1, starting transfers between devices, local(): far = lax.ppermute(near, 'c', [(0, 1), (1, 0)])  8.85 us
    all_to_all x1, blocking collectives, local(): lax.all_to_all(renewed, 'yl', split_axis=0, concat_axis=1, tiled=True)  8.82 us
  transfers between devices with their start and end apart: 9, of which 1 were waited for; matrix products, arithmetic and copies ran while one was open for 8% of the time, Pallas kernels for 0%

profile of v3, /device:TPU:1, one launch (start us, length us, event | category | flops | bytes accessed | tf_op | source)
XLA Modules:
  0.0 158.4 jit_solution(7230670812156224776)
XLA Ops:
  0.0 0.0 copy-start
  0.0 0.0 copy-start.2
  0.0 0.0 copy-start.1
  0.0 1.1 copy.26
  1.1 1.2 fusion.82
  2.4 4.8 %collective-permute-start = (f32[32,256]{1,0:T(8,128)S(1)}, f32[32,256]{1,0:T(8,128)S(1)}, u32[]{:S(2)}, u32[]{:S(2)}) collective-permute-start(f32[32,256]{1,0:T(8,128)S(1)} %get-tuple-element.15), channel_id=1, source_target_pairs={{0,1},{2,3},{4,5},{6,7},{8,9},{10,11},{12,13},{14,15},{1,0},{3,2},... | collective-permute-start | bytes 98312 | tf_op jit(solution)/shard_map/ppermute | solution.py:56
  7.2 0.7 collective-permute-start.1
  7.9 2.6 %fusion.32 = f32[7,32,256]{2,1,0:T(8,128)S(1)} fusion(f32[8,256,256]{2,1,0:T(8,128)} %param.4, f32[4,8,8,256]{3,2,1,0:T(8,128)} %bitcast.140), kind=kOutput, calls=%fused_computation.40 | convolution fusion | flops 88080384 | bytes 2326528 | tf_op jit(solution)/shard_map/dot_general | solution.py:28
  10.4 0.0 copy-done.2
  10.5 0.0 copy-done.1
  10.5 0.7 fusion.30
  11.2 0.0 copy-done
  11.2 1.0 fusion.4
  12.2 0.0 collective-permute-done
  12.2 0.0 collective-permute-done.1
  12.2 0.3 convolution_add_fusion
  12.5 0.2 broadcast_select_fusion.4
  12.7 7.3 %collective-permute-start.2 = (f32[32,256]{1,0:T(8,128)S(1)}, f32[32,256]{1,0:T(8,128)S(1)}, u32[]{:S(2)}, u32[]{:S(2)}) collective-permute-start(f32[32,256]{1,0:T(8,128)S(1)} %broadcast_select_fusion.5), channel_id=1, source_target_pairs={{0,1},{2,3},{4,5},{6,7},{8,9},{10,11},{12,13},{14,15},{1,0},{3,2},... | collective-permute-start | bytes 98312 | tf_op jit(solution)/shard_map/ppermute | solution.py:56
  20.1 0.7 collective-permute-start.3
  20.8 0.7 fusion.26
  21.5 1.0 fusion.28
  22.4 1.0 fusion.13
  23.5 0.0 collective-permute-done.2
  23.5 0.0 collective-permute-done.3
  23.5 0.3 fusion.17
  23.8 0.2 broadcast_select_fusion.2
  24.0 7.7 %collective-permute-start.4 = (f32[32,256]{1,0:T(8,128)S(1)}, f32[32,256]{1,0:T(8,128)S(1)}, u32[]{:S(2)}, u32[]{:S(2)}) collective-permute-start(f32[32,256]{1,0:T(8,128)S(1)} %broadcast_select_fusion.3), channel_id=1, source_target_pairs={{0,1},{2,3},{4,5},{6,7},{8,9},{10,11},{12,13},{14,15},{1,0},{3,2},... | collective-permute-start | bytes 98312 | tf_op jit(solution)/shard_map/ppermute | solution.py:56
  31.7 0.7 collective-permute-start.5
  32.4 0.7 fusion.22
  33.1 1.0 fusion.24
  34.0 1.0 fusion.11
  35.1 0.0 collective-permute-done.4
  35.1 0.0 collective-permute-done.5
  35.1 0.3 fusion.16
  35.4 0.2 broadcast_select_fusion.1
  35.6 0.7 collective-permute-start.7
  36.3 6.8 %collective-permute-start.6 = (f32[32,256]{1,0:T(8,128)S(1)}, f32[32,256]{1,0:T(8,128)S(1)}, u32[]{:S(2)}, u32[]{:S(2)}) collective-permute-start(f32[32,256]{1,0:T(8,128)S(1)} %get-tuple-element.9), channel_id=1, source_target_pairs={{0,1},{2,3},{4,5},{6,7},{8,9},{10,11},{12,13},{14,15},{1,0},{3,2},... | collective-permute-start | bytes 98312 | tf_op jit(solution)/shard_map/ppermute | solution.py:56
  43.1 0.7 fusion.18
  43.8 1.0 fusion.20
  44.8 1.0 fusion.9
  45.8 0.0 collective-permute-done.7
  45.9 0.0 collective-permute-done.6
  45.9 0.3 fusion.15
  46.2 10.4 %all_to_all.47 = f32[8,32,256]{2,1,0:T(8,128)S(1)} all-to-all(f32[8,32,256]{2,1,0:T(8,128)S(1)} %pad_maximum_fusion.3), channel_id=1, replica_groups=mesh['yl'=4,'x'=4,'c'=2,'yh'=2,'z'=8] {'yl'}, dimensions={0} | all-to-all | bytes 524288 | tf_op jit(solution)/shard_map/all_to_all | solution.py:174
  56.6 0.2 copy.10
  56.8 0.1 broadcast_in_dim.37
  56.9 13.6 %all_to_all.48 = f32[4,128,512]{2,1,0:T(8,128)S(1)} all-to-all(f32[4,128,512]{2,1,0:T(8,128)S(1)} %broadcast_in_dim.37), channel_id=1, replica_groups=mesh['yl'=4,'x'=4,'c'=2,'yh'=2,'z'=8] {'x'}, dimensions={0} | all-to-all | bytes 2097152 | tf_op jit(solution)/shard_map/all_to_all | solution.py:180
  70.5 8.9 %collective-permute-start.8 = (f32[512,512]{1,0:T(8,128)S(1)}, f32[512,512]{1,0:T(8,128)S(1)}, u32[]{:S(2)}, u32[]{:S(2)}) collective-permute-start(f32[512,512]{1,0:T(8,128)S(1)} %bitcast.128), channel_id=1, source_target_pairs={{0,16},{16,0},{1,17},{17,1},{2,18},{18,2},{3,19},{19,3},{4,20},{20... | collective-permute-start | bytes 3145736 | tf_op jit(solution)/shard_map/ppermute | solution.py:182
  79.3 2.3 %collective-permute-done.8.far_ref = f32[512,512]{1,0:T(8,128)S(1)} collective-permute-done((f32[512,512]{1,0:T(8,128)S(1)}, f32[512,512]{1,0:T(8,128)S(1)}, u32[]{:S(2)}, u32[]{:S(2)}) %collective-permute-start.8) | collective-permute-done | bytes 1048608 | tf_op jit(solution)/shard_map/ppermute | solution.py:182
  81.6 1.7 %shard_map.37 = f32[1088,128]{1,0:T(8,128)S(1)} custom-call(f32[128,512]{1,0:T(8,128)S(1)} %bitcast.132, f32[512,512]{1,0:T(8,128)S(1)} %bitcast.129, f32[512,512]{1,0:T(8,128)S(1)} %collective-permute-done.8.far_ref), custom_call_target="tpu_custom_call" | custom-call | tf_op jit(solution)/shard_map/pallas_call | solution.py:157
  83.3 40.0 %all_to_all.49 = f32[64,1,2176]{2,1,0:T(1,128)S(1)} all-to-all(f32[64,1,2176]{2,1,0:T(1,128)S(1)} %bitcast.137), channel_id=1, replica_groups=mesh['yl'=4,'x'=4,'c'=2,'yh'=2,'z'=8] {'yl','yh','z'}, dimensions={0} | all-to-all | bytes 1114112 | tf_op jit(solution)/shard_map/all_to_all | solution.py:188
  123.3 0.1 shard_map.38
  123.4 24.8 %all_to_all.50 = f32[64,1,2176]{2,1,0:T(1,128)S(1)} all-to-all(f32[64,1,2176]{2,1,0:T(1,128)S(1)} %bitcast.136), channel_id=1, replica_groups=mesh['yl'=4,'x'=4,'c'=2,'yh'=2,'z'=8] {'yl','yh','z'}, dimensions={0} | all-to-all | bytes 1114112 | tf_op jit(solution)/shard_map/all_to_all | solution.py:188
  148.1 0.7 shard_map.39
  148.9 8.8 %all_to_all.51 = f32[4,32,512]{2,1,0:T(8,128)S(1)} all-to-all(f32[4,32,512]{2,1,0:T(8,128)S(1)} %bitcast.138), channel_id=1, replica_groups=mesh['yl'=4,'x'=4,'c'=2,'yh'=2,'z'=8] {'yl'}, dimensions={0} | all-to-all | bytes 524288 | tf_op jit(solution)/shard_map/all_to_all | solution.py:195
  157.7 0.7 copy.15
  (10 shorter events, 0.1 us)
Async XLA Ops:
  0.0 11.2 %copy-start = (f32[8,256,256]{2,1,0:T(8,128)S(1)}, f32[8,256,256]{2,1,0:T(8,128)}, u32[]{:S(2)}) copy-start(f32[8,256,256]{2,1,0:T(8,128)} %param.3) | copy-start | bytes 6291460
  0.0 10.5 %copy-start.2 = (f32[32,2048]{1,0:T(8,128)S(1)}, f32[32,2048]{1,0:T(8,128)}, u32[]{:S(2)}) copy-start(f32[32,2048]{1,0:T(8,128)} %param.5) | copy-start | bytes 786436
  0.0 10.5 %copy-start.1 = (f32[8,256,256]{2,1,0:T(8,128)S(1)}, f32[8,256,256]{2,1,0:T(8,128)}, u32[]{:S(2)}) copy-start(f32[8,256,256]{2,1,0:T(8,128)} %param.4) | copy-start | bytes 6291460
  2.4 9.8 %collective-permute-start = (f32[32,256]{1,0:T(8,128)S(1)}, f32[32,256]{1,0:T(8,128)S(1)}, u32[]{:S(2)}, u32[]{:S(2)}) collective-permute-start(f32[32,256]{1,0:T(8,128)S(1)} %get-tuple-element.15), channel_id=1, source_target_pairs={{0,1},{2,3},{4,5},{6,7},{8,9},{10,11},{12,13},{14,15},{1,0},{3,2},... | collective-permute-start | bytes 98312 | tf_op jit(solution)/shard_map/ppermute | solution.py:56
  7.2 5.0 %collective-permute-start.1 = (f32[32,256]{1,0:T(8,128)S(1)}, f32[32,256]{1,0:T(8,128)S(1)}, u32[]{:S(2)}, u32[]{:S(2)}) collective-permute-start(f32[32,256]{1,0:T(8,128)S(1)} %get-tuple-element.16), channel_id=1, source_target_pairs={{1,2},{3,4},{5,6},{7,8},{9,10},{11,12},{13,14},{2,1},{4,3},{6,5},{... | collective-permute-start | bytes 98312 | tf_op jit(solution)/shard_map/ppermute | solution.py:55
  12.7 10.8 %collective-permute-start.2 = (f32[32,256]{1,0:T(8,128)S(1)}, f32[32,256]{1,0:T(8,128)S(1)}, u32[]{:S(2)}, u32[]{:S(2)}) collective-permute-start(f32[32,256]{1,0:T(8,128)S(1)} %broadcast_select_fusion.5), channel_id=1, source_target_pairs={{0,1},{2,3},{4,5},{6,7},{8,9},{10,11},{12,13},{14,15},{1,0},{3,2},... | collective-permute-start | bytes 98312 | tf_op jit(solution)/shard_map/ppermute | solution.py:56
  20.1 3.4 %collective-permute-start.3 = (f32[32,256]{1,0:T(8,128)S(1)}, f32[32,256]{1,0:T(8,128)S(1)}, u32[]{:S(2)}, u32[]{:S(2)}) collective-permute-start(f32[32,256]{1,0:T(8,128)S(1)} %get-tuple-element.13), channel_id=1, source_target_pairs={{1,2},{3,4},{5,6},{7,8},{9,10},{11,12},{13,14},{2,1},{4,3},{6,5},{... | collective-permute-start | bytes 98312 | tf_op jit(solution)/shard_map/ppermute | solution.py:55
  24.0 11.1 %collective-permute-start.4 = (f32[32,256]{1,0:T(8,128)S(1)}, f32[32,256]{1,0:T(8,128)S(1)}, u32[]{:S(2)}, u32[]{:S(2)}) collective-permute-start(f32[32,256]{1,0:T(8,128)S(1)} %broadcast_select_fusion.3), channel_id=1, source_target_pairs={{0,1},{2,3},{4,5},{6,7},{8,9},{10,11},{12,13},{14,15},{1,0},{3,2},... | collective-permute-start | bytes 98312 | tf_op jit(solution)/shard_map/ppermute | solution.py:56
  31.7 3.4 %collective-permute-start.5 = (f32[32,256]{1,0:T(8,128)S(1)}, f32[32,256]{1,0:T(8,128)S(1)}, u32[]{:S(2)}, u32[]{:S(2)}) collective-permute-start(f32[32,256]{1,0:T(8,128)S(1)} %get-tuple-element.11), channel_id=1, source_target_pairs={{1,2},{3,4},{5,6},{7,8},{9,10},{11,12},{13,14},{2,1},{4,3},{6,5},{... | collective-permute-start | bytes 98312 | tf_op jit(solution)/shard_map/ppermute | solution.py:55
  35.6 10.2 %collective-permute-start.7 = (f32[32,256]{1,0:T(8,128)S(1)}, f32[32,256]{1,0:T(8,128)S(1)}, u32[]{:S(2)}, u32[]{:S(2)}) collective-permute-start(f32[32,256]{1,0:T(8,128)S(1)} %broadcast_select_fusion), channel_id=1, source_target_pairs={{1,2},{3,4},{5,6},{7,8},{9,10},{11,12},{13,14},{2,1},{4,3},{6,5},{... | collective-permute-start | bytes 98312 | tf_op jit(solution)/shard_map/ppermute | solution.py:55
  36.3 9.6 %collective-permute-start.6 = (f32[32,256]{1,0:T(8,128)S(1)}, f32[32,256]{1,0:T(8,128)S(1)}, u32[]{:S(2)}, u32[]{:S(2)}) collective-permute-start(f32[32,256]{1,0:T(8,128)S(1)} %get-tuple-element.9), channel_id=1, source_target_pairs={{0,1},{2,3},{4,5},{6,7},{8,9},{10,11},{12,13},{14,15},{1,0},{3,2},... | collective-permute-start | bytes 98312 | tf_op jit(solution)/shard_map/ppermute | solution.py:56
  70.5 11.1 %collective-permute-start.8 = (f32[512,512]{1,0:T(8,128)S(1)}, f32[512,512]{1,0:T(8,128)S(1)}, u32[]{:S(2)}, u32[]{:S(2)}) collective-permute-start(f32[512,512]{1,0:T(8,128)S(1)} %bitcast.128), channel_id=1, source_target_pairs={{0,16},{16,0},{1,17},{17,1},{2,18},{18,2},{3,19},{19,3},{4,20},{20... | collective-permute-start | bytes 3145736 | tf_op jit(solution)/shard_map/ppermute | solution.py:182

commit v4 on v3

--- a/solution.py
+++ b/solution.py
@@ -28,42 +28,53 @@
     return lax.dot_general(a, b, (contract, batch), precision=precision)
 
 
+def flipped(yh, z):
+    return (yh + z) % 2 == 0
+
+
+def snake():
+    nyl, nyh, nz = (lax.axis_size(a) for a in SUM)
+    places = []
+    for yh in range(nyh):
+        for z in range(nz):
+            order = range(nyl)
+            for yl in reversed(order) if flipped(yh, z) else order:
+                places.append((yl * nyh + yh) * nz + z)
+    return places
+
+
 def local_terms(y, diag_blocks, coupling):
-    batch = ((0,), (0,))
-    result = dot(y, diag_blocks, ((2,), (2,)), batch) - filter_center * y
-    upper = dot(y[1:], coupling[:-1], ((2,), (2,)), batch)
-    lower = dot(y[:-1], coupling[:-1], ((2,), (1,)), batch)
-    none = jnp.zeros_like(y[:1])
-    return result + jnp.concatenate([upper, none]) + jnp.concatenate([none, lower])
-
-
-def chebyshev(vectors, diag_blocks, coupling):
-    count = vectors.shape[0]
-    blocks, size = diag_blocks.shape[0], diag_blocks.shape[1]
-    rows = lax.axis_size(ROW)
+    terms = []
+    for n, block in enumerate(y):
+        term = dot(block, diag_blocks[n], ((1,), (1,))) - filter_center * block
+        if n + 1 < len(y):
+            term = term + dot(y[n + 1], coupling[n], ((1,), (1,)))
+        if n > 0:
+            term = term + dot(y[n - 1], coupling[n - 1], ((1,), (0,)))
+        terms.append(term)
+    return terms
+
+
+def chebyshev(y, diag_blocks, coupling, is_odd):
+    places = snake()
     swaps = []
     for start in (1, 0):
-        ups = [(i, i + 1) for i in range(start, rows - 1, 2)]
+        ups = [(places[i], places[i + 1]) for i in range(start, len(places) - 1, 2)]
         swaps.append(ups + [(above, below) for below, above in ups])
-    is_odd = lax.axis_index(ROW) % 2 == 1
-    y = vectors.reshape(count, blocks, size).transpose(1, 0, 2)
-    last_coupling = coupling[-1]
-    first, last = y[0], y[-1]
     previous = None
     for turn in range(DEGREE):
-        last_term = dot(last, last_coupling, ((1,), (0,)))
-        odd = lax.ppermute(jnp.where(is_odd, last_term, first), ROW, swaps[0])
-        even = lax.ppermute(jnp.where(is_odd, first, last_term), ROW, swaps[1])
+        last_term = dot(y[-1], coupling[-1], ((1,), (0,)))
+        odd = lax.ppermute(jnp.where(is_odd, last_term, y[0]), SUM, swaps[0])
+        even = lax.ppermute(jnp.where(is_odd, y[0], last_term), SUM, swaps[1])
         scale = (1.0 if turn == 0 else 2.0) / filter_half
-        inner = scale * local_terms(y, diag_blocks, coupling)
+        inner = [scale * term for term in local_terms(y, diag_blocks, coupling)]
         if previous is not None:
-            inner = inner - previous
+            inner = [term - old for term, old in zip(inner, previous)]
         from_above = jnp.where(is_odd, odd, even)
         from_below = jnp.where(is_odd, even, odd)
-        last = inner[-1] + scale * dot(from_above, last_coupling, ((1,), (1,)))
-        first = inner[0] + scale * from_below
-        previous = y
-        y = jnp.concatenate([first[None], inner[1:-1], last[None]])
+        inner[-1] = inner[-1] + scale * dot(from_above, coupling[-1], ((1,), (1,)))
+        inner[0] = inner[0] + scale * from_below
+        previous, y = y, inner
     return y
 
 
@@ -165,17 +176,28 @@
 
 
 def local(diag_blocks, coupling, vectors):
-    count = vectors.shape[0]
+    count, width = vectors.shape
+    blocks, size = diag_blocks.shape[0], diag_blocks.shape[1]
+    nyl, nx, _ = (lax.axis_size(a) for a in VEC)
+    total_rows = width * lax.axis_size(ROW)
     at, vectors = lax.optimization_barrier((lax.axis_index("x").reshape(1), vectors))
-    y = chebyshev(vectors, diag_blocks, coupling)
-    blocks, _, size = y.shape
-    nyl, nx, _ = (lax.axis_size(a) for a in VEC)
-    total_rows = blocks * size * lax.axis_size(ROW)
-    swapped = lax.all_to_all(y, "yl", split_axis=0, concat_axis=0, tiled=True)
-    part = blocks // nyl
-    own = swapped.reshape(nyl, part, count, size).transpose(0, 2, 1, 3)
-    own = own.reshape(nyl * count, part * size)
-    group, depth = own.shape
+    flip = flipped(lax.axis_index("yh"), lax.axis_index("z"))
+    yl = lax.axis_index("yl")
+    chunk = jnp.where(flip, nyl - 1 - yl, yl)
+    part, group, depth = blocks // nyl, nyl * count, width // nyl
+    chunks = vectors.reshape(count, nyl, depth).transpose(1, 0, 2)
+    chunks = jnp.where(flip, chunks[::-1], chunks)
+    own = lax.all_to_all(chunks, "yl", split_axis=0, concat_axis=0, tiled=True)
+    own = own.reshape(group, depth)
+    own = jnp.concatenate(
+        chebyshev(
+            [own[:, n * size : (n + 1) * size] for n in range(part)],
+            lax.dynamic_slice_in_dim(diag_blocks, chunk * part, part),
+            lax.dynamic_slice_in_dim(coupling, chunk * part, part),
+            chunk % 2 == 1,
+        ),
+        axis=1,
+    )
     copies = jnp.broadcast_to(own[None], (nx, group, depth))
     near = lax.all_to_all(copies, "x", split_axis=0, concat_axis=0, tiled=True)
     near = near.reshape(nx * group, depth)
@@ -192,7 +214,10 @@
     renewed = call(
         functools.partial(mixing_kernel, total_rows), (group, depth), (at,), summed, own, near, far
     )
-    return lax.all_to_all(renewed, "yl", split_axis=0, concat_axis=1, tiled=True)
+    back = renewed.reshape(nyl, count, depth)
+    back = lax.all_to_all(back, "yl", split_axis=0, concat_axis=0, tiled=True)
+    back = jnp.where(flip, back[::-1], back)
+    return back.transpose(1, 0, 2).reshape(count, width)
 
 
 def solution(mesh):

time: 161 us -> 161 us (level)
  waiting for transfers between devices: 2.29 us -> 17.8 us
  blocking collectives: 97.5 us -> 85.3 us
  matrix products: 15.3 us -> 8.97 us
  starting transfers between devices: 38.1 us -> 39.9 us
    all_to_all x2 -> x1, blocking collectives: 19.2 us -> 8.83 us  [local(): back = lax.all_to_all(back, 'yl', split_axis=0, concat_axis=0, tiled=True)]
    ppermute x8, waiting for transfers between devices: 0.02 us -> 9.91 us  [the longest x4 5.83 us: chebyshev(): odd = lax.ppermute(jnp.where(is_odd, last_term, y[0]), SUM, swaps[0])]
    dot_general x20 -> x24, matrix products: 15.3 us -> 8.97 us  [dot(): return lax.dot_general(a, b, (contract, batch), precision=precision)]
    all_to_all x0 -> x1, waiting for transfers between devices: none -> 5.63 us  [local(): own = lax.all_to_all(chunks, 'yl', split_axis=0, concat_axis=0, tiled=True)]
    all_to_all x0 -> x1, starting transfers between devices: none -> 5.41 us  [local(): own = lax.all_to_all(chunks, 'yl', split_axis=0, concat_axis=0, tiled=True)]
    ppermute x8, starting transfers between devices: 29.3 us -> 24.1 us  [the longest x4 14.7 us: chebyshev(): odd = lax.ppermute(jnp.where(is_odd, last_term, y[0]), SUM, swaps[0])]
    all_to_all x2, blocking collectives: 64.8 us -> 63.1 us  [exchange(): lax.all_to_all(a, SUM, split_axis=0, concat_axis=0, tiled=True)]
  transfers between devices with their start and end apart: 9 -> 10, of which waited for: 1 -> 7; matrix products, arithmetic and copies ran while one was open for 8% -> 2% of each run, Pallas kernels for 0% -> 0%
where the time goes in v4:
time: 161 us; the launch traced here: 158 us
  blocking collectives  85.3 us (53%)
  starting transfers between devices  39.9 us (25%)
  waiting for transfers between devices  17.8 us (11%)
  matrix products  8.97 us (6%)
  Pallas kernels  2.49 us (2%)
  local copies, waits for them, and re-layouts  1.96 us (1%)
    all_to_all x2, blocking collectives, exchange(): lax.all_to_all(a, SUM, split_axis=0, concat_axis=0, tiled=True)  63.1 us
    ppermute x4, starting transfers between devices, chebyshev(): odd = lax.ppermute(jnp.where(is_odd, last_term, y[0]), SUM, swaps[0])  14.7 us
    all_to_all x1, blocking collectives, local(): near = lax.all_to_all(copies, 'x', split_axis=0, concat_axis=0, tiled=True)  13.4 us
    ppermute x1, starting transfers between devices, local(): far = lax.ppermute(near, 'c', [(0, 1), (1, 0)])  10.4 us
    ppermute x4, starting transfers between devices, chebyshev(): even = lax.ppermute(jnp.where(is_odd, y[0], last_term), SUM, swaps[1])  9.42 us
    dot_general x24, matrix products, dot(): return lax.dot_general(a, b, (contract, batch), precision=precision)  8.97 us
    all_to_all x1, blocking collectives, local(): back = lax.all_to_all(back, 'yl', split_axis=0, concat_axis=0, tiled=True)  8.83 us
    ppermute x4, waiting for transfers between devices, chebyshev(): odd = lax.ppermute(jnp.where(is_odd, last_term, y[0]), SUM, swaps[0])  5.83 us
  transfers between devices with their start and end apart: 10, of which 7 were waited for; matrix products, arithmetic and copies ran while one was open for 2% of the time, Pallas kernels for 0%

profile of v4, /device:TPU:1, one launch (start us, length us, event | category | flops | bytes accessed | tf_op | source)
XLA Modules:
  0.0 157.6 jit_solution(8312284778932205932)
XLA Ops:
  0.0 0.0 copy-start
  0.0 1.1 copy.13
  1.1 0.7 reverse_select_fusion.1
  1.9 5.4 %all-to-all-start = ((f32[4,32,512]{2,1,0:T(8,128)}), f32[4,32,512]{2,1,0:T(8,128)S(1)}, u32[]{:S(2)}, u32[]{:S(2)}) async-start(f32[4,32,512]{2,1,0:T(8,128)} %reverse_select_fusion.1), calls=%async_computation | async-start | bytes 524288 | tf_op jit(solution)/shard_map/all_to_all | solution.py:190
  7.3 5.6 %all-to-all-done = f32[4,32,512]{2,1,0:T(8,128)S(1)} async-done(((f32[4,32,512]{2,1,0:T(8,128)}), f32[4,32,512]{2,1,0:T(8,128)S(1)}, u32[]{:S(2)}, u32[]{:S(2)}) %all-to-all-start) | async-done | bytes 262176 | tf_op jit(solution)/shard_map/all_to_all | solution.py:190
  12.9 0.0 copy-start.1
  12.9 1.4 convolution_subtract_fusion.2
  14.3 0.0 copy-done
  14.3 0.2 convolution_add_fusion.4
  14.6 0.2 slice_select_fusion
  14.8 5.9 %collective-permute-start.1 = (f32[128,256]{1,0:T(8,128)S(1)}, f32[128,256]{1,0:T(8,128)S(1)}, u32[]{:S(2)}, u32[]{:S(2)}) collective-permute-start(f32[128,256]{1,0:T(8,128)S(1)} %get-tuple-element.9), channel_id=1, source_target_pairs={{256,128},{0,1},{129,257},{385,386},{258,130},{2,3},{131,259},{387... | collective-permute-start | bytes 393224 | tf_op jit(solution)/shard_map/ppermute | solution.py:67
  20.8 1.9 %collective-permute-start = (f32[128,256]{1,0:T(8,128)S(1)}, f32[128,256]{1,0:T(8,128)S(1)}, u32[]{:S(2)}, u32[]{:S(2)}) collective-permute-start(f32[128,256]{1,0:T(8,128)S(1)} %get-tuple-element.10), channel_id=1, source_target_pairs={{384,256},{128,0},{1,129},{257,385},{386,258},{130,2},{3,131},{259... | collective-permute-start | bytes 393224 | tf_op jit(solution)/shard_map/ppermute | solution.py:68
  22.7 1.3 convolution_subtract_fusion.4
  23.9 0.0 collective-permute-done.1
  24.0 2.8 %collective-permute-done = f32[128,256]{1,0:T(8,128)S(1)} collective-permute-done((f32[128,256]{1,0:T(8,128)S(1)}, f32[128,256]{1,0:T(8,128)S(1)}, u32[]{:S(2)}, u32[]{:S(2)}) %collective-permute-start) | collective-permute-done | bytes 131104 | tf_op jit(solution)/shard_map/ppermute | solution.py:68
  26.8 0.3 convolution_add_fusion.3
  27.1 0.0 copy-done.1
  27.1 0.3 fusion.24
  27.4 0.2 fusion.31
  27.6 0.3 broadcast_select_fusion.5
  28.0 1.9 %collective-permute-start.2 = (f32[128,256]{1,0:T(8,128)S(1)}, f32[128,256]{1,0:T(8,128)S(1)}, u32[]{:S(2)}, u32[]{:S(2)}) collective-permute-start(f32[128,256]{1,0:T(8,128)S(1)} %get-tuple-element.15), channel_id=1, source_target_pairs={{384,256},{128,0},{1,129},{257,385},{386,258},{130,2},{3,131},{259... | collective-permute-start | bytes 393224 | tf_op jit(solution)/shard_map/ppermute | solution.py:68
  29.9 1.9 %collective-permute-start.3 = (f32[128,256]{1,0:T(8,128)S(1)}, f32[128,256]{1,0:T(8,128)S(1)}, u32[]{:S(2)}, u32[]{:S(2)}) collective-permute-start(f32[128,256]{1,0:T(8,128)S(1)} %get-tuple-element.16), channel_id=1, source_target_pairs={{256,128},{0,1},{129,257},{385,386},{258,130},{2,3},{131,259},{387... | collective-permute-start | bytes 393224 | tf_op jit(solution)/shard_map/ppermute | solution.py:67
  31.8 0.3 fusion.12
  32.1 0.3 fusion.28
  32.4 1.3 collective-permute-done.2
  33.7 1.9 %collective-permute-done.3 = f32[128,256]{1,0:T(8,128)S(1)} collective-permute-done((f32[128,256]{1,0:T(8,128)S(1)}, f32[128,256]{1,0:T(8,128)S(1)}, u32[]{:S(2)}, u32[]{:S(2)}) %collective-permute-start.3) | collective-permute-done | bytes 131104 | tf_op jit(solution)/shard_map/ppermute | solution.py:67
  35.6 0.3 fusion.10
  35.9 0.3 fusion.23
  36.2 0.2 fusion.30
  36.5 0.3 broadcast_select_fusion.3
  36.8 3.7 %collective-permute-start.4 = (f32[128,256]{1,0:T(8,128)S(1)}, f32[128,256]{1,0:T(8,128)S(1)}, u32[]{:S(2)}, u32[]{:S(2)}) collective-permute-start(f32[128,256]{1,0:T(8,128)S(1)} %get-tuple-element.13), channel_id=1, source_target_pairs={{384,256},{128,0},{1,129},{257,385},{386,258},{130,2},{3,131},{259... | collective-permute-start | bytes 393224 | tf_op jit(solution)/shard_map/ppermute | solution.py:68
  40.5 3.2 %collective-permute-start.5 = (f32[128,256]{1,0:T(8,128)S(1)}, f32[128,256]{1,0:T(8,128)S(1)}, u32[]{:S(2)}, u32[]{:S(2)}) collective-permute-start(f32[128,256]{1,0:T(8,128)S(1)} %get-tuple-element.14), channel_id=1, source_target_pairs={{256,128},{0,1},{129,257},{385,386},{258,130},{2,3},{131,259},{387... | collective-permute-start | bytes 393224 | tf_op jit(solution)/shard_map/ppermute | solution.py:67
  43.7 0.3 fusion.27
  44.1 0.0 collective-permute-done.4
  44.1 2.1 %collective-permute-done.5 = f32[128,256]{1,0:T(8,128)S(1)} collective-permute-done((f32[128,256]{1,0:T(8,128)S(1)}, f32[128,256]{1,0:T(8,128)S(1)}, u32[]{:S(2)}, u32[]{:S(2)}) %collective-permute-start.5) | collective-permute-done | bytes 131104 | tf_op jit(solution)/shard_map/ppermute | solution.py:67
  46.2 0.3 convolution_multiply_fusion.1
  46.5 0.2 fusion.5
  46.8 0.3 fusion.25
  47.1 0.2 fusion.29
  47.3 0.3 broadcast_select_fusion.1
  47.7 1.9 %collective-permute-start.6 = (f32[128,256]{1,0:T(8,128)S(1)}, f32[128,256]{1,0:T(8,128)S(1)}, u32[]{:S(2)}, u32[]{:S(2)}) collective-permute-start(f32[128,256]{1,0:T(8,128)S(1)} %get-tuple-element.11), channel_id=1, source_target_pairs={{384,256},{128,0},{1,129},{257,385},{386,258},{130,2},{3,131},{259... | collective-permute-start | bytes 393224 | tf_op jit(solution)/shard_map/ppermute | solution.py:68
  49.6 3.5 %collective-permute-start.7 = (f32[128,256]{1,0:T(8,128)S(1)}, f32[128,256]{1,0:T(8,128)S(1)}, u32[]{:S(2)}, u32[]{:S(2)}) collective-permute-start(f32[128,256]{1,0:T(8,128)S(1)} %get-tuple-element.12), channel_id=1, source_target_pairs={{256,128},{0,1},{129,257},{385,386},{258,130},{2,3},{131,259},{387... | collective-permute-start | bytes 393224 | tf_op jit(solution)/shard_map/ppermute | solution.py:67
  53.2 0.2 fusion.2
  53.4 0.3 fusion.26
  53.7 0.0 collective-permute-done.6
  53.7 1.8 %collective-permute-done.7 = f32[128,256]{1,0:T(8,128)S(1)} collective-permute-done((f32[128,256]{1,0:T(8,128)S(1)}, f32[128,256]{1,0:T(8,128)S(1)}, u32[]{:S(2)}, u32[]{:S(2)}) %collective-permute-start.7) | collective-permute-done | bytes 131104 | tf_op jit(solution)/shard_map/ppermute | solution.py:67
  55.5 0.3 fusion.9
  55.8 0.3 fusion
  56.2 0.1 broadcast_in_dim.2
  56.3 13.4 %all_to_all.33 = f32[4,128,512]{2,1,0:T(8,128)S(1)} all-to-all(f32[4,128,512]{2,1,0:T(8,128)S(1)} %broadcast_in_dim.2), channel_id=1, replica_groups=mesh['yl'=4,'x'=4,'c'=2,'yh'=2,'z'=8] {'x'}, dimensions={0} | all-to-all | bytes 2097152 | tf_op jit(solution)/shard_map/all_to_all | solution.py:202
  69.7 10.4 %collective-permute-start.8 = (f32[512,512]{1,0:T(8,128)S(1)}, f32[512,512]{1,0:T(8,128)S(1)}, u32[]{:S(2)}, u32[]{:S(2)}) collective-permute-start(f32[512,512]{1,0:T(8,128)S(1)} %bitcast.78), channel_id=1, source_target_pairs={{0,16},{16,0},{1,17},{17,1},{2,18},{18,2},{3,19},{19,3},{4,20},{20... | collective-permute-start | bytes 3145736 | tf_op jit(solution)/shard_map/ppermute | solution.py:204
  80.2 2.3 %collective-permute-done.8.far_ref = f32[512,512]{1,0:T(8,128)S(1)} collective-permute-done((f32[512,512]{1,0:T(8,128)S(1)}, f32[512,512]{1,0:T(8,128)S(1)}, u32[]{:S(2)}, u32[]{:S(2)}) %collective-permute-start.8) | collective-permute-done | bytes 1048608 | tf_op jit(solution)/shard_map/ppermute | solution.py:204
  82.4 1.7 %shard_map.37 = f32[1088,128]{1,0:T(8,128)S(1)} custom-call(f32[128,512]{1,0:T(8,128)S(1)} %pad_maximum_fusion.own_ref, f32[512,512]{1,0:T(8,128)S(1)} %bitcast.79, f32[512,512]{1,0:T(8,128)S(1)} %collective-permute-done.8.far_ref), custom_call_target="tpu_custom_call" | custom-call | tf_op jit(solution)/shard_map/pallas_call | solution.py:168
  84.1 38.3 %all_to_all.34 = f32[64,1,2176]{2,1,0:T(1,128)S(1)} all-to-all(f32[64,1,2176]{2,1,0:T(1,128)S(1)} %bitcast.84), channel_id=1, replica_groups=mesh['yl'=4,'x'=4,'c'=2,'yh'=2,'z'=8] {'yl','yh','z'}, dimensions={0} | all-to-all | bytes 1114112 | tf_op jit(solution)/shard_map/all_to_all | solution.py:210
  122.4 0.1 shard_map.38
  122.5 24.8 %all_to_all.35 = f32[64,1,2176]{2,1,0:T(1,128)S(1)} all-to-all(f32[64,1,2176]{2,1,0:T(1,128)S(1)} %bitcast.83), channel_id=1, replica_groups=mesh['yl'=4,'x'=4,'c'=2,'yh'=2,'z'=8] {'yl','yh','z'}, dimensions={0} | all-to-all | bytes 1114112 | tf_op jit(solution)/shard_map/all_to_all | solution.py:210
  147.3 0.7 shard_map.39
  148.0 8.8 %all_to_all.36 = f32[4,32,512]{2,1,0:T(8,128)S(1)} all-to-all(f32[4,32,512]{2,1,0:T(8,128)S(1)} %bitcast.85), channel_id=1, replica_groups=mesh['yl'=4,'x'=4,'c'=2,'yh'=2,'z'=8] {'yl'}, dimensions={0} | all-to-all | bytes 524288 | tf_op jit(solution)/shard_map/all_to_all | solution.py:218
  156.9 0.7 copy.11
  (2 shorter events, 0.0 us)
Async XLA Ops:
  0.0 14.3 %copy-start = (f32[8,256,256]{2,1,0:T(8,128)S(1)}, f32[8,256,256]{2,1,0:T(8,128)}, u32[]{:S(2)}) copy-start(f32[8,256,256]{2,1,0:T(8,128)} %param.4) | copy-start | bytes 6291460
  1.9 11.0 %all-to-all-start = ((f32[4,32,512]{2,1,0:T(8,128)}), f32[4,32,512]{2,1,0:T(8,128)S(1)}, u32[]{:S(2)}, u32[]{:S(2)}) async-start(f32[4,32,512]{2,1,0:T(8,128)} %reverse_select_fusion.1), calls=%async_computation | async-start | bytes 524288 | tf_op jit(solution)/shard_map/all_to_all | solution.py:190
  12.9 14.2 %copy-start.1 = (f32[8,256,256]{2,1,0:T(8,128)S(1)}, f32[8,256,256]{2,1,0:T(8,128)}, u32[]{:S(2)}) copy-start(f32[8,256,256]{2,1,0:T(8,128)} %param.3) | copy-start | bytes 6291460
  14.8 9.1 %collective-permute-start.1 = (f32[128,256]{1,0:T(8,128)S(1)}, f32[128,256]{1,0:T(8,128)S(1)}, u32[]{:S(2)}, u32[]{:S(2)}) collective-permute-start(f32[128,256]{1,0:T(8,128)S(1)} %get-tuple-element.9), channel_id=1, source_target_pairs={{256,128},{0,1},{129,257},{385,386},{258,130},{2,3},{131,259},{387... | collective-permute-start | bytes 393224 | tf_op jit(solution)/shard_map/ppermute | solution.py:67
  20.8 6.0 %collective-permute-start = (f32[128,256]{1,0:T(8,128)S(1)}, f32[128,256]{1,0:T(8,128)S(1)}, u32[]{:S(2)}, u32[]{:S(2)}) collective-permute-start(f32[128,256]{1,0:T(8,128)S(1)} %get-tuple-element.10), channel_id=1, source_target_pairs={{384,256},{128,0},{1,129},{257,385},{386,258},{130,2},{3,131},{259... | collective-permute-start | bytes 393224 | tf_op jit(solution)/shard_map/ppermute | solution.py:68
  28.0 5.7 %collective-permute-start.2 = (f32[128,256]{1,0:T(8,128)S(1)}, f32[128,256]{1,0:T(8,128)S(1)}, u32[]{:S(2)}, u32[]{:S(2)}) collective-permute-start(f32[128,256]{1,0:T(8,128)S(1)} %get-tuple-element.15), channel_id=1, source_target_pairs={{384,256},{128,0},{1,129},{257,385},{386,258},{130,2},{3,131},{259... | collective-permute-start | bytes 393224 | tf_op jit(solution)/shard_map/ppermute | solution.py:68
  29.9 5.7 %collective-permute-start.3 = (f32[128,256]{1,0:T(8,128)S(1)}, f32[128,256]{1,0:T(8,128)S(1)}, u32[]{:S(2)}, u32[]{:S(2)}) collective-permute-start(f32[128,256]{1,0:T(8,128)S(1)} %get-tuple-element.16), channel_id=1, source_target_pairs={{256,128},{0,1},{129,257},{385,386},{258,130},{2,3},{131,259},{387... | collective-permute-start | bytes 393224 | tf_op jit(solution)/shard_map/ppermute | solution.py:67
  36.8 7.2 %collective-permute-start.4 = (f32[128,256]{1,0:T(8,128)S(1)}, f32[128,256]{1,0:T(8,128)S(1)}, u32[]{:S(2)}, u32[]{:S(2)}) collective-permute-start(f32[128,256]{1,0:T(8,128)S(1)} %get-tuple-element.13), channel_id=1, source_target_pairs={{384,256},{128,0},{1,129},{257,385},{386,258},{130,2},{3,131},{259... | collective-permute-start | bytes 393224 | tf_op jit(solution)/shard_map/ppermute | solution.py:68
  40.5 5.7 %collective-permute-start.5 = (f32[128,256]{1,0:T(8,128)S(1)}, f32[128,256]{1,0:T(8,128)S(1)}, u32[]{:S(2)}, u32[]{:S(2)}) collective-permute-start(f32[128,256]{1,0:T(8,128)S(1)} %get-tuple-element.14), channel_id=1, source_target_pairs={{256,128},{0,1},{129,257},{385,386},{258,130},{2,3},{131,259},{387... | collective-permute-start | bytes 393224 | tf_op jit(solution)/shard_map/ppermute | solution.py:67
  47.7 6.0 %collective-permute-start.6 = (f32[128,256]{1,0:T(8,128)S(1)}, f32[128,256]{1,0:T(8,128)S(1)}, u32[]{:S(2)}, u32[]{:S(2)}) collective-permute-start(f32[128,256]{1,0:T(8,128)S(1)} %get-tuple-element.11), channel_id=1, source_target_pairs={{384,256},{128,0},{1,129},{257,385},{386,258},{130,2},{3,131},{259... | collective-permute-start | bytes 393224 | tf_op jit(solution)/shard_map/ppermute | solution.py:68
  49.6 5.9 %collective-permute-start.7 = (f32[128,256]{1,0:T(8,128)S(1)}, f32[128,256]{1,0:T(8,128)S(1)}, u32[]{:S(2)}, u32[]{:S(2)}) collective-permute-start(f32[128,256]{1,0:T(8,128)S(1)} %get-tuple-element.12), channel_id=1, source_target_pairs={{256,128},{0,1},{129,257},{385,386},{258,130},{2,3},{131,259},{387... | collective-permute-start | bytes 393224 | tf_op jit(solution)/shard_map/ppermute | solution.py:67
  69.7 12.7 %collective-permute-start.8 = (f32[512,512]{1,0:T(8,128)S(1)}, f32[512,512]{1,0:T(8,128)S(1)}, u32[]{:S(2)}, u32[]{:S(2)}) collective-permute-start(f32[512,512]{1,0:T(8,128)S(1)} %bitcast.78), channel_id=1, source_target_pairs={{0,16},{16,0},{1,17},{17,1},{2,18},{18,2},{3,19},{19,3},{4,20},{20... | collective-permute-start | bytes 3145736 | tf_op jit(solution)/shard_map/ppermute | solution.py:204

commit v5 on v4

--- a/solution.py
+++ b/solution.py
@@ -55,26 +55,47 @@
     return terms
 
 
-def chebyshev(y, diag_blocks, coupling, is_odd):
+def edge_coupling(coupling, chunk):
+    places = snake()
+    nyl = lax.axis_size("yl")
+    crossings = [(places[i - 1], places[i]) for i in range(nyl, len(places), nyl)]
+    crossed = lax.ppermute(coupling[-1], SUM, crossings)
+    part = coupling.shape[0] // nyl
+    inside = lax.dynamic_index_in_dim(
+        coupling, jnp.maximum(chunk * part - 1, 0), axis=0, keepdims=False
+    )
+    return jnp.where(chunk == 0, crossed, inside)
+
+
+def chebyshev(y, diag_blocks, coupling, below, is_odd, is_top):
     places = snake()
     swaps = []
     for start in (1, 0):
         ups = [(places[i], places[i + 1]) for i in range(start, len(places) - 1, 2)]
         swaps.append(ups + [(above, below) for below, above in ups])
+    top = coupling[-1]
     previous = None
-    for turn in range(DEGREE):
-        last_term = dot(y[-1], coupling[-1], ((1,), (0,)))
-        odd = lax.ppermute(jnp.where(is_odd, last_term, y[0]), SUM, swaps[0])
-        even = lax.ppermute(jnp.where(is_odd, y[0], last_term), SUM, swaps[1])
+    for turn in range(0, DEGREE, 2):
         scale = (1.0 if turn == 0 else 2.0) / filter_half
-        inner = [scale * term for term in local_terms(y, diag_blocks, coupling)]
+        a = [scale * term for term in local_terms(y, diag_blocks, coupling)]
         if previous is not None:
-            inner = [term - old for term, old in zip(inner, previous)]
-        from_above = jnp.where(is_odd, odd, even)
-        from_below = jnp.where(is_odd, even, odd)
-        inner[-1] = inner[-1] + scale * dot(from_above, coupling[-1], ((1,), (1,)))
-        inner[0] = inner[0] + scale * from_below
-        previous, y = y, inner
+            a = [term - old for term, old in zip(a, previous)]
+        term_up = dot(y[-1], top, ((1,), (0,)))
+        up = jnp.concatenate([term_up, dot(a[-1], top, ((1,), (0,)))])
+        down = jnp.concatenate([y[0], a[0]])
+        odd = lax.ppermute(jnp.where(is_odd, up, down), SUM, swaps[0])
+        even = lax.ppermute(jnp.where(is_odd, down, up), SUM, swaps[1])
+        around = scale * dot(dot(y[0], below, ((1,), (1,))), below, ((1,), (0,)))
+        above_y, above_a = jnp.split(jnp.where(is_odd, odd, even), 2)
+        below_y, below_a = jnp.split(jnp.where(is_odd, even, odd), 2)
+        a[-1] = a[-1] + scale * dot(above_y, top, ((1,), (1,)))
+        a[0] = a[0] + scale * below_y
+        above_a = jnp.where(is_top, 0.0, above_a + scale * term_up)
+        below_a = below_a + around
+        b = [(2.0 / filter_half) * term - old for term, old in zip(local_terms(a, diag_blocks, coupling), y)]
+        b[-1] = b[-1] + (2.0 / filter_half) * dot(above_a, top, ((1,), (1,)))
+        b[0] = b[0] + (2.0 / filter_half) * below_a
+        previous, y = a, b
     return y
 
 
@@ -194,7 +215,9 @@
             [own[:, n * size : (n + 1) * size] for n in range(part)],
             lax.dynamic_slice_in_dim(diag_blocks, chunk * part, part),
             lax.dynamic_slice_in_dim(coupling, chunk * part, part),
+            edge_coupling(coupling, chunk),
             chunk % 2 == 1,
+            (lax.axis_index(ROW) == lax.axis_size(ROW) - 1) & (chunk == nyl - 1),
         ),
         axis=1,
     )

time: 161 us -> 148 us (0.919)
  starting transfers between devices: 39.9 us -> 31.4 us
  blocking collectives: 85.3 us -> 81.6 us
  waiting for transfers between devices: 17.8 us -> 14.2 us
    all_to_all x2, blocking collectives: 63.1 us -> 59 us  [exchange(): lax.all_to_all(a, SUM, split_axis=0, concat_axis=0, tiled=True)]
    ppermute x8 -> x5, starting transfers between devices: 24.1 us -> 20.2 us  [the longest x2 10.3 us: chebyshev(): odd = lax.ppermute(jnp.where(is_odd, up, down), SUM, swaps[0])]
    ppermute x1, starting transfers between devices: 10.4 us -> 7.87 us  [local(): far = lax.ppermute(near, 'c', [(0, 1), (1, 0)])]
    ppermute x8 -> x5, waiting for transfers between devices: 9.91 us -> 7.39 us  [the longest x2 6.85 us: chebyshev(): odd = lax.ppermute(jnp.where(is_odd, up, down), SUM, swaps[0])]
    all_to_all x1, starting transfers between devices: 5.41 us -> 3.41 us  [local(): own = lax.all_to_all(chunks, 'yl', split_axis=0, concat_axis=0, tiled=True)]
    dot_general x24 -> x28, matrix products: 8.97 us -> 10 us  [dot(): return lax.dot_general(a, b, (contract, batch), precision=precision)]
  transfers between devices with their start and end apart: 10 -> 7, of which waited for: 7 -> 5; matrix products, arithmetic and copies ran while one was open for 2% -> 2% of each run, Pallas kernels for 0% -> 0%
where the time goes in v5:
time: 148 us; the launch traced here: 145 us
  blocking collectives  81.6 us (55%)
  starting transfers between devices  31.4 us (21%)
  waiting for transfers between devices  14.2 us (10%)
  matrix products  10 us (7%)
  local copies, waits for them, and re-layouts  2.94 us (2%)
  Pallas kernels  2.48 us (2%)
  other arithmetic  1.91 us (1%)
    all_to_all x2, blocking collectives, exchange(): lax.all_to_all(a, SUM, split_axis=0, concat_axis=0, tiled=True)  59 us
    all_to_all x1, blocking collectives, local(): near = lax.all_to_all(copies, 'x', split_axis=0, concat_axis=0, tiled=True)  13.9 us
    ppermute x2, starting transfers between devices, chebyshev(): odd = lax.ppermute(jnp.where(is_odd, up, down), SUM, swaps[0])  10.3 us
    dot_general x28, matrix products, dot(): return lax.dot_general(a, b, (contract, batch), precision=precision)  10 us
    all_to_all x1, blocking collectives, local(): back = lax.all_to_all(back, 'yl', split_axis=0, concat_axis=0, tiled=True)  8.81 us
    ppermute x1, starting transfers between devices, local(): far = lax.ppermute(near, 'c', [(0, 1), (1, 0)])  7.87 us
    ppermute x2, waiting for transfers between devices, chebyshev(): odd = lax.ppermute(jnp.where(is_odd, up, down), SUM, swaps[0])  6.85 us
    ppermute x2, starting transfers between devices, chebyshev(): even = lax.ppermute(jnp.where(is_odd, down, up), SUM, swaps[1])  5.02 us
  transfers between devices with their start and end apart: 7, of which 5 were waited for; matrix products, arithmetic and copies ran while one was open for 2% of the time, Pallas kernels for 0%

profile of v5, /device:TPU:1, one launch (start us, length us, event | category | flops | bytes accessed | tf_op | source)
XLA Modules:
  0.0 145.1 jit_solution(16261836948950402777)
XLA Ops:
  0.0 0.0 copy-start
  0.0 1.1 slice_bitcast_fusion
  1.1 4.8 %collective-permute-start.2 = (f32[256,256]{1,0:T(8,128)S(1)}, f32[256,256]{1,0:T(8,128)S(1)}, u32[]{:S(2)}, u32[]{:S(2)}) collective-permute-start(f32[256,256]{1,0:T(8,128)S(1)} %slice_bitcast_fusion), channel_id=1, source_target_pairs={{0,1},{385,386},{2,3},{387,388},{4,5},{389,390},{6,7},{391,8},{392... | collective-permute-start | bytes 786440 | tf_op jit(solution)/shard_map/ppermute | solution.py:62
  6.0 1.0 copy.13
  7.0 0.7 reverse_select_fusion.1
  7.7 3.4 %all-to-all-start = ((f32[4,32,512]{2,1,0:T(8,128)}), f32[4,32,512]{2,1,0:T(8,128)S(1)}, u32[]{:S(2)}, u32[]{:S(2)}) async-start(f32[4,32,512]{2,1,0:T(8,128)} %reverse_select_fusion.1), calls=%async_computation | async-start | bytes 524288 | tf_op jit(solution)/shard_map/all_to_all | solution.py:211
  11.1 0.0 collective-permute-done.2
  11.1 1.0 bitcast_select_fusion
  12.1 4.6 %all-to-all-done = f32[4,32,512]{2,1,0:T(8,128)S(1)} async-done(((f32[4,32,512]{2,1,0:T(8,128)}), f32[4,32,512]{2,1,0:T(8,128)S(1)}, u32[]{:S(2)}, u32[]{:S(2)}) %all-to-all-start) | async-done | bytes 262176 | tf_op jit(solution)/shard_map/all_to_all | solution.py:211
  16.7 0.0 copy-start.1
  16.7 1.3 fusion.27
  18.0 0.0 copy-done
  18.0 0.3 convolution_subtract_fusion.6
  18.3 0.3 convolution_subtract_fusion.5
  18.7 1.3 convolution_add_fusion.7
  19.9 0.0 copy-done.1
  20.0 0.2 convolution_add_fusion.6
  20.2 0.2 fusion.26
  20.5 3.1 %collective-permute-start = (f32[256,256]{1,0:T(8,128)S(1)}, f32[256,256]{1,0:T(8,128)S(1)}, u32[]{:S(2)}, u32[]{:S(2)}) collective-permute-start(f32[256,256]{1,0:T(8,128)S(1)} %get-tuple-element.15), channel_id=1, source_target_pairs={{384,256},{128,0},{1,129},{257,385},{386,258},{130,2},{3,131},{259... | collective-permute-start | bytes 786440 | tf_op jit(solution)/shard_map/ppermute | solution.py:87
  23.6 6.0 %collective-permute-start.1 = (f32[256,256]{1,0:T(8,128)S(1)}, f32[256,256]{1,0:T(8,128)S(1)}, u32[]{:S(2)}, u32[]{:S(2)}) collective-permute-start(f32[256,256]{1,0:T(8,128)S(1)} %get-tuple-element.16), channel_id=1, source_target_pairs={{256,128},{0,1},{129,257},{385,386},{258,130},{2,3},{131,259},{387... | collective-permute-start | bytes 786440 | tf_op jit(solution)/shard_map/ppermute | solution.py:86
  29.6 0.3 fusion.78
  29.9 0.2 fusion.82
  30.1 0.0 collective-permute-done
  30.2 3.7 %collective-permute-done.1 = f32[256,256]{1,0:T(8,128)S(1)} collective-permute-done((f32[256,256]{1,0:T(8,128)S(1)}, f32[256,256]{1,0:T(8,128)S(1)}, u32[]{:S(2)}, u32[]{:S(2)}) %collective-permute-start.1) | collective-permute-done | bytes 262176 | tf_op jit(solution)/shard_map/ppermute | solution.py:86
  33.9 0.3 convolution_add_fusion.5
  34.2 0.3 fusion.22
  34.5 0.3 fusion.12
  34.7 0.3 fusion.10
  35.1 0.2 fusion.25
  35.3 0.3 convolution_subtract_fusion.2
  35.6 0.3 fusion.23
  35.9 0.3 fusion.16
  36.3 0.3 convolution_subtract_fusion.3
  36.6 0.2 fusion.7
  36.8 0.2 fusion.24
  37.1 0.3 fusion.9
  37.5 1.9 %collective-permute-start.3 = (f32[256,256]{1,0:T(8,128)S(1)}, f32[256,256]{1,0:T(8,128)S(1)}, u32[]{:S(2)}, u32[]{:S(2)}) collective-permute-start(f32[256,256]{1,0:T(8,128)S(1)} %get-tuple-element.11), channel_id=1, source_target_pairs={{384,256},{128,0},{1,129},{257,385},{386,258},{130,2},{3,131},{259... | collective-permute-start | bytes 786440 | tf_op jit(solution)/shard_map/ppermute | solution.py:87
  39.4 4.3 %collective-permute-start.4 = (f32[256,256]{1,0:T(8,128)S(1)}, f32[256,256]{1,0:T(8,128)S(1)}, u32[]{:S(2)}, u32[]{:S(2)}) collective-permute-start(f32[256,256]{1,0:T(8,128)S(1)} %get-tuple-element.12), channel_id=1, source_target_pairs={{256,128},{0,1},{129,257},{385,386},{258,130},{2,3},{131,259},{387... | collective-permute-start | bytes 786440 | tf_op jit(solution)/shard_map/ppermute | solution.py:86
  43.7 0.3 fusion.83
  44.0 0.5 collective-permute-done.3
  44.6 3.2 %collective-permute-done.4 = f32[256,256]{1,0:T(8,128)S(1)} collective-permute-done((f32[256,256]{1,0:T(8,128)S(1)}, f32[256,256]{1,0:T(8,128)S(1)}, u32[]{:S(2)}, u32[]{:S(2)}) %collective-permute-start.4) | collective-permute-done | bytes 262176 | tf_op jit(solution)/shard_map/ppermute | solution.py:86
  47.8 0.3 fusion.5
  48.1 0.3 convolution_subtract_fusion
  48.5 0.3 convolution_subtract_fusion.1
  48.8 0.2 fusion.2
  49.0 0.3 fusion
  49.3 0.3 fusion.4
  49.7 0.2 fusion.31
  49.9 0.1 broadcast_in_dim.12
  50.1 13.9 %all_to_all.33 = f32[4,128,512]{2,1,0:T(8,128)S(1)} all-to-all(f32[4,128,512]{2,1,0:T(8,128)S(1)} %broadcast_in_dim.12), channel_id=1, replica_groups=mesh['yl'=4,'x'=4,'c'=2,'yh'=2,'z'=8] {'x'}, dimensions={0} | all-to-all | bytes 2097152 | tf_op jit(solution)/shard_map/all_to_all | solution.py:225
  63.9 7.9 %collective-permute-start.5 = (f32[512,512]{1,0:T(8,128)S(1)}, f32[512,512]{1,0:T(8,128)S(1)}, u32[]{:S(2)}, u32[]{:S(2)}) collective-permute-start(f32[512,512]{1,0:T(8,128)S(1)} %bitcast.73), channel_id=1, source_target_pairs={{0,16},{16,0},{1,17},{17,1},{2,18},{18,2},{3,19},{19,3},{4,20},{20... | collective-permute-start | bytes 3145736 | tf_op jit(solution)/shard_map/ppermute | solution.py:227
  71.8 2.3 %collective-permute-done.5.far_ref = f32[512,512]{1,0:T(8,128)S(1)} collective-permute-done((f32[512,512]{1,0:T(8,128)S(1)}, f32[512,512]{1,0:T(8,128)S(1)}, u32[]{:S(2)}, u32[]{:S(2)}) %collective-permute-start.5) | collective-permute-done | bytes 1048608 | tf_op jit(solution)/shard_map/ppermute | solution.py:227
  74.1 1.7 %shard_map.37 = f32[1088,128]{1,0:T(8,128)S(1)} custom-call(f32[128,512]{1,0:T(8,128)S(1)} %pad_maximum_fusion.4.own_ref, f32[512,512]{1,0:T(8,128)S(1)} %bitcast.74, f32[512,512]{1,0:T(8,128)S(1)} %collective-permute-done.5.far_ref), custom_call_target="tpu_custom_call" | custom-call | tf_op jit(solution)/shard_map/pallas_call | solution.py:189
  75.8 34.2 %all_to_all.34 = f32[64,1,2176]{2,1,0:T(1,128)S(1)} all-to-all(f32[64,1,2176]{2,1,0:T(1,128)S(1)} %bitcast.79), channel_id=1, replica_groups=mesh['yl'=4,'x'=4,'c'=2,'yh'=2,'z'=8] {'yl','yh','z'}, dimensions={0} | all-to-all | bytes 1114112 | tf_op jit(solution)/shard_map/all_to_all | solution.py:233
  109.9 0.1 shard_map.38
  110.0 24.8 %all_to_all.35 = f32[64,1,2176]{2,1,0:T(1,128)S(1)} all-to-all(f32[64,1,2176]{2,1,0:T(1,128)S(1)} %bitcast.78), channel_id=1, replica_groups=mesh['yl'=4,'x'=4,'c'=2,'yh'=2,'z'=8] {'yl','yh','z'}, dimensions={0} | all-to-all | bytes 1114112 | tf_op jit(solution)/shard_map/all_to_all | solution.py:233
  134.8 0.7 shard_map.39
  135.5 8.8 %all_to_all.36 = f32[4,32,512]{2,1,0:T(8,128)S(1)} all-to-all(f32[4,32,512]{2,1,0:T(8,128)S(1)} %bitcast.80), channel_id=1, replica_groups=mesh['yl'=4,'x'=4,'c'=2,'yh'=2,'z'=8] {'yl'}, dimensions={0} | all-to-all | bytes 524288 | tf_op jit(solution)/shard_map/all_to_all | solution.py:241
  144.4 0.7 copy.11
  (7 shorter events, 0.2 us)
Async XLA Ops:
  0.0 18.0 %copy-start = (f32[8,256,256]{2,1,0:T(8,128)S(1)}, f32[8,256,256]{2,1,0:T(8,128)}, u32[]{:S(2)}) copy-start(f32[8,256,256]{2,1,0:T(8,128)} %param.3) | copy-start | bytes 6291460
  1.1 10.0 %collective-permute-start.2 = (f32[256,256]{1,0:T(8,128)S(1)}, f32[256,256]{1,0:T(8,128)S(1)}, u32[]{:S(2)}, u32[]{:S(2)}) collective-permute-start(f32[256,256]{1,0:T(8,128)S(1)} %slice_bitcast_fusion), channel_id=1, source_target_pairs={{0,1},{385,386},{2,3},{387,388},{4,5},{389,390},{6,7},{391,8},{392... | collective-permute-start | bytes 786440 | tf_op jit(solution)/shard_map/ppermute | solution.py:62
  7.7 9.0 %all-to-all-start = ((f32[4,32,512]{2,1,0:T(8,128)}), f32[4,32,512]{2,1,0:T(8,128)S(1)}, u32[]{:S(2)}, u32[]{:S(2)}) async-start(f32[4,32,512]{2,1,0:T(8,128)} %reverse_select_fusion.1), calls=%async_computation | async-start | bytes 524288 | tf_op jit(solution)/shard_map/all_to_all | solution.py:211
  16.7 3.3 %copy-start.1 = (f32[8,256,256]{2,1,0:T(8,128)S(1)}, f32[8,256,256]{2,1,0:T(8,128)}, u32[]{:S(2)}) copy-start(f32[8,256,256]{2,1,0:T(8,128)} %param.4) | copy-start | bytes 6291460
  20.5 9.6 %collective-permute-start = (f32[256,256]{1,0:T(8,128)S(1)}, f32[256,256]{1,0:T(8,128)S(1)}, u32[]{:S(2)}, u32[]{:S(2)}) collective-permute-start(f32[256,256]{1,0:T(8,128)S(1)} %get-tuple-element.15), channel_id=1, source_target_pairs={{384,256},{128,0},{1,129},{257,385},{386,258},{130,2},{3,131},{259... | collective-permute-start | bytes 786440 | tf_op jit(solution)/shard_map/ppermute | solution.py:87
  23.6 10.2 %collective-permute-start.1 = (f32[256,256]{1,0:T(8,128)S(1)}, f32[256,256]{1,0:T(8,128)S(1)}, u32[]{:S(2)}, u32[]{:S(2)}) collective-permute-start(f32[256,256]{1,0:T(8,128)S(1)} %get-tuple-element.16), channel_id=1, source_target_pairs={{256,128},{0,1},{129,257},{385,386},{258,130},{2,3},{131,259},{387... | collective-permute-start | bytes 786440 | tf_op jit(solution)/shard_map/ppermute | solution.py:86
  37.5 7.1 %collective-permute-start.3 = (f32[256,256]{1,0:T(8,128)S(1)}, f32[256,256]{1,0:T(8,128)S(1)}, u32[]{:S(2)}, u32[]{:S(2)}) collective-permute-start(f32[256,256]{1,0:T(8,128)S(1)} %get-tuple-element.11), channel_id=1, source_target_pairs={{384,256},{128,0},{1,129},{257,385},{386,258},{130,2},{3,131},{259... | collective-permute-start | bytes 786440 | tf_op jit(solution)/shard_map/ppermute | solution.py:87
  39.4 8.4 %collective-permute-start.4 = (f32[256,256]{1,0:T(8,128)S(1)}, f32[256,256]{1,0:T(8,128)S(1)}, u32[]{:S(2)}, u32[]{:S(2)}) collective-permute-start(f32[256,256]{1,0:T(8,128)S(1)} %get-tuple-element.12), channel_id=1, source_target_pairs={{256,128},{0,1},{129,257},{385,386},{258,130},{2,3},{131,259},{387... | collective-permute-start | bytes 786440 | tf_op jit(solution)/shard_map/ppermute | solution.py:86
  63.9 10.1 %collective-permute-start.5 = (f32[512,512]{1,0:T(8,128)S(1)}, f32[512,512]{1,0:T(8,128)S(1)}, u32[]{:S(2)}, u32[]{:S(2)}) collective-permute-start(f32[512,512]{1,0:T(8,128)S(1)} %bitcast.73), channel_id=1, source_target_pairs={{0,16},{16,0},{1,17},{17,1},{2,18},{18,2},{3,19},{19,3},{4,20},{20... | collective-permute-start | bytes 3145736 | tf_op jit(solution)/shard_map/ppermute | solution.py:227

commit v6 on v4

--- a/solution.py
+++ b/solution.py
@@ -43,51 +43,197 @@
     return places
 
 
-def local_terms(y, diag_blocks, coupling):
+def edge_coupling(coupling, chunk):
+    places = snake()
+    nyl = lax.axis_size("yl")
+    crossings = [(places[i - 1], places[i]) for i in range(nyl, len(places), nyl)]
+    crossed = lax.ppermute(coupling[-1], SUM, crossings)
+    part = coupling.shape[0] // nyl
+    inside = lax.dynamic_index_in_dim(
+        coupling, jnp.maximum(chunk * part - 1, 0), axis=0, keepdims=False
+    )
+    return jnp.where(chunk == 0, crossed, inside)
+
+
+def split(a):
+    high = a.astype(jnp.bfloat16)
+    return high, (a - high.astype(jnp.float32)).astype(jnp.bfloat16)
+
+
+def product(a, b, contract):
+    def one(x, y):
+        return lax.dot_general(x, y, (contract, ((), ())), preferred_element_type=jnp.float32)
+
+    return one(a[0], b[0]) + (one(a[0], b[1]) + one(a[1], b[0]))
+
+
+def blocks_of(ref, size):
+    return [ref[:, n : n + size] for n in range(0, ref.shape[1], size)]
+
+
+def local_terms(y, parts, diagonal, coupling):
     terms = []
     for n, block in enumerate(y):
-        term = dot(block, diag_blocks[n], ((1,), (1,))) - filter_center * block
+        term = product(parts[n], diagonal(n), ((1,), (1,))) - filter_center * block
         if n + 1 < len(y):
-            term = term + dot(y[n + 1], coupling[n], ((1,), (1,)))
+            term = term + product(parts[n + 1], coupling(n), ((1,), (1,)))
         if n > 0:
-            term = term + dot(y[n - 1], coupling[n - 1], ((1,), (0,)))
+            term = term + product(parts[n - 1], coupling(n - 1), ((1,), (0,)))
         terms.append(term)
     return terms
 
 
-def chebyshev(y, diag_blocks, coupling, is_odd):
+def send(is_odd, y, parts, a, top, odd_ref, even_ref, term_ref):
+    rows = y[0].shape[0]
+    term_up = product(parts[-1], top, ((1,), (0,)))
+    term_ref[...] = term_up
+    up = (term_up, product(split(a[-1]), top, ((1,), (0,))))
+    down = (y[0], a[0])
+    for holds, up_ref, down_ref in (
+        (is_odd, odd_ref, even_ref),
+        (jnp.logical_not(is_odd), even_ref, odd_ref),
+    ):
+
+        @pl.when(holds)
+        def _(up_ref=up_ref, down_ref=down_ref):
+            for ref, pair in ((up_ref, up), (down_ref, down)):
+                ref[:rows, :] = pair[0]
+                ref[rows:, :] = pair[1]
+
+
+def start_kernel(flags, y_ref, d_ref, c_ref, dh, dl, ch, cl, a_ref, odd_ref, even_ref, term_ref):
+    for ref, high, low in ((d_ref, dh, dl), (c_ref, ch, cl)):
+        for n in range(ref.shape[0]):
+            high[n], low[n] = split(ref[n])
+    size = d_ref.shape[1]
+    y = blocks_of(y_ref, size)
+    parts = [split(block) for block in y]
+    coupling = lambda n: (ch[n], cl[n])
+    a = local_terms(y, parts, lambda n: (dh[n], dl[n]), coupling)
+    a = [term / filter_half for term in a]
+    a_ref[...] = jnp.concatenate(a, axis=1)
+    send(flags[0] == 1, y, parts, a, coupling(len(y) - 1), odd_ref, even_ref, term_ref)
+
+
+def step_kernel(
+    scale,
+    flags,
+    y_ref,
+    a_ref,
+    got_odd,
+    got_even,
+    around_ref,
+    got_term,
+    dh,
+    dl,
+    ch,
+    cl,
+    b_ref,
+    next_ref=None,
+    odd_ref=None,
+    even_ref=None,
+    term_ref=None,
+):
+    size = dh.shape[1]
+    double = 2.0 / filter_half
+    is_odd = flags[0] == 1
+    diagonal, coupling = lambda n: (dh[n], dl[n]), lambda n: (ch[n], cl[n])
+    y, a = blocks_of(y_ref, size), blocks_of(a_ref, size)
+    top = coupling(len(y) - 1)
+    rows = y[0].shape[0]
+
+    def above(rows_of):
+        return jnp.where(is_odd, got_odd[rows_of, :], got_even[rows_of, :])
+
+    def below(rows_of):
+        return jnp.where(is_odd, got_even[rows_of, :], got_odd[rows_of, :])
+
+    edge, part = slice(0, rows), slice(rows, 2 * rows)
+    a[-1] = a[-1] + scale * product(split(above(edge)), top, ((1,), (1,)))
+    a[0] = a[0] + scale * below(edge)
+    above_a = jnp.where(flags[1] == 1, 0.0, above(part) + scale * got_term[...])
+    below_a = below(part) + around_ref[...]
+    terms = local_terms(a, [split(block) for block in a], diagonal, coupling)
+    b = [double * term - old for term, old in zip(terms, y)]
+    b[-1] = b[-1] + double * product(split(above_a), top, ((1,), (1,)))
+    b[0] = b[0] + double * below_a
+    b_ref[...] = jnp.concatenate(b, axis=1)
+    if next_ref is not None:
+        parts = [split(block) for block in b]
+        terms = local_terms(b, parts, diagonal, coupling)
+        a = [double * term - old for term, old in zip(terms, a)]
+        next_ref[...] = jnp.concatenate(a, axis=1)
+        send(is_odd, b, parts, a, top, odd_ref, even_ref, term_ref)
+
+
+def chebyshev(y, diag_blocks, coupling, below, flags):
     places = snake()
     swaps = []
     for start in (1, 0):
         ups = [(places[i], places[i + 1]) for i in range(start, len(places) - 1, 2)]
         swaps.append(ups + [(above, below) for below, above in ups])
-    previous = None
-    for turn in range(DEGREE):
-        last_term = dot(y[-1], coupling[-1], ((1,), (0,)))
-        odd = lax.ppermute(jnp.where(is_odd, last_term, y[0]), SUM, swaps[0])
-        even = lax.ppermute(jnp.where(is_odd, y[0], last_term), SUM, swaps[1])
+    rows, size = y.shape[0], diag_blocks.shape[1]
+    message = jax.ShapeDtypeStruct((2 * rows, size), jnp.float32)
+    panel = jax.ShapeDtypeStruct(y.shape, jnp.float32)
+    sends = [panel, message, message, jax.ShapeDtypeStruct((rows, size), jnp.float32)]
+    halves = [jax.ShapeDtypeStruct(diag_blocks.shape, jnp.bfloat16)] * 4
+    *hamiltonian, a, odd, even, term = call(
+        start_kernel, halves + sends, (flags,), y, diag_blocks, coupling
+    )
+    for turn in range(0, DEGREE, 2):
         scale = (1.0 if turn == 0 else 2.0) / filter_half
-        inner = [scale * term for term in local_terms(y, diag_blocks, coupling)]
-        if previous is not None:
-            inner = [term - old for term, old in zip(inner, previous)]
-        from_above = jnp.where(is_odd, odd, even)
-        from_below = jnp.where(is_odd, even, odd)
-        inner[-1] = inner[-1] + scale * dot(from_above, coupling[-1], ((1,), (1,)))
-        inner[0] = inner[0] + scale * from_below
-        previous, y = y, inner
+        odd = lax.ppermute(odd, SUM, swaps[0])
+        even = lax.ppermute(even, SUM, swaps[1])
+        around = scale * dot(
+            dot(y[:, :size], below, ((1,), (1,))), below, ((1,), (0,))
+        )
+        final = turn + 2 >= DEGREE
+        result = call(
+            functools.partial(step_kernel, scale),
+            [panel] if final else [panel] + sends,
+            (flags,),
+            y,
+            a,
+            odd,
+            even,
+            around,
+            term,
+            *hamiltonian,
+        )
+        y = result[0]
+        if not final:
+            a, odd, even, term = result[1:]
     return y
 
 
-def split(a):
-    high = a.astype(jnp.bfloat16)
-    return high, (a - high.astype(jnp.float32)).astype(jnp.bfloat16)
-
-
-def product(a, b, contract):
-    def one(x, y):
-        return lax.dot_general(x, y, (contract, ((), ())), preferred_element_type=jnp.float32)
-
-    return one(a[0], b[0]) + (one(a[0], b[1]) + one(a[1], b[0]))
+def spread_kernel(flip, in_ref, out_ref, sems):
+    count, _, depth = out_ref.shape
+    copies = []
+    for j in range(count):
+        at = jnp.where(flip[0] == 1, count - 1 - j, j) * depth
+        source = in_ref.at[:, pl.ds(pl.multiple_of(at, depth), depth)]
+        copies.append(pltpu.make_async_copy(source, out_ref.at[j], sems.at[j]))
+    for copy in copies:
+        copy.start()
+    for copy in copies:
+        copy.wait()
+
+
+def spread(flip, vectors, count):
+    rows, width = vectors.shape
+    return pl.pallas_call(
+        spread_kernel,
+        out_shape=jax.ShapeDtypeStruct((count, rows, width // count), jnp.float32),
+        in_specs=[
+            pl.BlockSpec(memory_space=pltpu.SMEM),
+            pl.BlockSpec(memory_space=pl.ANY),
+        ],
+        out_specs=pl.BlockSpec(memory_space=pltpu.VMEM),
+        scratch_shapes=[pltpu.SemaphoreType.DMA((count,))],
+        name="spread",
+        compiler_params=pltpu.CompilerParams(vmem_limit_bytes=24 * 2**20),
+        interpret=INTERPRET,
+    )(flip, vectors)
 
 
 def gram_kernel(own_ref, near_ref, far_ref, out_ref):
@@ -162,14 +308,14 @@
     out_ref[...] = result
 
 
-def call(kernel, out_shape, scalars, *arrays):
+def call(kernel, out_shapes, scalars, *arrays):
     vmem = pl.BlockSpec(memory_space=pltpu.VMEM)
     smem = pl.BlockSpec(memory_space=pltpu.SMEM)
     return pl.pallas_call(
         kernel,
-        out_shape=jax.ShapeDtypeStruct(out_shape, jnp.float32),
+        out_shape=out_shapes,
         in_specs=[smem] * len(scalars) + [vmem] * len(arrays),
-        out_specs=vmem,
+        out_specs=[vmem] * len(out_shapes),
         compiler_params=pltpu.CompilerParams(vmem_limit_bytes=24 * 2**20),
         interpret=INTERPRET,
     )(*scalars, *arrays)
@@ -177,7 +323,7 @@
 
 def local(diag_blocks, coupling, vectors):
     count, width = vectors.shape
-    blocks, size = diag_blocks.shape[0], diag_blocks.shape[1]
+    blocks = diag_blocks.shape[0]
     nyl, nx, _ = (lax.axis_size(a) for a in VEC)
     total_rows = width * lax.axis_size(ROW)
     at, vectors = lax.optimization_barrier((lax.axis_index("x").reshape(1), vectors))
@@ -185,18 +331,18 @@
     yl = lax.axis_index("yl")
     chunk = jnp.where(flip, nyl - 1 - yl, yl)
     part, group, depth = blocks // nyl, nyl * count, width // nyl
-    chunks = vectors.reshape(count, nyl, depth).transpose(1, 0, 2)
-    chunks = jnp.where(flip, chunks[::-1], chunks)
+    chunks = spread(flip.astype(jnp.int32).reshape(1), vectors, nyl)
     own = lax.all_to_all(chunks, "yl", split_axis=0, concat_axis=0, tiled=True)
     own = own.reshape(group, depth)
-    own = jnp.concatenate(
-        chebyshev(
-            [own[:, n * size : (n + 1) * size] for n in range(part)],
-            lax.dynamic_slice_in_dim(diag_blocks, chunk * part, part),
-            lax.dynamic_slice_in_dim(coupling, chunk * part, part),
-            chunk % 2 == 1,
-        ),
-        axis=1,
+    is_top = (lax.axis_index(ROW) == lax.axis_size(ROW) - 1) & (chunk == nyl - 1)
+    own_diag = lax.dynamic_slice_in_dim(diag_blocks, chunk * part, part)
+    own_coupling = lax.dynamic_slice_in_dim(coupling, chunk * part, part)
+    own = chebyshev(
+        own,
+        own_diag,
+        own_coupling,
+        edge_coupling(coupling, chunk),
+        jnp.stack([chunk % 2, is_top.astype(jnp.int32)]),
     )
     copies = jnp.broadcast_to(own[None], (nx, group, depth))
     near = lax.all_to_all(copies, "x", split_axis=0, concat_axis=0, tiled=True)
@@ -204,16 +350,23 @@
     far = lax.ppermute(near, "c", [(0, 1), (1, 0)])
     members = group // TILE * nx
     packed = (members * (2 * TILE + 1), LANES)
+    packed_type = jax.ShapeDtypeStruct(packed, jnp.float32)
 
     def exchange(a):
         a = a.reshape(lax.axis_size(SUM), -1)
         return lax.all_to_all(a, SUM, split_axis=0, concat_axis=0, tiled=True).reshape(packed)
 
-    pieces = exchange(call(gram_kernel, packed, (), own, near, far))
-    summed = exchange(call(sum_kernel, packed, (), pieces))
+    pieces = exchange(call(gram_kernel, [packed_type], (), own, near, far)[0])
+    summed = exchange(call(sum_kernel, [packed_type], (), pieces)[0])
     renewed = call(
-        functools.partial(mixing_kernel, total_rows), (group, depth), (at,), summed, own, near, far
-    )
+        functools.partial(mixing_kernel, total_rows),
+        [jax.ShapeDtypeStruct((group, depth), jnp.float32)],
+        (at,),
+        summed,
+        own,
+        near,
+        far,
+    )[0]
     back = renewed.reshape(nyl, count, depth)
     back = lax.all_to_all(back, "yl", split_axis=0, concat_axis=0, tiled=True)
     back = jnp.where(flip, back[::-1], back)

time: 161 us -> 145 us (0.901)
  the two profiles are of different devices: /device:TPU:1 before, /device:TPU:8 now
where the time goes in v6:
time: 145 us; the launch traced here: 144 us
  blocking collectives  90.3 us (62%)
  starting transfers between devices  27.8 us (19%)
  waiting for transfers between devices  8.52 us (6%)
  Pallas kernels  8.16 us (6%)
  local copies, waits for them, and re-layouts  4.74 us (3%)
  matrix products  2.96 us (2%)
  other arithmetic  1.8 us (1%)
    all_to_all x2, blocking collectives, exchange(): lax.all_to_all(a, SUM, split_axis=0, concat_axis=0, tiled=True)  63.6 us
    all_to_all x1, blocking collectives, local(): near = lax.all_to_all(copies, 'x', split_axis=0, concat_axis=0, tiled=True)  16.9 us
    ppermute x2, starting transfers between devices, chebyshev(): even = lax.ppermute(even, SUM, swaps[1])  10.3 us
    all_to_all x1, blocking collectives, local(): back = lax.all_to_all(back, 'yl', split_axis=0, concat_axis=0, tiled=True)  9.76 us
    all_to_all x1, starting transfers between devices, local(): own = lax.all_to_all(chunks, 'yl', split_axis=0, concat_axis=0, tiled=True)  9.18 us
    pallas_call x6, Pallas kernels, call(): pl.pallas_call(kernel, out_shape=out_shapes, in_specs=[smem] * len(scalar...  7.33 us
    ppermute x2, starting transfers between devices, chebyshev(): odd = lax.ppermute(odd, SUM, swaps[0])  5.05 us
    ppermute x2, waiting for transfers between devices, chebyshev(): even = lax.ppermute(even, SUM, swaps[1])  3.81 us
  transfers between devices with their start and end apart: 7, of which 5 were waited for; matrix products, arithmetic and copies ran while one was open for 5% of the time, Pallas kernels for 0%

profile of v6, /device:TPU:8, one launch (start us, length us, event | category | flops | bytes accessed | tf_op | source)
XLA Modules:
  0.0 144.5 jit_solution(530288473471151557)
XLA Ops:
  0.0 0.0 copy-start
  0.0 0.0 copy-start.1
  0.0 1.1 copy-done.1
  1.1 0.8 spread.1
  1.9 9.2 %all-to-all-start = ((f32[4,32,512]{2,1,0:T(8,128)}), f32[4,32,512]{2,1,0:T(8,128)S(1)}, u32[]{:S(2)}, u32[]{:S(2)}) async-start(f32[4,32,512]{2,1,0:T(8,128)} %spread.1), calls=%async_computation | async-start | bytes 524288 | tf_op jit(solution)/shard_map/all_to_all | solution.py:335
  11.1 1.7 %slice_bitcast_fusion = f32[256,256]{1,0:T(8,128)} fusion(f32[8,256,256]{2,1,0:T(8,128)} %param.4), kind=kLoop, calls=%fused_computation.4 | loop fusion | bytes 524288 | tf_op jit(solution)/shard_map/squeeze | solution.py:50
  12.8 1.4 collective-permute-start.2
  14.2 1.1 constant_dynamic-slice_fusion.c_ref
  15.3 0.1 pad_add_fusion.flags
  15.3 0.0 copy-done
  15.4 0.0 collective-permute-done.2
  15.4 1.7 %bitcast_select_fusion = f32[256,256]{1,0:T(8,128)} fusion(f32[256,256]{1,0:T(8,128)} %collective-permute-done.2, f32[8,256,256]{2,1,0:T(8,128)} %param.4, s32[]{:T(128)S(6)} %max.3, pred[]{:T(512)S(6)} %eq.18), kind=kLoop, calls=%fused_computation.3 | loop fusion | flops 65536 | bytes 786437 | tf_op jit(solution)/shard_map/jit(_where)/select_n | solution.py:55
  17.1 0.2 all-to-all-done
  17.3 0.0 copy-start.2
  17.3 1.4 shard_map.37
  18.7 3.1 %collective-permute-start = (f32[256,256]{1,0:T(8,128)S(1)}, f32[256,256]{1,0:T(8,128)S(1)}, u32[]{:S(2)}, u32[]{:S(2)}) collective-permute-start(f32[256,256]{1,0:T(8,128)S(1)} %get-tuple-element.23), channel_id=1, source_target_pairs={{256,128},{0,1},{129,257},{385,386},{258,130},{2,3},{131,259},{387... | collective-permute-start | bytes 786440 | tf_op jit(solution)/shard_map/ppermute | solution.py:185
  21.8 6.4 %collective-permute-start.1 = (f32[256,256]{1,0:T(8,128)S(1)}, f32[256,256]{1,0:T(8,128)S(1)}, u32[]{:S(2)}, u32[]{:S(2)}) collective-permute-start(f32[256,256]{1,0:T(8,128)S(1)} %get-tuple-element.24), channel_id=1, source_target_pairs={{384,256},{128,0},{1,129},{257,385},{386,258},{130,2},{3,131},{259... | collective-permute-start | bytes 786440 | tf_op jit(solution)/shard_map/ppermute | solution.py:186
  28.3 1.2 fusion.1
  29.5 1.2 fusion.5.around_ref
  30.7 0.0 collective-permute-done.got_odd
  30.7 1.9 %collective-permute-done.1.got_even = f32[256,256]{1,0:T(8,128)S(1)} collective-permute-done((f32[256,256]{1,0:T(8,128)S(1)}, f32[256,256]{1,0:T(8,128)S(1)}, u32[]{:S(2)}, u32[]{:S(2)}) %collective-permute-start.1) | collective-permute-done | bytes 262176 | tf_op jit(solution)/shard_map/ppermute | solution.py:186
  32.6 2.1 %shard_map.38 = (f32[128,512]{1,0:T(8,128)S(1)}, f32[128,512]{1,0:T(8,128)S(1)}, f32[256,256]{1,0:T(8,128)S(1)}, f32[256,256]{1,0:T(8,128)S(1)}, f32[128,256]{1,0:T(8,128)S(1)}) custom-call(s32[2]{0:T(128)S(1)} %pad_add_fusion.flags, f32[128,512]{1,0:T(8,128)S(1)} %bitcast.30, f32[128,512]{1,0:T(8,128)S(1)} %get-tuple-element.22.a_ref, ...), custom_call_target="tpu_custom_call" | custom-call | tf_op jit(solution)/shard_map/pallas_call | solution.py:314
  34.7 1.9 %collective-permute-start.3 = (f32[256,256]{1,0:T(8,128)S(1)}, f32[256,256]{1,0:T(8,128)S(1)}, u32[]{:S(2)}, u32[]{:S(2)}) collective-permute-start(f32[256,256]{1,0:T(8,128)S(1)} %get-tuple-element.32), channel_id=1, source_target_pairs={{256,128},{0,1},{129,257},{385,386},{258,130},{2,3},{131,259},{387... | collective-permute-start | bytes 786440 | tf_op jit(solution)/shard_map/ppermute | solution.py:185
  36.6 3.9 %collective-permute-start.4 = (f32[256,256]{1,0:T(8,128)S(1)}, f32[256,256]{1,0:T(8,128)S(1)}, u32[]{:S(2)}, u32[]{:S(2)}) collective-permute-start(f32[256,256]{1,0:T(8,128)S(1)} %get-tuple-element.33), channel_id=1, source_target_pairs={{384,256},{128,0},{1,129},{257,385},{386,258},{130,2},{3,131},{259... | collective-permute-start | bytes 786440 | tf_op jit(solution)/shard_map/ppermute | solution.py:186
  40.5 0.0 copy-done.2
  40.5 0.3 fusion.3
  40.9 0.2 convolution_multiply_fusion.around_ref
  41.1 1.8 %collective-permute-done.3.got_odd = f32[256,256]{1,0:T(8,128)S(1)} collective-permute-done((f32[256,256]{1,0:T(8,128)S(1)}, f32[256,256]{1,0:T(8,128)S(1)}, u32[]{:S(2)}, u32[]{:S(2)}) %collective-permute-start.3) | collective-permute-done | bytes 262176 | tf_op jit(solution)/shard_map/ppermute | solution.py:185
  42.9 1.9 %collective-permute-done.4.got_even = f32[256,256]{1,0:T(8,128)S(1)} collective-permute-done((f32[256,256]{1,0:T(8,128)S(1)}, f32[256,256]{1,0:T(8,128)S(1)}, u32[]{:S(2)}, u32[]{:S(2)}) %collective-permute-start.4) | collective-permute-done | bytes 262176 | tf_op jit(solution)/shard_map/ppermute | solution.py:186
  44.9 1.4 shard_map.39.own_ref
  46.3 0.1 broadcast_in_dim.2
  46.4 16.9 %all_to_all.33 = f32[4,128,512]{2,1,0:T(8,128)S(1)} all-to-all(f32[4,128,512]{2,1,0:T(8,128)S(1)} %broadcast_in_dim.2), channel_id=1, replica_groups=mesh['yl'=4,'x'=4,'c'=2,'yh'=2,'z'=8] {'x'}, dimensions={0} | all-to-all | bytes 2097152 | tf_op jit(solution)/shard_map/all_to_all | solution.py:348
  63.3 1.9 %collective-permute-start.5 = (f32[512,512]{1,0:T(8,128)S(1)}, f32[512,512]{1,0:T(8,128)S(1)}, u32[]{:S(2)}, u32[]{:S(2)}) collective-permute-start(f32[512,512]{1,0:T(8,128)S(1)} %bitcast.25), channel_id=1, source_target_pairs={{0,16},{16,0},{1,17},{17,1},{2,18},{18,2},{3,19},{19,3},{4,20},{20... | collective-permute-start | bytes 3145736 | tf_op jit(solution)/shard_map/ppermute | solution.py:350
  65.2 2.6 %collective-permute-done.5.far_ref = f32[512,512]{1,0:T(8,128)S(1)} collective-permute-done((f32[512,512]{1,0:T(8,128)S(1)}, f32[512,512]{1,0:T(8,128)S(1)}, u32[]{:S(2)}, u32[]{:S(2)}) %collective-permute-start.5) | collective-permute-done | bytes 1048608 | tf_op jit(solution)/shard_map/ppermute | solution.py:350
  67.8 1.7 %shard_map.40 = f32[1088,128]{1,0:T(8,128)S(1)} custom-call(f32[128,512]{1,0:T(8,128)S(1)} %shard_map.39.own_ref, f32[512,512]{1,0:T(8,128)S(1)} %bitcast.26, f32[512,512]{1,0:T(8,128)S(1)} %collective-permute-done.5.far_ref), custom_call_target="tpu_custom_call" | custom-call | tf_op jit(solution)/shard_map/pallas_call | solution.py:314
  69.5 38.5 %all_to_all.34 = f32[64,1,2176]{2,1,0:T(1,128)S(1)} all-to-all(f32[64,1,2176]{2,1,0:T(1,128)S(1)} %bitcast.34), channel_id=1, replica_groups=mesh['yl'=4,'x'=4,'c'=2,'yh'=2,'z'=8] {'yl','yh','z'}, dimensions={0} | all-to-all | bytes 1114112 | tf_op jit(solution)/shard_map/all_to_all | solution.py:357
  108.0 0.1 shard_map.41
  108.1 25.2 %all_to_all.35 = f32[64,1,2176]{2,1,0:T(1,128)S(1)} all-to-all(f32[64,1,2176]{2,1,0:T(1,128)S(1)} %bitcast.33), channel_id=1, replica_groups=mesh['yl'=4,'x'=4,'c'=2,'yh'=2,'z'=8] {'yl','yh','z'}, dimensions={0} | all-to-all | bytes 1114112 | tf_op jit(solution)/shard_map/all_to_all | solution.py:357
  133.3 0.7 shard_map.42
  134.0 9.8 %all_to_all.36 = f32[4,32,512]{2,1,0:T(8,128)S(1)} all-to-all(f32[4,32,512]{2,1,0:T(8,128)S(1)} %bitcast.35), channel_id=1, replica_groups=mesh['yl'=4,'x'=4,'c'=2,'yh'=2,'z'=8] {'yl'}, dimensions={0} | all-to-all | bytes 524288 | tf_op jit(solution)/shard_map/all_to_all | solution.py:371
  143.8 0.7 copy.8
  (2 shorter events, 0.1 us)
Async XLA Ops:
  0.0 15.3 %copy-start = (f32[8,256,256]{2,1,0:T(8,128)S(1)}, f32[8,256,256]{2,1,0:T(8,128)}, u32[]{:S(2)}) copy-start(f32[8,256,256]{2,1,0:T(8,128)} %param.3) | copy-start | bytes 6291460
  0.0 1.1 copy-start.1
  1.9 15.4 %all-to-all-start = ((f32[4,32,512]{2,1,0:T(8,128)}), f32[4,32,512]{2,1,0:T(8,128)S(1)}, u32[]{:S(2)}, u32[]{:S(2)}) async-start(f32[4,32,512]{2,1,0:T(8,128)} %spread.1), calls=%async_computation | async-start | bytes 524288 | tf_op jit(solution)/shard_map/all_to_all | solution.py:335
  12.8 2.6 %collective-permute-start.2 = (f32[256,256]{1,0:T(8,128)}, f32[256,256]{1,0:T(8,128)}, u32[]{:S(2)}, u32[]{:S(2)}) collective-permute-start(f32[256,256]{1,0:T(8,128)} %slice_bitcast_fusion), channel_id=1, source_target_pairs={{0,1},{385,386},{2,3},{387,388},{4,5},{389,390},{6,7},{391,8},{392... | collective-permute-start | bytes 786440 | tf_op jit(solution)/shard_map/ppermute | solution.py:50
  17.3 23.2 %copy-start.2 = (f32[256,256]{1,0:T(8,128)S(1)}, f32[256,256]{1,0:T(8,128)}, u32[]{:S(2)}) copy-start(f32[256,256]{1,0:T(8,128)} %bitcast_select_fusion) | copy-start | bytes 786436
  18.7 12.0 %collective-permute-start = (f32[256,256]{1,0:T(8,128)S(1)}, f32[256,256]{1,0:T(8,128)S(1)}, u32[]{:S(2)}, u32[]{:S(2)}) collective-permute-start(f32[256,256]{1,0:T(8,128)S(1)} %get-tuple-element.23), channel_id=1, source_target_pairs={{256,128},{0,1},{129,257},{385,386},{258,130},{2,3},{131,259},{387... | collective-permute-start | bytes 786440 | tf_op jit(solution)/shard_map/ppermute | solution.py:185
  21.8 10.8 %collective-permute-start.1 = (f32[256,256]{1,0:T(8,128)S(1)}, f32[256,256]{1,0:T(8,128)S(1)}, u32[]{:S(2)}, u32[]{:S(2)}) collective-permute-start(f32[256,256]{1,0:T(8,128)S(1)} %get-tuple-element.24), channel_id=1, source_target_pairs={{384,256},{128,0},{1,129},{257,385},{386,258},{130,2},{3,131},{259... | collective-permute-start | bytes 786440 | tf_op jit(solution)/shard_map/ppermute | solution.py:186
  34.7 8.3 %collective-permute-start.3 = (f32[256,256]{1,0:T(8,128)S(1)}, f32[256,256]{1,0:T(8,128)S(1)}, u32[]{:S(2)}, u32[]{:S(2)}) collective-permute-start(f32[256,256]{1,0:T(8,128)S(1)} %get-tuple-element.32), channel_id=1, source_target_pairs={{256,128},{0,1},{129,257},{385,386},{258,130},{2,3},{131,259},{387... | collective-permute-start | bytes 786440 | tf_op jit(solution)/shard_map/ppermute | solution.py:185
  36.6 8.3 %collective-permute-start.4 = (f32[256,256]{1,0:T(8,128)S(1)}, f32[256,256]{1,0:T(8,128)S(1)}, u32[]{:S(2)}, u32[]{:S(2)}) collective-permute-start(f32[256,256]{1,0:T(8,128)S(1)} %get-tuple-element.33), channel_id=1, source_target_pairs={{384,256},{128,0},{1,129},{257,385},{386,258},{130,2},{3,131},{259... | collective-permute-start | bytes 786440 | tf_op jit(solution)/shard_map/ppermute | solution.py:186
  63.3 4.5 %collective-permute-start.5 = (f32[512,512]{1,0:T(8,128)S(1)}, f32[512,512]{1,0:T(8,128)S(1)}, u32[]{:S(2)}, u32[]{:S(2)}) collective-permute-start(f32[512,512]{1,0:T(8,128)S(1)} %bitcast.25), channel_id=1, source_target_pairs={{0,16},{16,0},{1,17},{17,1},{2,18},{18,2},{3,19},{19,3},{4,20},{20... | collective-permute-start | bytes 3145736 | tf_op jit(solution)/shard_map/ppermute | solution.py:350

commit v7 on v6

--- a/solution.py
+++ b/solution.py
@@ -226,7 +226,7 @@
         out_shape=jax.ShapeDtypeStruct((count, rows, width // count), jnp.float32),
         in_specs=[
             pl.BlockSpec(memory_space=pltpu.SMEM),
-            pl.BlockSpec(memory_space=pl.ANY),
+            pl.BlockSpec(memory_space=pltpu.HBM),
         ],
         out_specs=pl.BlockSpec(memory_space=pltpu.VMEM),
         scratch_shapes=[pltpu.SemaphoreType.DMA((count,))],
@@ -236,19 +236,23 @@
     )(flip, vectors)
 
 
-def gram_kernel(own_ref, near_ref, far_ref, out_ref):
-    own = split(own_ref[...])
+def gram_half(own_ref, ref):
+    tiles = product(split(own_ref[...]), split(ref[...]), ((1,), (1,)))
     ones = jnp.ones((TILE, own_ref.shape[1]), jnp.bfloat16)
-    tiles, squares = [], []
-    for ref in (near_ref, far_ref):
-        tiles.append(product(own, split(ref[...]), ((1,), (1,))))
-        square = split(ref[...] * ref[...])
-        sums = [
-            lax.dot_general(ones, part, (((1,), (1,)), ((), ())), preferred_element_type=jnp.float32)
-            for part in square
-        ]
-        squares.append(sums[0] + sums[1])
-    across = near_ref.shape[0] // LANES
+    sums = [
+        lax.dot_general(ones, part, (((1,), (1,)), ((), ())), preferred_element_type=jnp.float32)
+        for part in split(ref[...] * ref[...])
+    ]
+    return tiles, sums[0] + sums[1]
+
+
+def near_kernel(own_ref, near_ref, tiles_ref, squares_ref):
+    tiles_ref[...], squares_ref[...] = gram_half(own_ref, near_ref)
+
+
+def gram_kernel(own_ref, tiles_ref, squares_ref, far_ref, out_ref):
+    tiles, squares = zip((tiles_ref[...], squares_ref[...]), gram_half(own_ref, far_ref))
+    across = far_ref.shape[0] // LANES
     step = 2 * TILE + 1
     for m in range(out_ref.shape[0] // step):
         i, j = m // across * TILE, m % across * LANES
@@ -348,6 +352,8 @@
     near = lax.all_to_all(copies, "x", split_axis=0, concat_axis=0, tiled=True)
     near = near.reshape(nx * group, depth)
     far = lax.ppermute(near, "c", [(0, 1), (1, 0)])
+    half_types = [jax.ShapeDtypeStruct((n, nx * group), jnp.float32) for n in (group, TILE)]
+    halves = call(near_kernel, half_types, (), own, near)
     members = group // TILE * nx
     packed = (members * (2 * TILE + 1), LANES)
     packed_type = jax.ShapeDtypeStruct(packed, jnp.float32)
@@ -356,7 +362,7 @@
         a = a.reshape(lax.axis_size(SUM), -1)
         return lax.all_to_all(a, SUM, split_axis=0, concat_axis=0, tiled=True).reshape(packed)
 
-    pieces = exchange(call(gram_kernel, [packed_type], (), own, near, far)[0])
+    pieces = exchange(call(gram_kernel, [packed_type], (), own, *halves, far)[0])
     summed = exchange(call(sum_kernel, [packed_type], (), pieces)[0])
     renewed = call(
         functools.partial(mixing_kernel, total_rows),

time: 145 us -> 144 us (level)
    pallas_call x6 -> x7, Pallas kernels: 7.33 us -> 7.45 us  [call(): pl.pallas_call(kernel, out_shape=out_shapes, in_specs=[smem] * len(scalar...]
  transfers between devices with their start and end apart: 7 -> 7, of which waited for: 5 -> 5; matrix products, arithmetic and copies ran while one was open for 5% -> 5% of each run, Pallas kernels for 0% -> 1%
where the time goes in v7:
time: 144 us
  blocking collectives  90.3 us (63%)
  starting transfers between devices  27.8 us (19%)
  Pallas kernels  8.27 us (6%)
  waiting for transfers between devices  7.67 us (5%)
  local copies, waits for them, and re-layouts  4.72 us (3%)
  matrix products  2.97 us (2%)
  other arithmetic  1.79 us (1%)
    all_to_all x2, blocking collectives, exchange(): lax.all_to_all(a, SUM, split_axis=0, concat_axis=0, tiled=True)  63.6 us
    all_to_all x1, blocking collectives, local(): near = lax.all_to_all(copies, 'x', split_axis=0, concat_axis=0, tiled=True)  16.9 us
    ppermute x2, starting transfers between devices, chebyshev(): even = lax.ppermute(even, SUM, swaps[1])  10.4 us
    all_to_all x1, blocking collectives, local(): back = lax.all_to_all(back, 'yl', split_axis=0, concat_axis=0, tiled=True)  9.76 us
    all_to_all x1, starting transfers between devices, local(): own = lax.all_to_all(chunks, 'yl', split_axis=0, concat_axis=0, tiled=True)  9.18 us
    pallas_call x7, Pallas kernels, call(): pl.pallas_call(kernel, out_shape=out_shapes, in_specs=[smem] * len(scalar...  7.45 us
    ppermute x2, starting transfers between devices, chebyshev(): odd = lax.ppermute(odd, SUM, swaps[0])  5.01 us
    ppermute x2, waiting for transfers between devices, chebyshev(): even = lax.ppermute(even, SUM, swaps[1])  3.81 us
  transfers between devices with their start and end apart: 7, of which 5 were waited for; matrix products, arithmetic and copies ran while one was open for 5% of the time, Pallas kernels for 1%

profile of v7, /device:TPU:8, one launch (start us, length us, event | category | flops | bytes accessed | tf_op | source)
XLA Modules:
  0.0 143.7 jit_solution(5292014523795241093)
XLA Ops:
  0.0 0.0 copy-start
  0.0 0.0 copy-start.1
  0.0 1.1 copy-done.1
  1.1 0.8 spread.1
  1.9 9.2 %all-to-all-start = ((f32[4,32,512]{2,1,0:T(8,128)}), f32[4,32,512]{2,1,0:T(8,128)S(1)}, u32[]{:S(2)}, u32[]{:S(2)}) async-start(f32[4,32,512]{2,1,0:T(8,128)} %spread.1), calls=%async_computation | async-start | bytes 524288 | tf_op jit(solution)/shard_map/all_to_all | solution.py:339
  11.1 1.7 %slice_bitcast_fusion = f32[256,256]{1,0:T(8,128)} fusion(f32[8,256,256]{2,1,0:T(8,128)} %param.4), kind=kLoop, calls=%fused_computation.4 | loop fusion | bytes 524288 | tf_op jit(solution)/shard_map/squeeze | solution.py:50
  12.8 1.4 collective-permute-start.2
  14.1 1.1 constant_dynamic-slice_fusion.c_ref
  15.2 0.1 pad_add_fusion.flags
  15.3 0.0 copy-done
  15.4 0.0 collective-permute-done.2
  15.4 1.7 %bitcast_select_fusion = f32[256,256]{1,0:T(8,128)} fusion(f32[256,256]{1,0:T(8,128)} %collective-permute-done.2, f32[8,256,256]{2,1,0:T(8,128)} %param.4, s32[]{:T(128)S(6)} %max.3, pred[]{:T(512)S(6)} %eq.18), kind=kLoop, calls=%fused_computation.3 | loop fusion | flops 65536 | bytes 786437 | tf_op jit(solution)/shard_map/jit(_where)/select_n | solution.py:55
  17.1 0.3 all-to-all-done
  17.3 0.0 copy-start.2
  17.3 1.4 shard_map.37
  18.7 3.1 %collective-permute-start = (f32[256,256]{1,0:T(8,128)S(1)}, f32[256,256]{1,0:T(8,128)S(1)}, u32[]{:S(2)}, u32[]{:S(2)}) collective-permute-start(f32[256,256]{1,0:T(8,128)S(1)} %get-tuple-element.25), channel_id=1, source_target_pairs={{256,128},{0,1},{129,257},{385,386},{258,130},{2,3},{131,259},{387... | collective-permute-start | bytes 786440 | tf_op jit(solution)/shard_map/ppermute | solution.py:185
  21.8 6.4 %collective-permute-start.1 = (f32[256,256]{1,0:T(8,128)S(1)}, f32[256,256]{1,0:T(8,128)S(1)}, u32[]{:S(2)}, u32[]{:S(2)}) collective-permute-start(f32[256,256]{1,0:T(8,128)S(1)} %get-tuple-element.26), channel_id=1, source_target_pairs={{384,256},{128,0},{1,129},{257,385},{386,258},{130,2},{3,131},{259... | collective-permute-start | bytes 786440 | tf_op jit(solution)/shard_map/ppermute | solution.py:186
  28.2 1.2 fusion.1
  29.5 1.2 fusion.5.around_ref
  30.7 0.0 collective-permute-done.got_odd
  30.7 1.9 %collective-permute-done.1.got_even = f32[256,256]{1,0:T(8,128)S(1)} collective-permute-done((f32[256,256]{1,0:T(8,128)S(1)}, f32[256,256]{1,0:T(8,128)S(1)}, u32[]{:S(2)}, u32[]{:S(2)}) %collective-permute-start.1) | collective-permute-done | bytes 262176 | tf_op jit(solution)/shard_map/ppermute | solution.py:186
  32.6 2.1 %shard_map.38 = (f32[128,512]{1,0:T(8,128)S(1)}, f32[128,512]{1,0:T(8,128)S(1)}, f32[256,256]{1,0:T(8,128)S(1)}, f32[256,256]{1,0:T(8,128)S(1)}, f32[128,256]{1,0:T(8,128)S(1)}) custom-call(s32[2]{0:T(128)S(1)} %pad_add_fusion.flags, f32[128,512]{1,0:T(8,128)S(1)} %bitcast.30, f32[128,512]{1,0:T(8,128)S(1)} %get-tuple-element.24.a_ref, ...), custom_call_target="tpu_custom_call" | custom-call | tf_op jit(solution)/shard_map/pallas_call | solution.py:318
  34.6 1.9 %collective-permute-start.3 = (f32[256,256]{1,0:T(8,128)S(1)}, f32[256,256]{1,0:T(8,128)S(1)}, u32[]{:S(2)}, u32[]{:S(2)}) collective-permute-start(f32[256,256]{1,0:T(8,128)S(1)} %get-tuple-element.34), channel_id=1, source_target_pairs={{256,128},{0,1},{129,257},{385,386},{258,130},{2,3},{131,259},{387... | collective-permute-start | bytes 786440 | tf_op jit(solution)/shard_map/ppermute | solution.py:185
  36.6 3.9 %collective-permute-start.4 = (f32[256,256]{1,0:T(8,128)S(1)}, f32[256,256]{1,0:T(8,128)S(1)}, u32[]{:S(2)}, u32[]{:S(2)}) collective-permute-start(f32[256,256]{1,0:T(8,128)S(1)} %get-tuple-element.35), channel_id=1, source_target_pairs={{384,256},{128,0},{1,129},{257,385},{386,258},{130,2},{3,131},{259... | collective-permute-start | bytes 786440 | tf_op jit(solution)/shard_map/ppermute | solution.py:186
  40.5 0.0 copy-done.2
  40.5 0.3 fusion.3
  40.8 0.2 convolution_multiply_fusion.around_ref
  41.1 1.8 %collective-permute-done.3.got_odd = f32[256,256]{1,0:T(8,128)S(1)} collective-permute-done((f32[256,256]{1,0:T(8,128)S(1)}, f32[256,256]{1,0:T(8,128)S(1)}, u32[]{:S(2)}, u32[]{:S(2)}) %collective-permute-start.3) | collective-permute-done | bytes 262176 | tf_op jit(solution)/shard_map/ppermute | solution.py:185
  42.9 1.9 %collective-permute-done.4.got_even = f32[256,256]{1,0:T(8,128)S(1)} collective-permute-done((f32[256,256]{1,0:T(8,128)S(1)}, f32[256,256]{1,0:T(8,128)S(1)}, u32[]{:S(2)}, u32[]{:S(2)}) %collective-permute-start.4) | collective-permute-done | bytes 262176 | tf_op jit(solution)/shard_map/ppermute | solution.py:186
  44.8 1.4 shard_map.39.own_ref
  46.3 0.1 broadcast_in_dim.2
  46.4 16.9 %all_to_all.33 = f32[4,128,512]{2,1,0:T(8,128)S(1)} all-to-all(f32[4,128,512]{2,1,0:T(8,128)S(1)} %broadcast_in_dim.2), channel_id=1, replica_groups=mesh['yl'=4,'x'=4,'c'=2,'yh'=2,'z'=8] {'x'}, dimensions={0} | all-to-all | bytes 2097152 | tf_op jit(solution)/shard_map/all_to_all | solution.py:352
  63.3 1.9 %collective-permute-start.5 = (f32[512,512]{1,0:T(8,128)S(1)}, f32[512,512]{1,0:T(8,128)S(1)}, u32[]{:S(2)}, u32[]{:S(2)}) collective-permute-start(f32[512,512]{1,0:T(8,128)S(1)} %bitcast.25), channel_id=1, source_target_pairs={{0,16},{16,0},{1,17},{17,1},{2,18},{18,2},{3,19},{19,3},{4,20},{20... | collective-permute-start | bytes 3145736 | tf_op jit(solution)/shard_map/ppermute | solution.py:354
  65.2 0.9 shard_map.40
  66.1 1.7 %collective-permute-done.5.far_ref = f32[512,512]{1,0:T(8,128)S(1)} collective-permute-done((f32[512,512]{1,0:T(8,128)S(1)}, f32[512,512]{1,0:T(8,128)S(1)}, u32[]{:S(2)}, u32[]{:S(2)}) %collective-permute-start.5) | collective-permute-done | bytes 1048608 | tf_op jit(solution)/shard_map/ppermute | solution.py:354
  67.8 0.9 shard_map.41
  68.7 38.5 %all_to_all.34 = f32[64,1,2176]{2,1,0:T(1,128)S(1)} all-to-all(f32[64,1,2176]{2,1,0:T(1,128)S(1)} %bitcast.32), channel_id=1, replica_groups=mesh['yl'=4,'x'=4,'c'=2,'yh'=2,'z'=8] {'yl','yh','z'}, dimensions={0} | all-to-all | bytes 1114112 | tf_op jit(solution)/shard_map/all_to_all | solution.py:363
  107.2 0.1 shard_map.42
  107.3 25.2 %all_to_all.35 = f32[64,1,2176]{2,1,0:T(1,128)S(1)} all-to-all(f32[64,1,2176]{2,1,0:T(1,128)S(1)} %bitcast.34), channel_id=1, replica_groups=mesh['yl'=4,'x'=4,'c'=2,'yh'=2,'z'=8] {'yl','yh','z'}, dimensions={0} | all-to-all | bytes 1114112 | tf_op jit(solution)/shard_map/all_to_all | solution.py:363
  132.5 0.7 shard_map.43
  133.2 9.8 %all_to_all.36 = f32[4,32,512]{2,1,0:T(8,128)S(1)} all-to-all(f32[4,32,512]{2,1,0:T(8,128)S(1)} %bitcast.35), channel_id=1, replica_groups=mesh['yl'=4,'x'=4,'c'=2,'yh'=2,'z'=8] {'yl'}, dimensions={0} | all-to-all | bytes 524288 | tf_op jit(solution)/shard_map/all_to_all | solution.py:377
  143.0 0.7 copy.8
  (2 shorter events, 0.1 us)
Async XLA Ops:
  0.0 15.3 %copy-start = (f32[8,256,256]{2,1,0:T(8,128)S(1)}, f32[8,256,256]{2,1,0:T(8,128)}, u32[]{:S(2)}) copy-start(f32[8,256,256]{2,1,0:T(8,128)} %param.3) | copy-start | bytes 6291460
  0.0 1.1 copy-start.1
  1.9 15.4 %all-to-all-start = ((f32[4,32,512]{2,1,0:T(8,128)}), f32[4,32,512]{2,1,0:T(8,128)S(1)}, u32[]{:S(2)}, u32[]{:S(2)}) async-start(f32[4,32,512]{2,1,0:T(8,128)} %spread.1), calls=%async_computation | async-start | bytes 524288 | tf_op jit(solution)/shard_map/all_to_all | solution.py:339
  12.8 2.6 %collective-permute-start.2 = (f32[256,256]{1,0:T(8,128)}, f32[256,256]{1,0:T(8,128)}, u32[]{:S(2)}, u32[]{:S(2)}) collective-permute-start(f32[256,256]{1,0:T(8,128)} %slice_bitcast_fusion), channel_id=1, source_target_pairs={{0,1},{385,386},{2,3},{387,388},{4,5},{389,390},{6,7},{391,8},{392... | collective-permute-start | bytes 786440 | tf_op jit(solution)/shard_map/ppermute | solution.py:50
  17.3 23.2 %copy-start.2 = (f32[256,256]{1,0:T(8,128)S(1)}, f32[256,256]{1,0:T(8,128)}, u32[]{:S(2)}) copy-start(f32[256,256]{1,0:T(8,128)} %bitcast_select_fusion) | copy-start | bytes 786436
  18.7 12.0 %collective-permute-start = (f32[256,256]{1,0:T(8,128)S(1)}, f32[256,256]{1,0:T(8,128)S(1)}, u32[]{:S(2)}, u32[]{:S(2)}) collective-permute-start(f32[256,256]{1,0:T(8,128)S(1)} %get-tuple-element.25), channel_id=1, source_target_pairs={{256,128},{0,1},{129,257},{385,386},{258,130},{2,3},{131,259},{387... | collective-permute-start | bytes 786440 | tf_op jit(solution)/shard_map/ppermute | solution.py:185
  21.8 10.8 %collective-permute-start.1 = (f32[256,256]{1,0:T(8,128)S(1)}, f32[256,256]{1,0:T(8,128)S(1)}, u32[]{:S(2)}, u32[]{:S(2)}) collective-permute-start(f32[256,256]{1,0:T(8,128)S(1)} %get-tuple-element.26), channel_id=1, source_target_pairs={{384,256},{128,0},{1,129},{257,385},{386,258},{130,2},{3,131},{259... | collective-permute-start | bytes 786440 | tf_op jit(solution)/shard_map/ppermute | solution.py:186
  34.6 8.3 %collective-permute-start.3 = (f32[256,256]{1,0:T(8,128)S(1)}, f32[256,256]{1,0:T(8,128)S(1)}, u32[]{:S(2)}, u32[]{:S(2)}) collective-permute-start(f32[256,256]{1,0:T(8,128)S(1)} %get-tuple-element.34), channel_id=1, source_target_pairs={{256,128},{0,1},{129,257},{385,386},{258,130},{2,3},{131,259},{387... | collective-permute-start | bytes 786440 | tf_op jit(solution)/shard_map/ppermute | solution.py:185
  36.6 8.3 %collective-permute-start.4 = (f32[256,256]{1,0:T(8,128)S(1)}, f32[256,256]{1,0:T(8,128)S(1)}, u32[]{:S(2)}, u32[]{:S(2)}) collective-permute-start(f32[256,256]{1,0:T(8,128)S(1)} %get-tuple-element.35), channel_id=1, source_target_pairs={{384,256},{128,0},{1,129},{257,385},{386,258},{130,2},{3,131},{259... | collective-permute-start | bytes 786440 | tf_op jit(solution)/shard_map/ppermute | solution.py:186
  63.3 4.5 %collective-permute-start.5 = (f32[512,512]{1,0:T(8,128)S(1)}, f32[512,512]{1,0:T(8,128)S(1)}, u32[]{:S(2)}, u32[]{:S(2)}) collective-permute-start(f32[512,512]{1,0:T(8,128)S(1)} %bitcast.25), channel_id=1, source_target_pairs={{0,16},{16,0},{1,17},{17,1},{2,18},{18,2},{3,19},{19,3},{4,20},{20... | collective-permute-start | bytes 3145736 | tf_op jit(solution)/shard_map/ppermute | solution.py:354

commit v8 on v7

--- a/solution.py
+++ b/solution.py
@@ -74,7 +74,7 @@
 def local_terms(y, parts, diagonal, coupling):
     terms = []
     for n, block in enumerate(y):
-        term = product(parts[n], diagonal(n), ((1,), (1,))) - filter_center * block
+        term = product(parts[n], diagonal(n), ((1,), (0,))) - filter_center * block
         if n + 1 < len(y):
             term = term + product(parts[n + 1], coupling(n), ((1,), (1,)))
         if n > 0:
@@ -101,12 +101,22 @@
                 ref[rows:, :] = pair[1]
 
 
-def start_kernel(flags, y_ref, d_ref, c_ref, dh, dl, ch, cl, a_ref, odd_ref, even_ref, term_ref):
+def split_kernel(d_ref, c_ref, dh, dl, ch, cl):
     for ref, high, low in ((d_ref, dh, dl), (c_ref, ch, cl)):
         for n in range(ref.shape[0]):
             high[n], low[n] = split(ref[n])
-    size = d_ref.shape[1]
-    y = blocks_of(y_ref, size)
+
+
+def in_rank_order(flags, count):
+    return [jnp.where(flags[2] == 1, count - 1 - i, i) for i in range(count)]
+
+
+def start_kernel(count, flags, got_ref, dh, dl, ch, cl, y_ref, a_ref, odd_ref, even_ref, term_ref):
+    rows = got_ref.shape[0] // count
+    for i, at in enumerate(in_rank_order(flags, count)):
+        at = pl.multiple_of(at * rows, rows)
+        y_ref[i * rows : (i + 1) * rows, :] = got_ref[pl.ds(at, rows), :]
+    y = blocks_of(y_ref, dh.shape[1])
     parts = [split(block) for block in y]
     coupling = lambda n: (ch[n], cl[n])
     a = local_terms(y, parts, lambda n: (dh[n], dl[n]), coupling)
@@ -177,8 +187,13 @@
     panel = jax.ShapeDtypeStruct(y.shape, jnp.float32)
     sends = [panel, message, message, jax.ShapeDtypeStruct((rows, size), jnp.float32)]
     halves = [jax.ShapeDtypeStruct(diag_blocks.shape, jnp.bfloat16)] * 4
-    *hamiltonian, a, odd, even, term = call(
-        start_kernel, halves + sends, (flags,), y, diag_blocks, coupling
+    hamiltonian = call(split_kernel, halves, (), diag_blocks, coupling)
+    y, a, odd, even, term = call(
+        functools.partial(start_kernel, lax.axis_size("yl")),
+        [panel] + sends,
+        (flags,),
+        y,
+        *hamiltonian,
     )
     for turn in range(0, DEGREE, 2):
         scale = (1.0 if turn == 0 else 2.0) / filter_half
@@ -206,36 +221,6 @@
     return y
 
 
-def spread_kernel(flip, in_ref, out_ref, sems):
-    count, _, depth = out_ref.shape
-    copies = []
-    for j in range(count):
-        at = jnp.where(flip[0] == 1, count - 1 - j, j) * depth
-        source = in_ref.at[:, pl.ds(pl.multiple_of(at, depth), depth)]
-        copies.append(pltpu.make_async_copy(source, out_ref.at[j], sems.at[j]))
-    for copy in copies:
-        copy.start()
-    for copy in copies:
-        copy.wait()
-
-
-def spread(flip, vectors, count):
-    rows, width = vectors.shape
-    return pl.pallas_call(
-        spread_kernel,
-        out_shape=jax.ShapeDtypeStruct((count, rows, width // count), jnp.float32),
-        in_specs=[
-            pl.BlockSpec(memory_space=pltpu.SMEM),
-            pl.BlockSpec(memory_space=pltpu.HBM),
-        ],
-        out_specs=pl.BlockSpec(memory_space=pltpu.VMEM),
-        scratch_shapes=[pltpu.SemaphoreType.DMA((count,))],
-        name="spread",
-        compiler_params=pltpu.CompilerParams(vmem_limit_bytes=24 * 2**20),
-        interpret=INTERPRET,
-    )(flip, vectors)
-
-
 def gram_half(own_ref, ref):
     tiles = product(split(own_ref[...]), split(ref[...]), ((1,), (1,)))
     ones = jnp.ones((TILE, own_ref.shape[1]), jnp.bfloat16)
@@ -282,7 +267,7 @@
         out_ref[group * g : group * (g + 1), :] = total
 
 
-def mixing_kernel(total_rows, at_ref, summed_ref, own_ref, near_ref, far_ref, out_ref):
+def mixing_kernel(total_rows, count, at_ref, flags, summed_ref, own_ref, near_ref, far_ref, out_ref):
     step = 2 * TILE + 1
     across = near_ref.shape[0] // LANES
     group = own_ref.shape[0]
@@ -309,7 +294,10 @@
             columns.append((0.5 / total_rows) * (column * mine * scale) * scale)
         mixing = jnp.concatenate(columns, axis=1)
         result = result - product(split(mixing), split(ref[...]), ((1,), (0,)))
-    out_ref[...] = result
+    rows = group // count
+    for i, to in enumerate(in_rank_order(flags, count)):
+        to = pl.multiple_of(to * rows, rows)
+        out_ref[pl.ds(to, rows), :] = result[i * rows : (i + 1) * rows, :]
 
 
 def call(kernel, out_shapes, scalars, *arrays):
@@ -332,21 +320,30 @@
     total_rows = width * lax.axis_size(ROW)
     at, vectors = lax.optimization_barrier((lax.axis_index("x").reshape(1), vectors))
     flip = flipped(lax.axis_index("yh"), lax.axis_index("z"))
+    places = snake()
+    groups = [places[i : i + nyl] for i in range(0, len(places), nyl)]
+
+    def exchange_chunks(a):
+        return lax.all_to_all(
+            a, SUM, split_axis=0, concat_axis=0, axis_index_groups=groups, tiled=True
+        )
+
     yl = lax.axis_index("yl")
     chunk = jnp.where(flip, nyl - 1 - yl, yl)
     part, group, depth = blocks // nyl, nyl * count, width // nyl
-    chunks = spread(flip.astype(jnp.int32).reshape(1), vectors, nyl)
-    own = lax.all_to_all(chunks, "yl", split_axis=0, concat_axis=0, tiled=True)
+    chunks = vectors.reshape(count, nyl, depth).transpose(1, 0, 2)
+    own = exchange_chunks(chunks)
     own = own.reshape(group, depth)
     is_top = (lax.axis_index(ROW) == lax.axis_size(ROW) - 1) & (chunk == nyl - 1)
     own_diag = lax.dynamic_slice_in_dim(diag_blocks, chunk * part, part)
     own_coupling = lax.dynamic_slice_in_dim(coupling, chunk * part, part)
+    flags = jnp.stack([chunk % 2, is_top.astype(jnp.int32), flip.astype(jnp.int32)])
     own = chebyshev(
         own,
         own_diag,
         own_coupling,
         edge_coupling(coupling, chunk),
-        jnp.stack([chunk % 2, is_top.astype(jnp.int32)]),
+        flags,
     )
     copies = jnp.broadcast_to(own[None], (nx, group, depth))
     near = lax.all_to_all(copies, "x", split_axis=0, concat_axis=0, tiled=True)
@@ -365,17 +362,16 @@
     pieces = exchange(call(gram_kernel, [packed_type], (), own, *halves, far)[0])
     summed = exchange(call(sum_kernel, [packed_type], (), pieces)[0])
     renewed = call(
-        functools.partial(mixing_kernel, total_rows),
+        functools.partial(mixing_kernel, total_rows, nyl),
         [jax.ShapeDtypeStruct((group, depth), jnp.float32)],
-        (at,),
+        (at, flags),
         summed,
         own,
         near,
         far,
     )[0]
     back = renewed.reshape(nyl, count, depth)
-    back = lax.all_to_all(back, "yl", split_axis=0, concat_axis=0, tiled=True)
-    back = jnp.where(flip, back[::-1], back)
+    back = exchange_chunks(back)
     return back.transpose(1, 0, 2).reshape(count, width)
 
 

time: 144 us -> 144 us (level)
  the two profiles are of different devices: /device:TPU:8 before, /device:TPU:1 now
where the time goes in v8:
time: 144 us; the launch traced here: 141 us
  blocking collectives  84.1 us (58%)
  starting transfers between devices  26.1 us (18%)
  waiting for transfers between devices  9.34 us (6%)
  local copies, waits for them, and re-layouts  9.11 us (6%)
  Pallas kernels  7.85 us (5%)
  matrix products  2.96 us (2%)
  other arithmetic  1.77 us (1%)
    all_to_all x2, blocking collectives, exchange(): lax.all_to_all(a, SUM, split_axis=0, concat_axis=0, tiled=True)  59.9 us
    all_to_all x1, blocking collectives, local(): near = lax.all_to_all(copies, 'x', split_axis=0, concat_axis=0, tiled=True)  15.6 us
    all_to_all x1, blocking collectives, exchange_chunks(): lax.all_to_all(a, SUM, split_axis=0, concat_axis=0, axis_index_groups=gro...  8.72 us
    pallas_call x8, Pallas kernels, call(): pl.pallas_call(kernel, out_shape=out_shapes, in_specs=[smem] * len(scalar...  7.85 us
    all_to_all x1, starting transfers between devices, exchange_chunks(): lax.all_to_all(a, SUM, split_axis=0, concat_axis=0, axis_index_groups=gro...  7.52 us
    ppermute x1, starting transfers between devices, local(): far = lax.ppermute(near, 'c', [(0, 1), (1, 0)])  6.83 us
    ppermute x2, waiting for transfers between devices, chebyshev(): even = lax.ppermute(even, SUM, swaps[1])  5.9 us
    ppermute x2, starting transfers between devices, chebyshev(): odd = lax.ppermute(odd, SUM, swaps[0])  5.3 us
  transfers between devices with their start and end apart: 7, of which 5 were waited for; matrix products, arithmetic and copies ran while one was open for 6% of the time, Pallas kernels for 1%

profile of v8, /device:TPU:1, one launch (start us, length us, event | category | flops | bytes accessed | tf_op | source)
XLA Modules:
  0.0 141.4 jit_solution(6388072633912821500)
XLA Ops:
  0.0 0.0 copy-start
  0.0 1.8 %copy.13 = f32[4,4,8,512]{3,2,0,1:T(8,128)} copy(f32[4,4,8,512]{3,2,1,0:T(8,128)} %bitcast.41) | data formatting | bytes 524288 | tf_op jit(solution)/shard_map/reshape | solution.py:334
  1.8 7.5 %all-to-all-start = ((f32[4,32,512]{2,1,0:T(8,128)}), f32[4,32,512]{2,1,0:T(8,128)S(1)}, u32[]{:S(2)}, u32[]{:S(2)}) async-start(f32[4,32,512]{2,1,0:T(8,128)} %bitcast.30), calls=%async_computation | async-start | bytes 524288 | tf_op jit(solution)/shard_map/all_to_all | solution.py:327
  9.3 1.7 %slice_bitcast_fusion = f32[256,256]{1,0:T(8,128)} fusion(f32[8,256,256]{2,1,0:T(8,128)} %param.4), kind=kLoop, calls=%fused_computation.3 | loop fusion | bytes 524288 | tf_op jit(solution)/shard_map/squeeze | solution.py:50
  11.0 2.6 %collective-permute-start.2 = (f32[256,256]{1,0:T(8,128)}, f32[256,256]{1,0:T(8,128)}, u32[]{:S(2)}, u32[]{:S(2)}) collective-permute-start(f32[256,256]{1,0:T(8,128)} %slice_bitcast_fusion), channel_id=1, source_target_pairs={{0,1},{385,386},{2,3},{387,388},{4,5},{389,390},{6,7},{391,8},{392... | collective-permute-start | bytes 786440 | tf_op jit(solution)/shard_map/ppermute | solution.py:50
  13.6 1.9 %constant_dynamic-slice_fusion.c_ref = f32[2,256,256]{2,1,0:T(8,128)} fusion(f32[8,256,256]{2,1,0:T(8,128)} %param.4, s32[]{:T(128)S(6)} %select_n.31), kind=kLoop, calls=%fused_computation.8 | loop fusion | bytes 1048580 | tf_op jit(solution)/shard_map/dynamic_slice | solution.py:339
  15.5 0.0 copy-done
  15.5 0.8 constant_dynamic-slice_fusion.1.d_ref
  16.3 0.0 copy-start.1
  16.3 1.0 copy-done.1
  17.4 0.0 copy-start.2
  17.4 1.0 copy-done.2
  18.4 0.2 shard_map.37
  18.6 0.1 pad_add_fusion.flags
  18.6 0.0 collective-permute-done.2
  18.6 1.7 %bitcast_select_fusion = f32[256,256]{1,0:T(8,128)} fusion(f32[256,256]{1,0:T(8,128)} %collective-permute-done.2, f32[8,256,256]{2,1,0:T(8,128)} %param.4, s32[]{:T(128)S(6)} %max.3, pred[]{:T(512)S(6)} %eq.18), kind=kLoop, calls=%fused_computation.2 | loop fusion | flops 65536 | bytes 786437 | tf_op jit(solution)/shard_map/jit(_where)/select_n | solution.py:55
  20.3 0.0 all-to-all-done
  20.3 0.0 copy-start.3
  20.3 1.2 shard_map.38
  21.5 2.0 %collective-permute-start = (f32[256,256]{1,0:T(8,128)S(1)}, f32[256,256]{1,0:T(8,128)S(1)}, u32[]{:S(2)}, u32[]{:S(2)}) collective-permute-start(f32[256,256]{1,0:T(8,128)S(1)} %get-tuple-element.31), channel_id=1, source_target_pairs={{256,128},{0,1},{129,257},{385,386},{258,130},{2,3},{131,259},{387... | collective-permute-start | bytes 786440 | tf_op jit(solution)/shard_map/ppermute | solution.py:200
  23.5 1.9 %collective-permute-start.1 = (f32[256,256]{1,0:T(8,128)S(1)}, f32[256,256]{1,0:T(8,128)S(1)}, u32[]{:S(2)}, u32[]{:S(2)}) collective-permute-start(f32[256,256]{1,0:T(8,128)S(1)} %get-tuple-element.32), channel_id=1, source_target_pairs={{384,256},{128,0},{1,129},{257,385},{386,258},{130,2},{3,131},{259... | collective-permute-start | bytes 786440 | tf_op jit(solution)/shard_map/ppermute | solution.py:201
  25.4 1.2 fusion.2
  26.7 1.2 fusion.4.around_ref
  27.9 0.8 collective-permute-done.got_odd
  28.6 2.3 %collective-permute-done.1.got_even = f32[256,256]{1,0:T(8,128)S(1)} collective-permute-done((f32[256,256]{1,0:T(8,128)S(1)}, f32[256,256]{1,0:T(8,128)S(1)}, u32[]{:S(2)}, u32[]{:S(2)}) %collective-permute-start.1) | collective-permute-done | bytes 262176 | tf_op jit(solution)/shard_map/ppermute | solution.py:201
  30.9 2.0 %shard_map.39 = (f32[128,512]{1,0:T(8,128)S(1)}, f32[128,512]{1,0:T(8,128)S(1)}, f32[256,256]{1,0:T(8,128)S(1)}, f32[256,256]{1,0:T(8,128)S(1)}, f32[128,256]{1,0:T(8,128)S(1)}) custom-call(s32[3]{0:T(128)S(1)} %pad_add_fusion.flags, f32[128,512]{1,0:T(8,128)S(1)} %get-tuple-element.29.y_ref, f32[128,512]{1,0:T(8,128)S(1)} %get-tuple-element.30.a_ref, ...), custom_call_target="tpu_custom_call" | custom-call | tf_op jit(solution)/shard_map/pallas_call | solution.py:306
  32.9 3.3 %collective-permute-start.3 = (f32[256,256]{1,0:T(8,128)S(1)}, f32[256,256]{1,0:T(8,128)S(1)}, u32[]{:S(2)}, u32[]{:S(2)}) collective-permute-start(f32[256,256]{1,0:T(8,128)S(1)} %get-tuple-element.36), channel_id=1, source_target_pairs={{256,128},{0,1},{129,257},{385,386},{258,130},{2,3},{131,259},{387... | collective-permute-start | bytes 786440 | tf_op jit(solution)/shard_map/ppermute | solution.py:200
  36.2 1.9 %collective-permute-start.4 = (f32[256,256]{1,0:T(8,128)S(1)}, f32[256,256]{1,0:T(8,128)S(1)}, u32[]{:S(2)}, u32[]{:S(2)}) collective-permute-start(f32[256,256]{1,0:T(8,128)S(1)} %get-tuple-element.37), channel_id=1, source_target_pairs={{384,256},{128,0},{1,129},{257,385},{386,258},{130,2},{3,131},{259... | collective-permute-start | bytes 786440 | tf_op jit(solution)/shard_map/ppermute | solution.py:201
  38.1 0.0 copy-done.3
  38.1 0.3 fusion
  38.5 0.2 convolution_multiply_fusion.around_ref
  38.7 1.3 collective-permute-done.3.got_odd
  40.0 3.6 %collective-permute-done.4.got_even = f32[256,256]{1,0:T(8,128)S(1)} collective-permute-done((f32[256,256]{1,0:T(8,128)S(1)}, f32[256,256]{1,0:T(8,128)S(1)}, u32[]{:S(2)}, u32[]{:S(2)}) %collective-permute-start.4) | collective-permute-done | bytes 262176 | tf_op jit(solution)/shard_map/ppermute | solution.py:201
  43.6 1.4 shard_map.40.own_ref
  45.0 0.1 broadcast_in_dim.2
  45.2 15.6 %all_to_all.33 = f32[4,128,512]{2,1,0:T(8,128)S(1)} all-to-all(f32[4,128,512]{2,1,0:T(8,128)S(1)} %broadcast_in_dim.2), channel_id=1, replica_groups=mesh['yl'=4,'x'=4,'c'=2,'yh'=2,'z'=8] {'x'}, dimensions={0} | all-to-all | bytes 2097152 | tf_op jit(solution)/shard_map/all_to_all | solution.py:349
  60.7 6.8 %collective-permute-start.5 = (f32[512,512]{1,0:T(8,128)S(1)}, f32[512,512]{1,0:T(8,128)S(1)}, u32[]{:S(2)}, u32[]{:S(2)}) collective-permute-start(f32[512,512]{1,0:T(8,128)S(1)} %bitcast.31), channel_id=1, source_target_pairs={{0,16},{16,0},{1,17},{17,1},{2,18},{18,2},{3,19},{19,3},{4,20},{20... | collective-permute-start | bytes 3145736 | tf_op jit(solution)/shard_map/ppermute | solution.py:351
  67.6 0.9 shard_map.41
  68.5 1.4 collective-permute-done.5.far_ref
  69.8 0.9 shard_map.42
  70.7 35.1 %all_to_all.34 = f32[64,1,2176]{2,1,0:T(1,128)S(1)} all-to-all(f32[64,1,2176]{2,1,0:T(1,128)S(1)} %bitcast.35), channel_id=1, replica_groups=mesh['yl'=4,'x'=4,'c'=2,'yh'=2,'z'=8] {'yl','yh','z'}, dimensions={0} | all-to-all | bytes 1114112 | tf_op jit(solution)/shard_map/all_to_all | solution.py:360
  105.8 0.1 shard_map.43
  105.9 24.8 %all_to_all.35 = f32[64,1,2176]{2,1,0:T(1,128)S(1)} all-to-all(f32[64,1,2176]{2,1,0:T(1,128)S(1)} %bitcast.37), channel_id=1, replica_groups=mesh['yl'=4,'x'=4,'c'=2,'yh'=2,'z'=8] {'yl','yh','z'}, dimensions={0} | all-to-all | bytes 1114112 | tf_op jit(solution)/shard_map/all_to_all | solution.py:360
  130.7 1.3 shard_map.44
  132.0 8.7 %all_to_all.36 = f32[4,32,512]{2,1,0:T(8,128)S(1)} all-to-all(f32[4,32,512]{2,1,0:T(8,128)S(1)} %bitcast.39), channel_id=1, replica_groups={{384,256,128,0},{1,129,257,385},{386,258,130,2},{3,131,259,387},{388,26..., dimensions={0} | all-to-all | bytes 524288 | tf_op jit(solution)/shard_map/all_to_all | solution.py:327
  140.7 0.7 copy.11
Async XLA Ops:
  0.0 15.5 %copy-start = (f32[8,256,256]{2,1,0:T(8,128)S(1)}, f32[8,256,256]{2,1,0:T(8,128)}, u32[]{:S(2)}) copy-start(f32[8,256,256]{2,1,0:T(8,128)} %param.3) | copy-start | bytes 6291460
  1.8 18.5 %all-to-all-start = ((f32[4,32,512]{2,1,0:T(8,128)}), f32[4,32,512]{2,1,0:T(8,128)S(1)}, u32[]{:S(2)}, u32[]{:S(2)}) async-start(f32[4,32,512]{2,1,0:T(8,128)} %bitcast.30), calls=%async_computation | async-start | bytes 524288 | tf_op jit(solution)/shard_map/all_to_all | solution.py:327
  11.0 7.6 %collective-permute-start.2 = (f32[256,256]{1,0:T(8,128)}, f32[256,256]{1,0:T(8,128)}, u32[]{:S(2)}, u32[]{:S(2)}) collective-permute-start(f32[256,256]{1,0:T(8,128)} %slice_bitcast_fusion), channel_id=1, source_target_pairs={{0,1},{385,386},{2,3},{387,388},{4,5},{389,390},{6,7},{391,8},{392... | collective-permute-start | bytes 786440 | tf_op jit(solution)/shard_map/ppermute | solution.py:50
  16.3 1.0 copy-start.1
  17.4 1.0 copy-start.2
  20.3 17.8 %copy-start.3 = (f32[256,256]{1,0:T(8,128)S(1)}, f32[256,256]{1,0:T(8,128)}, u32[]{:S(2)}) copy-start(f32[256,256]{1,0:T(8,128)} %bitcast_select_fusion) | copy-start | bytes 786436
  21.5 7.1 %collective-permute-start = (f32[256,256]{1,0:T(8,128)S(1)}, f32[256,256]{1,0:T(8,128)S(1)}, u32[]{:S(2)}, u32[]{:S(2)}) collective-permute-start(f32[256,256]{1,0:T(8,128)S(1)} %get-tuple-element.31), channel_id=1, source_target_pairs={{256,128},{0,1},{129,257},{385,386},{258,130},{2,3},{131,259},{387... | collective-permute-start | bytes 786440 | tf_op jit(solution)/shard_map/ppermute | solution.py:200
  23.5 7.4 %collective-permute-start.1 = (f32[256,256]{1,0:T(8,128)S(1)}, f32[256,256]{1,0:T(8,128)S(1)}, u32[]{:S(2)}, u32[]{:S(2)}) collective-permute-start(f32[256,256]{1,0:T(8,128)S(1)} %get-tuple-element.32), channel_id=1, source_target_pairs={{384,256},{128,0},{1,129},{257,385},{386,258},{130,2},{3,131},{259... | collective-permute-start | bytes 786440 | tf_op jit(solution)/shard_map/ppermute | solution.py:201
  32.9 7.1 %collective-permute-start.3 = (f32[256,256]{1,0:T(8,128)S(1)}, f32[256,256]{1,0:T(8,128)S(1)}, u32[]{:S(2)}, u32[]{:S(2)}) collective-permute-start(f32[256,256]{1,0:T(8,128)S(1)} %get-tuple-element.36), channel_id=1, source_target_pairs={{256,128},{0,1},{129,257},{385,386},{258,130},{2,3},{131,259},{387... | collective-permute-start | bytes 786440 | tf_op jit(solution)/shard_map/ppermute | solution.py:200
  36.2 7.4 %collective-permute-start.4 = (f32[256,256]{1,0:T(8,128)S(1)}, f32[256,256]{1,0:T(8,128)S(1)}, u32[]{:S(2)}, u32[]{:S(2)}) collective-permute-start(f32[256,256]{1,0:T(8,128)S(1)} %get-tuple-element.37), channel_id=1, source_target_pairs={{384,256},{128,0},{1,129},{257,385},{386,258},{130,2},{3,131},{259... | collective-permute-start | bytes 786440 | tf_op jit(solution)/shard_map/ppermute | solution.py:201
  60.7 9.1 %collective-permute-start.5 = (f32[512,512]{1,0:T(8,128)S(1)}, f32[512,512]{1,0:T(8,128)S(1)}, u32[]{:S(2)}, u32[]{:S(2)}) collective-permute-start(f32[512,512]{1,0:T(8,128)S(1)} %bitcast.31), channel_id=1, source_target_pairs={{0,16},{16,0},{1,17},{17,1},{2,18},{18,2},{3,19},{19,3},{4,20},{20... | collective-permute-start | bytes 3145736 | tf_op jit(solution)/shard_map/ppermute | solution.py:351

commit v9 on v8

--- a/solution.py
+++ b/solution.py
@@ -18,7 +18,8 @@
 SPLIT = (("yl", 4), ("x", 4), ("c", 2), ("yh", 2), ("z", 8))
 VEC = ("yl", "x", "c")
 ROW = ("yh", "z")
-SUM = ("yl", "yh", "z")
+SUM = ("yh", "yl", "z")
+PLANE = ("yl", "yh", "z")
 
 TILE, LANES = 8, 128
 INTERPRET = False
@@ -33,7 +34,7 @@
 
 
 def snake():
-    nyl, nyh, nz = (lax.axis_size(a) for a in SUM)
+    nyl, nyh, nz = (lax.axis_size(a) for a in PLANE)
     places = []
     for yh in range(nyh):
         for z in range(nz):
@@ -47,7 +48,7 @@
     places = snake()
     nyl = lax.axis_size("yl")
     crossings = [(places[i - 1], places[i]) for i in range(nyl, len(places), nyl)]
-    crossed = lax.ppermute(coupling[-1], SUM, crossings)
+    crossed = lax.ppermute(coupling[-1], PLANE, crossings)
     part = coupling.shape[0] // nyl
     inside = lax.dynamic_index_in_dim(
         coupling, jnp.maximum(chunk * part - 1, 0), axis=0, keepdims=False
@@ -197,8 +198,8 @@
     )
     for turn in range(0, DEGREE, 2):
         scale = (1.0 if turn == 0 else 2.0) / filter_half
-        odd = lax.ppermute(odd, SUM, swaps[0])
-        even = lax.ppermute(even, SUM, swaps[1])
+        odd = lax.ppermute(odd, PLANE, swaps[0])
+        even = lax.ppermute(even, PLANE, swaps[1])
         around = scale * dot(
             dot(y[:, :size], below, ((1,), (1,))), below, ((1,), (0,))
         )
@@ -295,9 +296,16 @@
         mixing = jnp.concatenate(columns, axis=1)
         result = result - product(split(mixing), split(ref[...]), ((1,), (0,)))
     rows = group // count
-    for i, to in enumerate(in_rank_order(flags, count)):
-        to = pl.multiple_of(to * rows, rows)
-        out_ref[pl.ds(to, rows), :] = result[i * rows : (i + 1) * rows, :]
+    reverse = flags[2] == 1
+    for holds, order in (
+        (reverse, range(count - 1, -1, -1)),
+        (jnp.logical_not(reverse), range(count)),
+    ):
+
+        @pl.when(holds)
+        def _(order=order):
+            for i, to in enumerate(order):
+                out_ref[to * rows : (to + 1) * rows, :] = result[i * rows : (i + 1) * rows, :]
 
 
 def call(kernel, out_shapes, scalars, *arrays):
@@ -325,7 +333,7 @@
 
     def exchange_chunks(a):
         return lax.all_to_all(
-            a, SUM, split_axis=0, concat_axis=0, axis_index_groups=groups, tiled=True
+            a, PLANE, split_axis=0, concat_axis=0, axis_index_groups=groups, tiled=True
         )
 
     yl = lax.axis_index("yl")

time: 144 us -> 144 us (level)
    all_to_all x1, blocking collectives: 8.72 us -> 10.4 us  [exchange_chunks(): lax.all_to_all(a, PLANE, split_axis=0, concat_axis=0, axis_index_groups=g...]
    all_to_all x2, blocking collectives: 59.9 us -> 58.4 us  [exchange(): lax.all_to_all(a, SUM, split_axis=0, concat_axis=0, tiled=True)]
where the time goes in v9:
time: 144 us; the launch traced here: 142 us
  blocking collectives  84.4 us (59%)
  starting transfers between devices  26.1 us (18%)
  waiting for transfers between devices  9.34 us (6%)
  local copies, waits for them, and re-layouts  9.11 us (6%)
  Pallas kernels  7.85 us (5%)
  matrix products  2.96 us (2%)
  other arithmetic  1.77 us (1%)
    all_to_all x2, blocking collectives, exchange(): lax.all_to_all(a, SUM, split_axis=0, concat_axis=0, tiled=True)  58.4 us
    all_to_all x1, blocking collectives, local(): near = lax.all_to_all(copies, 'x', split_axis=0, concat_axis=0, tiled=True)  15.6 us
    all_to_all x1, blocking collectives, exchange_chunks(): lax.all_to_all(a, PLANE, split_axis=0, concat_axis=0, axis_index_groups=g...  10.4 us
    pallas_call x8, Pallas kernels, call(): pl.pallas_call(kernel, out_shape=out_shapes, in_specs=[smem] * len(scalar...  7.85 us
    all_to_all x1, starting transfers between devices, exchange_chunks(): lax.all_to_all(a, PLANE, split_axis=0, concat_axis=0, axis_index_groups=g...  7.52 us
    ppermute x1, starting transfers between devices, local(): far = lax.ppermute(near, 'c', [(0, 1), (1, 0)])  6.83 us
    ppermute x2, waiting for transfers between devices, chebyshev(): even = lax.ppermute(even, PLANE, swaps[1])  5.9 us
    ppermute x2, starting transfers between devices, chebyshev(): odd = lax.ppermute(odd, PLANE, swaps[0])  5.3 us
  transfers between devices with their start and end apart: 7, of which 5 were waited for; matrix products, arithmetic and copies ran while one was open for 6% of the time, Pallas kernels for 1%

profile of v9, /device:TPU:1, one launch (start us, length us, event | category | flops | bytes accessed | tf_op | source)
XLA Modules:
  0.0 141.7 jit_solution(7805411706204187895)
XLA Ops:
  0.0 0.0 copy-start
  0.0 1.8 %copy.13 = f32[4,4,8,512]{3,2,0,1:T(8,128)} copy(f32[4,4,8,512]{3,2,1,0:T(8,128)} %bitcast.41) | data formatting | bytes 524288 | tf_op jit(solution)/shard_map/reshape | solution.py:342
  1.8 7.5 %all-to-all-start = ((f32[4,32,512]{2,1,0:T(8,128)}), f32[4,32,512]{2,1,0:T(8,128)S(1)}, u32[]{:S(2)}, u32[]{:S(2)}) async-start(f32[4,32,512]{2,1,0:T(8,128)} %bitcast.30), calls=%async_computation | async-start | bytes 524288 | tf_op jit(solution)/shard_map/all_to_all | solution.py:335
  9.3 1.7 %slice_bitcast_fusion = f32[256,256]{1,0:T(8,128)} fusion(f32[8,256,256]{2,1,0:T(8,128)} %param.4), kind=kLoop, calls=%fused_computation.3 | loop fusion | bytes 524288 | tf_op jit(solution)/shard_map/squeeze | solution.py:51
  11.0 2.6 %collective-permute-start.2 = (f32[256,256]{1,0:T(8,128)}, f32[256,256]{1,0:T(8,128)}, u32[]{:S(2)}, u32[]{:S(2)}) collective-permute-start(f32[256,256]{1,0:T(8,128)} %slice_bitcast_fusion), channel_id=1, source_target_pairs={{0,1},{385,386},{2,3},{387,388},{4,5},{389,390},{6,7},{391,8},{392... | collective-permute-start | bytes 786440 | tf_op jit(solution)/shard_map/ppermute | solution.py:51
  13.6 1.9 %constant_dynamic-slice_fusion.c_ref = f32[2,256,256]{2,1,0:T(8,128)} fusion(f32[8,256,256]{2,1,0:T(8,128)} %param.4, s32[]{:T(128)S(6)} %select_n.31), kind=kLoop, calls=%fused_computation.8 | loop fusion | bytes 1048580 | tf_op jit(solution)/shard_map/dynamic_slice | solution.py:347
  15.5 0.0 copy-done
  15.5 0.8 constant_dynamic-slice_fusion.1.d_ref
  16.3 0.0 copy-start.1
  16.3 1.0 copy-done.1
  17.4 0.0 copy-start.2
  17.4 1.0 copy-done.2
  18.4 0.2 shard_map.37
  18.6 0.1 pad_add_fusion.flags
  18.6 0.0 collective-permute-done.2
  18.6 1.7 %bitcast_select_fusion = f32[256,256]{1,0:T(8,128)} fusion(f32[256,256]{1,0:T(8,128)} %collective-permute-done.2, f32[8,256,256]{2,1,0:T(8,128)} %param.4, s32[]{:T(128)S(6)} %max.3, pred[]{:T(512)S(6)} %eq.18), kind=kLoop, calls=%fused_computation.2 | loop fusion | flops 65536 | bytes 786437 | tf_op jit(solution)/shard_map/jit(_where)/select_n | solution.py:56
  20.3 0.0 all-to-all-done
  20.3 0.0 copy-start.3
  20.3 1.2 shard_map.38
  21.5 2.0 %collective-permute-start = (f32[256,256]{1,0:T(8,128)S(1)}, f32[256,256]{1,0:T(8,128)S(1)}, u32[]{:S(2)}, u32[]{:S(2)}) collective-permute-start(f32[256,256]{1,0:T(8,128)S(1)} %get-tuple-element.31), channel_id=1, source_target_pairs={{256,128},{0,1},{129,257},{385,386},{258,130},{2,3},{131,259},{387... | collective-permute-start | bytes 786440 | tf_op jit(solution)/shard_map/ppermute | solution.py:201
  23.5 1.9 %collective-permute-start.1 = (f32[256,256]{1,0:T(8,128)S(1)}, f32[256,256]{1,0:T(8,128)S(1)}, u32[]{:S(2)}, u32[]{:S(2)}) collective-permute-start(f32[256,256]{1,0:T(8,128)S(1)} %get-tuple-element.32), channel_id=1, source_target_pairs={{384,256},{128,0},{1,129},{257,385},{386,258},{130,2},{3,131},{259... | collective-permute-start | bytes 786440 | tf_op jit(solution)/shard_map/ppermute | solution.py:202
  25.4 1.2 fusion.2
  26.7 1.2 fusion.4.around_ref
  27.9 0.8 collective-permute-done.got_odd
  28.6 2.3 %collective-permute-done.1.got_even = f32[256,256]{1,0:T(8,128)S(1)} collective-permute-done((f32[256,256]{1,0:T(8,128)S(1)}, f32[256,256]{1,0:T(8,128)S(1)}, u32[]{:S(2)}, u32[]{:S(2)}) %collective-permute-start.1) | collective-permute-done | bytes 262176 | tf_op jit(solution)/shard_map/ppermute | solution.py:202
  30.9 2.0 %shard_map.39 = (f32[128,512]{1,0:T(8,128)S(1)}, f32[128,512]{1,0:T(8,128)S(1)}, f32[256,256]{1,0:T(8,128)S(1)}, f32[256,256]{1,0:T(8,128)S(1)}, f32[128,256]{1,0:T(8,128)S(1)}) custom-call(s32[3]{0:T(128)S(1)} %pad_add_fusion.flags, f32[128,512]{1,0:T(8,128)S(1)} %get-tuple-element.29.y_ref, f32[128,512]{1,0:T(8,128)S(1)} %get-tuple-element.30.a_ref, ...), custom_call_target="tpu_custom_call" | custom-call | tf_op jit(solution)/shard_map/pallas_call | solution.py:314
  32.9 3.3 %collective-permute-start.3 = (f32[256,256]{1,0:T(8,128)S(1)}, f32[256,256]{1,0:T(8,128)S(1)}, u32[]{:S(2)}, u32[]{:S(2)}) collective-permute-start(f32[256,256]{1,0:T(8,128)S(1)} %get-tuple-element.36), channel_id=1, source_target_pairs={{256,128},{0,1},{129,257},{385,386},{258,130},{2,3},{131,259},{387... | collective-permute-start | bytes 786440 | tf_op jit(solution)/shard_map/ppermute | solution.py:201
  36.2 1.9 %collective-permute-start.4 = (f32[256,256]{1,0:T(8,128)S(1)}, f32[256,256]{1,0:T(8,128)S(1)}, u32[]{:S(2)}, u32[]{:S(2)}) collective-permute-start(f32[256,256]{1,0:T(8,128)S(1)} %get-tuple-element.37), channel_id=1, source_target_pairs={{384,256},{128,0},{1,129},{257,385},{386,258},{130,2},{3,131},{259... | collective-permute-start | bytes 786440 | tf_op jit(solution)/shard_map/ppermute | solution.py:202
  38.1 0.0 copy-done.3
  38.1 0.3 fusion
  38.5 0.2 convolution_multiply_fusion.around_ref
  38.7 1.3 collective-permute-done.3.got_odd
  40.0 3.6 %collective-permute-done.4.got_even = f32[256,256]{1,0:T(8,128)S(1)} collective-permute-done((f32[256,256]{1,0:T(8,128)S(1)}, f32[256,256]{1,0:T(8,128)S(1)}, u32[]{:S(2)}, u32[]{:S(2)}) %collective-permute-start.4) | collective-permute-done | bytes 262176 | tf_op jit(solution)/shard_map/ppermute | solution.py:202
  43.6 1.4 shard_map.40.own_ref
  45.0 0.1 broadcast_in_dim.2
  45.2 15.6 %all_to_all.33 = f32[4,128,512]{2,1,0:T(8,128)S(1)} all-to-all(f32[4,128,512]{2,1,0:T(8,128)S(1)} %broadcast_in_dim.2), channel_id=1, replica_groups=mesh['yl'=4,'x'=4,'c'=2,'yh'=2,'z'=8] {'x'}, dimensions={0} | all-to-all | bytes 2097152 | tf_op jit(solution)/shard_map/all_to_all | solution.py:357
  60.7 6.8 %collective-permute-start.5 = (f32[512,512]{1,0:T(8,128)S(1)}, f32[512,512]{1,0:T(8,128)S(1)}, u32[]{:S(2)}, u32[]{:S(2)}) collective-permute-start(f32[512,512]{1,0:T(8,128)S(1)} %bitcast.31), channel_id=1, source_target_pairs={{0,16},{16,0},{1,17},{17,1},{2,18},{18,2},{3,19},{19,3},{4,20},{20... | collective-permute-start | bytes 3145736 | tf_op jit(solution)/shard_map/ppermute | solution.py:359
  67.6 0.9 shard_map.41
  68.5 1.4 collective-permute-done.5.far_ref
  69.8 0.9 shard_map.42
  70.7 34.0 %all_to_all.34 = f32[64,1,2176]{2,1,0:T(1,128)S(1)} all-to-all(f32[64,1,2176]{2,1,0:T(1,128)S(1)} %bitcast.35), channel_id=1, replica_groups=mesh['yl'=4,'x'=4,'c'=2,'yh'=2,'z'=8] {'yh','yl','z'}, dimensions={0} | all-to-all | bytes 1114112 | tf_op jit(solution)/shard_map/all_to_all | solution.py:368
  104.7 0.1 shard_map.43
  104.8 24.4 %all_to_all.35 = f32[64,1,2176]{2,1,0:T(1,128)S(1)} all-to-all(f32[64,1,2176]{2,1,0:T(1,128)S(1)} %bitcast.37), channel_id=1, replica_groups=mesh['yl'=4,'x'=4,'c'=2,'yh'=2,'z'=8] {'yh','yl','z'}, dimensions={0} | all-to-all | bytes 1114112 | tf_op jit(solution)/shard_map/all_to_all | solution.py:368
  129.2 1.3 shard_map.44
  130.5 10.4 %all_to_all.36 = f32[4,32,512]{2,1,0:T(8,128)S(1)} all-to-all(f32[4,32,512]{2,1,0:T(8,128)S(1)} %bitcast.39), channel_id=1, replica_groups={{384,256,128,0},{1,129,257,385},{386,258,130,2},{3,131,259,387},{388,26..., dimensions={0} | all-to-all | bytes 524288 | tf_op jit(solution)/shard_map/all_to_all | solution.py:335
  140.9 0.7 copy.11
Async XLA Ops:
  0.0 15.5 %copy-start = (f32[8,256,256]{2,1,0:T(8,128)S(1)}, f32[8,256,256]{2,1,0:T(8,128)}, u32[]{:S(2)}) copy-start(f32[8,256,256]{2,1,0:T(8,128)} %param.3) | copy-start | bytes 6291460
  1.8 18.5 %all-to-all-start = ((f32[4,32,512]{2,1,0:T(8,128)}), f32[4,32,512]{2,1,0:T(8,128)S(1)}, u32[]{:S(2)}, u32[]{:S(2)}) async-start(f32[4,32,512]{2,1,0:T(8,128)} %bitcast.30), calls=%async_computation | async-start | bytes 524288 | tf_op jit(solution)/shard_map/all_to_all | solution.py:335
  11.0 7.6 %collective-permute-start.2 = (f32[256,256]{1,0:T(8,128)}, f32[256,256]{1,0:T(8,128)}, u32[]{:S(2)}, u32[]{:S(2)}) collective-permute-start(f32[256,256]{1,0:T(8,128)} %slice_bitcast_fusion), channel_id=1, source_target_pairs={{0,1},{385,386},{2,3},{387,388},{4,5},{389,390},{6,7},{391,8},{392... | collective-permute-start | bytes 786440 | tf_op jit(solution)/shard_map/ppermute | solution.py:51
  16.3 1.0 copy-start.1
  17.4 1.0 copy-start.2
  20.3 17.8 %copy-start.3 = (f32[256,256]{1,0:T(8,128)S(1)}, f32[256,256]{1,0:T(8,128)}, u32[]{:S(2)}) copy-start(f32[256,256]{1,0:T(8,128)} %bitcast_select_fusion) | copy-start | bytes 786436
  21.5 7.1 %collective-permute-start = (f32[256,256]{1,0:T(8,128)S(1)}, f32[256,256]{1,0:T(8,128)S(1)}, u32[]{:S(2)}, u32[]{:S(2)}) collective-permute-start(f32[256,256]{1,0:T(8,128)S(1)} %get-tuple-element.31), channel_id=1, source_target_pairs={{256,128},{0,1},{129,257},{385,386},{258,130},{2,3},{131,259},{387... | collective-permute-start | bytes 786440 | tf_op jit(solution)/shard_map/ppermute | solution.py:201
  23.5 7.4 %collective-permute-start.1 = (f32[256,256]{1,0:T(8,128)S(1)}, f32[256,256]{1,0:T(8,128)S(1)}, u32[]{:S(2)}, u32[]{:S(2)}) collective-permute-start(f32[256,256]{1,0:T(8,128)S(1)} %get-tuple-element.32), channel_id=1, source_target_pairs={{384,256},{128,0},{1,129},{257,385},{386,258},{130,2},{3,131},{259... | collective-permute-start | bytes 786440 | tf_op jit(solution)/shard_map/ppermute | solution.py:202
  32.9 7.1 %collective-permute-start.3 = (f32[256,256]{1,0:T(8,128)S(1)}, f32[256,256]{1,0:T(8,128)S(1)}, u32[]{:S(2)}, u32[]{:S(2)}) collective-permute-start(f32[256,256]{1,0:T(8,128)S(1)} %get-tuple-element.36), channel_id=1, source_target_pairs={{256,128},{0,1},{129,257},{385,386},{258,130},{2,3},{131,259},{387... | collective-permute-start | bytes 786440 | tf_op jit(solution)/shard_map/ppermute | solution.py:201
  36.2 7.4 %collective-permute-start.4 = (f32[256,256]{1,0:T(8,128)S(1)}, f32[256,256]{1,0:T(8,128)S(1)}, u32[]{:S(2)}, u32[]{:S(2)}) collective-permute-start(f32[256,256]{1,0:T(8,128)S(1)} %get-tuple-element.37), channel_id=1, source_target_pairs={{384,256},{128,0},{1,129},{257,385},{386,258},{130,2},{3,131},{259... | collective-permute-start | bytes 786440 | tf_op jit(solution)/shard_map/ppermute | solution.py:202
  60.7 9.1 %collective-permute-start.5 = (f32[512,512]{1,0:T(8,128)S(1)}, f32[512,512]{1,0:T(8,128)S(1)}, u32[]{:S(2)}, u32[]{:S(2)}) collective-permute-start(f32[512,512]{1,0:T(8,128)S(1)} %bitcast.31), channel_id=1, source_target_pairs={{0,16},{16,0},{1,17},{17,1},{2,18},{18,2},{3,19},{19,3},{4,20},{20... | collective-permute-start | bytes 3145736 | tf_op jit(solution)/shard_map/ppermute | solution.py:359

commit v10 on v7

--- a/solution.py
+++ b/solution.py
@@ -18,7 +18,8 @@
 SPLIT = (("yl", 4), ("x", 4), ("c", 2), ("yh", 2), ("z", 8))
 VEC = ("yl", "x", "c")
 ROW = ("yh", "z")
-SUM = ("yl", "yh", "z")
+SUM = ("yh", "yl", "z")
+PLANE = ("yl", "yh", "z")
 
 TILE, LANES = 8, 128
 INTERPRET = False
@@ -33,7 +34,7 @@
 
 
 def snake():
-    nyl, nyh, nz = (lax.axis_size(a) for a in SUM)
+    nyl, nyh, nz = (lax.axis_size(a) for a in PLANE)
     places = []
     for yh in range(nyh):
         for z in range(nz):
@@ -47,7 +48,7 @@
     places = snake()
     nyl = lax.axis_size("yl")
     crossings = [(places[i - 1], places[i]) for i in range(nyl, len(places), nyl)]
-    crossed = lax.ppermute(coupling[-1], SUM, crossings)
+    crossed = lax.ppermute(coupling[-1], PLANE, crossings)
     part = coupling.shape[0] // nyl
     inside = lax.dynamic_index_in_dim(
         coupling, jnp.maximum(chunk * part - 1, 0), axis=0, keepdims=False
@@ -64,7 +65,9 @@
     def one(x, y):
         return lax.dot_general(x, y, (contract, ((), ())), preferred_element_type=jnp.float32)
 
-    return one(a[0], b[0]) + (one(a[0], b[1]) + one(a[1], b[0]))
+    rows = a[0].shape[0]
+    both = one(jnp.concatenate(a), b[0])
+    return both[:rows] + (both[rows:] + one(a[0], b[1]))
 
 
 def blocks_of(ref, size):
@@ -74,7 +77,7 @@
 def local_terms(y, parts, diagonal, coupling):
     terms = []
     for n, block in enumerate(y):
-        term = product(parts[n], diagonal(n), ((1,), (1,))) - filter_center * block
+        term = product(parts[n], diagonal(n), ((1,), (0,))) - filter_center * block
         if n + 1 < len(y):
             term = term + product(parts[n + 1], coupling(n), ((1,), (1,)))
         if n > 0:
@@ -182,8 +185,8 @@
     )
     for turn in range(0, DEGREE, 2):
         scale = (1.0 if turn == 0 else 2.0) / filter_half
-        odd = lax.ppermute(odd, SUM, swaps[0])
-        even = lax.ppermute(even, SUM, swaps[1])
+        odd = lax.ppermute(odd, PLANE, swaps[0])
+        even = lax.ppermute(even, PLANE, swaps[1])
         around = scale * dot(
             dot(y[:, :size], below, ((1,), (1,))), below, ((1,), (0,))
         )

time: 144 us -> 144 us (level)
    all_to_all x1, blocking collectives: 9.76 us -> 11.5 us  [local(): back = lax.all_to_all(back, 'yl', split_axis=0, concat_axis=0, tiled=True)]
  transfers between devices with their start and end apart: 7 -> 7, of which waited for: 5 -> 5; matrix products, arithmetic and copies ran while one was open for 5% -> 5% of each run, Pallas kernels for 1% -> 0%
where the time goes in v10:
time: 144 us; the launch traced here: 143 us
  blocking collectives  90.8 us (63%)
  starting transfers between devices  27.8 us (19%)
  waiting for transfers between devices  7.89 us (5%)
  Pallas kernels  7.05 us (5%)
  local copies, waits for them, and re-layouts  4.72 us (3%)
  matrix products  2.96 us (2%)
  other arithmetic  1.79 us (1%)
    all_to_all x2, blocking collectives, exchange(): lax.all_to_all(a, SUM, split_axis=0, concat_axis=0, tiled=True)  62.5 us
    all_to_all x1, blocking collectives, local(): near = lax.all_to_all(copies, 'x', split_axis=0, concat_axis=0, tiled=True)  16.9 us
    all_to_all x1, blocking collectives, local(): back = lax.all_to_all(back, 'yl', split_axis=0, concat_axis=0, tiled=True)  11.5 us
    ppermute x2, starting transfers between devices, chebyshev(): even = lax.ppermute(even, PLANE, swaps[1])  10.4 us
    all_to_all x1, starting transfers between devices, local(): own = lax.all_to_all(chunks, 'yl', split_axis=0, concat_axis=0, tiled=True)  9.18 us
    pallas_call x7, Pallas kernels, call(): pl.pallas_call(kernel, out_shape=out_shapes, in_specs=[smem] * len(scalar...  6.23 us
    ppermute x2, starting transfers between devices, chebyshev(): odd = lax.ppermute(odd, PLANE, swaps[0])  5.01 us
    ppermute x2, waiting for transfers between devices, chebyshev(): even = lax.ppermute(even, PLANE, swaps[1])  3.81 us
  transfers between devices with their start and end apart: 7, of which 5 were waited for; matrix products, arithmetic and copies ran while one was open for 5% of the time, Pallas kernels for 0%

profile of v10, /device:TPU:8, one launch (start us, length us, event | category | flops | bytes accessed | tf_op | source)
XLA Modules:
  0.0 143.2 jit_solution(15792996692066761617)
XLA Ops:
  0.0 0.0 copy-start
  0.0 0.0 copy-start.1
  0.0 1.1 copy-done.1
  1.1 0.8 spread.1
  1.9 9.2 %all-to-all-start = ((f32[4,32,512]{2,1,0:T(8,128)}), f32[4,32,512]{2,1,0:T(8,128)S(1)}, u32[]{:S(2)}, u32[]{:S(2)}) async-start(f32[4,32,512]{2,1,0:T(8,128)} %spread.1), calls=%async_computation | async-start | bytes 524288 | tf_op jit(solution)/shard_map/all_to_all | solution.py:342
  11.1 1.7 %slice_bitcast_fusion = f32[256,256]{1,0:T(8,128)} fusion(f32[8,256,256]{2,1,0:T(8,128)} %param.4), kind=kLoop, calls=%fused_computation.4 | loop fusion | bytes 524288 | tf_op jit(solution)/shard_map/squeeze | solution.py:51
  12.8 1.4 collective-permute-start.2
  14.1 1.1 constant_dynamic-slice_fusion.c_ref
  15.2 0.1 pad_add_fusion.flags
  15.3 0.0 copy-done
  15.4 0.0 collective-permute-done.2
  15.4 1.7 %bitcast_select_fusion = f32[256,256]{1,0:T(8,128)} fusion(f32[256,256]{1,0:T(8,128)} %collective-permute-done.2, f32[8,256,256]{2,1,0:T(8,128)} %param.4, s32[]{:T(128)S(6)} %max.3, pred[]{:T(512)S(6)} %eq.18), kind=kLoop, calls=%fused_computation.3 | loop fusion | flops 65536 | bytes 786437 | tf_op jit(solution)/shard_map/jit(_where)/select_n | solution.py:56
  17.1 0.3 all-to-all-done
  17.3 0.0 copy-start.2
  17.3 1.2 shard_map.37
  18.5 3.1 %collective-permute-start = (f32[256,256]{1,0:T(8,128)S(1)}, f32[256,256]{1,0:T(8,128)S(1)}, u32[]{:S(2)}, u32[]{:S(2)}) collective-permute-start(f32[256,256]{1,0:T(8,128)S(1)} %get-tuple-element.25), channel_id=1, source_target_pairs={{256,128},{0,1},{129,257},{385,386},{258,130},{2,3},{131,259},{387... | collective-permute-start | bytes 786440 | tf_op jit(solution)/shard_map/ppermute | solution.py:188
  21.6 6.4 %collective-permute-start.1 = (f32[256,256]{1,0:T(8,128)S(1)}, f32[256,256]{1,0:T(8,128)S(1)}, u32[]{:S(2)}, u32[]{:S(2)}) collective-permute-start(f32[256,256]{1,0:T(8,128)S(1)} %get-tuple-element.26), channel_id=1, source_target_pairs={{384,256},{128,0},{1,129},{257,385},{386,258},{130,2},{3,131},{259... | collective-permute-start | bytes 786440 | tf_op jit(solution)/shard_map/ppermute | solution.py:189
  28.1 1.2 fusion.1
  29.3 1.2 fusion.5.around_ref
  30.5 0.0 collective-permute-done.got_odd
  30.5 1.9 %collective-permute-done.1.got_even = f32[256,256]{1,0:T(8,128)S(1)} collective-permute-done((f32[256,256]{1,0:T(8,128)S(1)}, f32[256,256]{1,0:T(8,128)S(1)}, u32[]{:S(2)}, u32[]{:S(2)}) %collective-permute-start.1) | collective-permute-done | bytes 262176 | tf_op jit(solution)/shard_map/ppermute | solution.py:189
  32.4 1.7 %shard_map.38 = (f32[128,512]{1,0:T(8,128)S(1)}, f32[128,512]{1,0:T(8,128)S(1)}, f32[256,256]{1,0:T(8,128)S(1)}, f32[256,256]{1,0:T(8,128)S(1)}, f32[128,256]{1,0:T(8,128)S(1)}) custom-call(s32[2]{0:T(128)S(1)} %pad_add_fusion.flags, f32[128,512]{1,0:T(8,128)S(1)} %bitcast.30, f32[128,512]{1,0:T(8,128)S(1)} %get-tuple-element.24.a_ref, ...), custom_call_target="tpu_custom_call" | custom-call | tf_op jit(solution)/shard_map/pallas_call | solution.py:321
  34.2 1.9 %collective-permute-start.3 = (f32[256,256]{1,0:T(8,128)S(1)}, f32[256,256]{1,0:T(8,128)S(1)}, u32[]{:S(2)}, u32[]{:S(2)}) collective-permute-start(f32[256,256]{1,0:T(8,128)S(1)} %get-tuple-element.34), channel_id=1, source_target_pairs={{256,128},{0,1},{129,257},{385,386},{258,130},{2,3},{131,259},{387... | collective-permute-start | bytes 786440 | tf_op jit(solution)/shard_map/ppermute | solution.py:188
  36.1 3.9 %collective-permute-start.4 = (f32[256,256]{1,0:T(8,128)S(1)}, f32[256,256]{1,0:T(8,128)S(1)}, u32[]{:S(2)}, u32[]{:S(2)}) collective-permute-start(f32[256,256]{1,0:T(8,128)S(1)} %get-tuple-element.35), channel_id=1, source_target_pairs={{384,256},{128,0},{1,129},{257,385},{386,258},{130,2},{3,131},{259... | collective-permute-start | bytes 786440 | tf_op jit(solution)/shard_map/ppermute | solution.py:189
  40.0 0.0 copy-done.2
  40.0 0.3 fusion.3
  40.3 0.2 convolution_multiply_fusion.around_ref
  40.6 1.8 %collective-permute-done.3.got_odd = f32[256,256]{1,0:T(8,128)S(1)} collective-permute-done((f32[256,256]{1,0:T(8,128)S(1)}, f32[256,256]{1,0:T(8,128)S(1)}, u32[]{:S(2)}, u32[]{:S(2)}) %collective-permute-start.3) | collective-permute-done | bytes 262176 | tf_op jit(solution)/shard_map/ppermute | solution.py:188
  42.4 1.9 %collective-permute-done.4.got_even = f32[256,256]{1,0:T(8,128)S(1)} collective-permute-done((f32[256,256]{1,0:T(8,128)S(1)}, f32[256,256]{1,0:T(8,128)S(1)}, u32[]{:S(2)}, u32[]{:S(2)}) %collective-permute-start.4) | collective-permute-done | bytes 262176 | tf_op jit(solution)/shard_map/ppermute | solution.py:189
  44.3 1.2 shard_map.39.own_ref
  45.5 0.1 broadcast_in_dim.2
  45.7 16.9 %all_to_all.33 = f32[4,128,512]{2,1,0:T(8,128)S(1)} all-to-all(f32[4,128,512]{2,1,0:T(8,128)S(1)} %broadcast_in_dim.2), channel_id=1, replica_groups=mesh['yl'=4,'x'=4,'c'=2,'yh'=2,'z'=8] {'x'}, dimensions={0} | all-to-all | bytes 2097152 | tf_op jit(solution)/shard_map/all_to_all | solution.py:355
  62.6 1.9 %collective-permute-start.5 = (f32[512,512]{1,0:T(8,128)S(1)}, f32[512,512]{1,0:T(8,128)S(1)}, u32[]{:S(2)}, u32[]{:S(2)}) collective-permute-start(f32[512,512]{1,0:T(8,128)S(1)} %bitcast.25), channel_id=1, source_target_pairs={{0,16},{16,0},{1,17},{17,1},{2,18},{18,2},{3,19},{19,3},{4,20},{20... | collective-permute-start | bytes 3145736 | tf_op jit(solution)/shard_map/ppermute | solution.py:357
  64.5 0.7 shard_map.40
  65.1 2.0 %collective-permute-done.5.far_ref = f32[512,512]{1,0:T(8,128)S(1)} collective-permute-done((f32[512,512]{1,0:T(8,128)S(1)}, f32[512,512]{1,0:T(8,128)S(1)}, u32[]{:S(2)}, u32[]{:S(2)}) %collective-permute-start.5) | collective-permute-done | bytes 1048608 | tf_op jit(solution)/shard_map/ppermute | solution.py:357
  67.1 0.7 shard_map.41
  67.8 37.5 %all_to_all.34 = f32[64,1,2176]{2,1,0:T(1,128)S(1)} all-to-all(f32[64,1,2176]{2,1,0:T(1,128)S(1)} %bitcast.32), channel_id=1, replica_groups=mesh['yl'=4,'x'=4,'c'=2,'yh'=2,'z'=8] {'yh','yl','z'}, dimensions={0} | all-to-all | bytes 1114112 | tf_op jit(solution)/shard_map/all_to_all | solution.py:366
  105.3 0.1 shard_map.42
  105.4 25.0 %all_to_all.35 = f32[64,1,2176]{2,1,0:T(1,128)S(1)} all-to-all(f32[64,1,2176]{2,1,0:T(1,128)S(1)} %bitcast.34), channel_id=1, replica_groups=mesh['yl'=4,'x'=4,'c'=2,'yh'=2,'z'=8] {'yh','yl','z'}, dimensions={0} | all-to-all | bytes 1114112 | tf_op jit(solution)/shard_map/all_to_all | solution.py:366
  130.4 0.7 shard_map.43
  131.0 11.5 %all_to_all.36 = f32[4,32,512]{2,1,0:T(8,128)S(1)} all-to-all(f32[4,32,512]{2,1,0:T(8,128)S(1)} %bitcast.35), channel_id=1, replica_groups=mesh['yl'=4,'x'=4,'c'=2,'yh'=2,'z'=8] {'yl'}, dimensions={0} | all-to-all | bytes 524288 | tf_op jit(solution)/shard_map/all_to_all | solution.py:380
  142.5 0.7 copy.8
  (2 shorter events, 0.1 us)
Async XLA Ops:
  0.0 15.3 %copy-start = (f32[8,256,256]{2,1,0:T(8,128)S(1)}, f32[8,256,256]{2,1,0:T(8,128)}, u32[]{:S(2)}) copy-start(f32[8,256,256]{2,1,0:T(8,128)} %param.3) | copy-start | bytes 6291460
  0.0 1.1 copy-start.1
  1.9 15.4 %all-to-all-start = ((f32[4,32,512]{2,1,0:T(8,128)}), f32[4,32,512]{2,1,0:T(8,128)S(1)}, u32[]{:S(2)}, u32[]{:S(2)}) async-start(f32[4,32,512]{2,1,0:T(8,128)} %spread.1), calls=%async_computation | async-start | bytes 524288 | tf_op jit(solution)/shard_map/all_to_all | solution.py:342
  12.8 2.6 %collective-permute-start.2 = (f32[256,256]{1,0:T(8,128)}, f32[256,256]{1,0:T(8,128)}, u32[]{:S(2)}, u32[]{:S(2)}) collective-permute-start(f32[256,256]{1,0:T(8,128)} %slice_bitcast_fusion), channel_id=1, source_target_pairs={{0,1},{385,386},{2,3},{387,388},{4,5},{389,390},{6,7},{391,8},{392... | collective-permute-start | bytes 786440 | tf_op jit(solution)/shard_map/ppermute | solution.py:51
  17.3 22.7 %copy-start.2 = (f32[256,256]{1,0:T(8,128)S(1)}, f32[256,256]{1,0:T(8,128)}, u32[]{:S(2)}) copy-start(f32[256,256]{1,0:T(8,128)} %bitcast_select_fusion) | copy-start | bytes 786436
  18.5 12.0 %collective-permute-start = (f32[256,256]{1,0:T(8,128)S(1)}, f32[256,256]{1,0:T(8,128)S(1)}, u32[]{:S(2)}, u32[]{:S(2)}) collective-permute-start(f32[256,256]{1,0:T(8,128)S(1)} %get-tuple-element.25), channel_id=1, source_target_pairs={{256,128},{0,1},{129,257},{385,386},{258,130},{2,3},{131,259},{387... | collective-permute-start | bytes 786440 | tf_op jit(solution)/shard_map/ppermute | solution.py:188
  21.6 10.8 %collective-permute-start.1 = (f32[256,256]{1,0:T(8,128)S(1)}, f32[256,256]{1,0:T(8,128)S(1)}, u32[]{:S(2)}, u32[]{:S(2)}) collective-permute-start(f32[256,256]{1,0:T(8,128)S(1)} %get-tuple-element.26), channel_id=1, source_target_pairs={{384,256},{128,0},{1,129},{257,385},{386,258},{130,2},{3,131},{259... | collective-permute-start | bytes 786440 | tf_op jit(solution)/shard_map/ppermute | solution.py:189
  34.2 8.3 %collective-permute-start.3 = (f32[256,256]{1,0:T(8,128)S(1)}, f32[256,256]{1,0:T(8,128)S(1)}, u32[]{:S(2)}, u32[]{:S(2)}) collective-permute-start(f32[256,256]{1,0:T(8,128)S(1)} %get-tuple-element.34), channel_id=1, source_target_pairs={{256,128},{0,1},{129,257},{385,386},{258,130},{2,3},{131,259},{387... | collective-permute-start | bytes 786440 | tf_op jit(solution)/shard_map/ppermute | solution.py:188
  36.1 8.3 %collective-permute-start.4 = (f32[256,256]{1,0:T(8,128)S(1)}, f32[256,256]{1,0:T(8,128)S(1)}, u32[]{:S(2)}, u32[]{:S(2)}) collective-permute-start(f32[256,256]{1,0:T(8,128)S(1)} %get-tuple-element.35), channel_id=1, source_target_pairs={{384,256},{128,0},{1,129},{257,385},{386,258},{130,2},{3,131},{259... | collective-permute-start | bytes 786440 | tf_op jit(solution)/shard_map/ppermute | solution.py:189
  62.6 4.5 %collective-permute-start.5 = (f32[512,512]{1,0:T(8,128)S(1)}, f32[512,512]{1,0:T(8,128)S(1)}, u32[]{:S(2)}, u32[]{:S(2)}) collective-permute-start(f32[512,512]{1,0:T(8,128)S(1)} %bitcast.25), channel_id=1, source_target_pairs={{0,16},{16,0},{1,17},{17,1},{2,18},{18,2},{3,19},{19,3},{4,20},{20... | collective-permute-start | bytes 3145736 | tf_op jit(solution)/shard_map/ppermute | solution.py:357

commit v11 on v10

--- a/solution.py
+++ b/solution.py
@@ -161,7 +161,10 @@
     b[-1] = b[-1] + double * product(split(above_a), top, ((1,), (1,)))
     b[0] = b[0] + double * below_a
     b_ref[...] = jnp.concatenate(b, axis=1)
-    if next_ref is not None:
+    if odd_ref is None:
+        for i in range(next_ref.shape[0]):
+            next_ref[i] = jnp.concatenate(b, axis=1)
+    else:
         parts = [split(block) for block in b]
         terms = local_terms(b, parts, diagonal, coupling)
         a = [double * term - old for term, old in zip(terms, a)]
@@ -178,6 +181,7 @@
     rows, size = y.shape[0], diag_blocks.shape[1]
     message = jax.ShapeDtypeStruct((2 * rows, size), jnp.float32)
     panel = jax.ShapeDtypeStruct(y.shape, jnp.float32)
+    copies = jax.ShapeDtypeStruct((lax.axis_size("x"), *y.shape), jnp.float32)
     sends = [panel, message, message, jax.ShapeDtypeStruct((rows, size), jnp.float32)]
     halves = [jax.ShapeDtypeStruct(diag_blocks.shape, jnp.bfloat16)] * 4
     *hamiltonian, a, odd, even, term = call(
@@ -193,7 +197,7 @@
         final = turn + 2 >= DEGREE
         result = call(
             functools.partial(step_kernel, scale),
-            [panel] if final else [panel] + sends,
+            [panel, copies] if final else [panel] + sends,
             (flags,),
             y,
             a,
@@ -206,7 +210,7 @@
         y = result[0]
         if not final:
             a, odd, even, term = result[1:]
-    return y
+    return result
 
 
 def spread_kernel(flip, in_ref, out_ref, sems):
@@ -344,14 +348,13 @@
     is_top = (lax.axis_index(ROW) == lax.axis_size(ROW) - 1) & (chunk == nyl - 1)
     own_diag = lax.dynamic_slice_in_dim(diag_blocks, chunk * part, part)
     own_coupling = lax.dynamic_slice_in_dim(coupling, chunk * part, part)
-    own = chebyshev(
+    own, copies = chebyshev(
         own,
         own_diag,
         own_coupling,
         edge_coupling(coupling, chunk),
         jnp.stack([chunk % 2, is_top.astype(jnp.int32)]),
     )
-    copies = jnp.broadcast_to(own[None], (nx, group, depth))
     near = lax.all_to_all(copies, "x", split_axis=0, concat_axis=0, tiled=True)
     near = near.reshape(nx * group, depth)
     far = lax.ppermute(near, "c", [(0, 1), (1, 0)])

time: 144 us -> 144 us (level)
  no operation moved by 1% of the time
where the time goes in v11:
time: 144 us; the launch traced here: 143 us
  blocking collectives  90.8 us (63%)
  starting transfers between devices  27.8 us (19%)
  waiting for transfers between devices  7.87 us (5%)
  Pallas kernels  7.09 us (5%)
  local copies, waits for them, and re-layouts  4.61 us (3%)
  matrix products  2.96 us (2%)
  other arithmetic  1.8 us (1%)
    all_to_all x2, blocking collectives, exchange(): lax.all_to_all(a, SUM, split_axis=0, concat_axis=0, tiled=True)  62.5 us
    all_to_all x1, blocking collectives, local(): near = lax.all_to_all(copies, 'x', split_axis=0, concat_axis=0, tiled=True)  16.9 us
    all_to_all x1, blocking collectives, local(): back = lax.all_to_all(back, 'yl', split_axis=0, concat_axis=0, tiled=True)  11.5 us
    ppermute x2, starting transfers between devices, chebyshev(): even = lax.ppermute(even, PLANE, swaps[1])  10.3 us
    all_to_all x1, starting transfers between devices, local(): own = lax.all_to_all(chunks, 'yl', split_axis=0, concat_axis=0, tiled=True)  9.18 us
    pallas_call x7, Pallas kernels, call(): pl.pallas_call(kernel, out_shape=out_shapes, in_specs=[smem] * len(scalar...  6.27 us
    ppermute x2, starting transfers between devices, chebyshev(): odd = lax.ppermute(odd, PLANE, swaps[0])  5.03 us
    ppermute x2, waiting for transfers between devices, chebyshev(): even = lax.ppermute(even, PLANE, swaps[1])  3.81 us
  transfers between devices with their start and end apart: 7, of which 5 were waited for; matrix products, arithmetic and copies ran while one was open for 5% of the time, Pallas kernels for 0%

profile of v11, /device:TPU:8, one launch (start us, length us, event | category | flops | bytes accessed | tf_op | source)
XLA Modules:
  0.0 143.2 jit_solution(9800747258836778895)
XLA Ops:
  0.0 0.0 copy-start
  0.0 0.0 copy-start.1
  0.0 1.1 copy-done.1
  1.1 0.8 spread.1
  1.9 9.2 %all-to-all-start = ((f32[4,32,512]{2,1,0:T(8,128)}), f32[4,32,512]{2,1,0:T(8,128)S(1)}, u32[]{:S(2)}, u32[]{:S(2)}) async-start(f32[4,32,512]{2,1,0:T(8,128)} %spread.1), calls=%async_computation | async-start | bytes 524288 | tf_op jit(solution)/shard_map/all_to_all | solution.py:346
  11.1 1.7 %slice_bitcast_fusion = f32[256,256]{1,0:T(8,128)} fusion(f32[8,256,256]{2,1,0:T(8,128)} %param.4), kind=kLoop, calls=%fused_computation.4 | loop fusion | bytes 524288 | tf_op jit(solution)/shard_map/squeeze | solution.py:51
  12.8 1.4 collective-permute-start.2
  14.1 1.1 constant_dynamic-slice_fusion.c_ref
  15.2 0.1 pad_add_fusion.flags
  15.3 0.0 copy-done
  15.4 0.0 collective-permute-done.2
  15.4 1.7 %bitcast_select_fusion = f32[256,256]{1,0:T(8,128)} fusion(f32[256,256]{1,0:T(8,128)} %collective-permute-done.2, f32[8,256,256]{2,1,0:T(8,128)} %param.4, s32[]{:T(128)S(6)} %max.3, pred[]{:T(512)S(6)} %eq.18), kind=kLoop, calls=%fused_computation.3 | loop fusion | flops 65536 | bytes 786437 | tf_op jit(solution)/shard_map/jit(_where)/select_n | solution.py:56
  17.1 0.3 all-to-all-done
  17.3 0.0 copy-start.2
  17.3 1.2 shard_map.37
  18.5 3.1 %collective-permute-start = (f32[256,256]{1,0:T(8,128)S(1)}, f32[256,256]{1,0:T(8,128)S(1)}, u32[]{:S(2)}, u32[]{:S(2)}) collective-permute-start(f32[256,256]{1,0:T(8,128)S(1)} %get-tuple-element.27), channel_id=1, source_target_pairs={{256,128},{0,1},{129,257},{385,386},{258,130},{2,3},{131,259},{387... | collective-permute-start | bytes 786440 | tf_op jit(solution)/shard_map/ppermute | solution.py:192
  21.6 6.4 %collective-permute-start.1 = (f32[256,256]{1,0:T(8,128)S(1)}, f32[256,256]{1,0:T(8,128)S(1)}, u32[]{:S(2)}, u32[]{:S(2)}) collective-permute-start(f32[256,256]{1,0:T(8,128)S(1)} %get-tuple-element.28), channel_id=1, source_target_pairs={{384,256},{128,0},{1,129},{257,385},{386,258},{130,2},{3,131},{259... | collective-permute-start | bytes 786440 | tf_op jit(solution)/shard_map/ppermute | solution.py:193
  28.1 1.2 fusion.1
  29.3 1.2 fusion.5.around_ref
  30.5 0.0 collective-permute-done.got_odd
  30.5 1.9 %collective-permute-done.1.got_even = f32[256,256]{1,0:T(8,128)S(1)} collective-permute-done((f32[256,256]{1,0:T(8,128)S(1)}, f32[256,256]{1,0:T(8,128)S(1)}, u32[]{:S(2)}, u32[]{:S(2)}) %collective-permute-start.1) | collective-permute-done | bytes 262176 | tf_op jit(solution)/shard_map/ppermute | solution.py:193
  32.4 1.7 %shard_map.38 = (f32[128,512]{1,0:T(8,128)S(1)}, f32[128,512]{1,0:T(8,128)S(1)}, f32[256,256]{1,0:T(8,128)S(1)}, f32[256,256]{1,0:T(8,128)S(1)}, f32[128,256]{1,0:T(8,128)S(1)}) custom-call(s32[2]{0:T(128)S(1)} %pad_add_fusion.flags, f32[128,512]{1,0:T(8,128)S(1)} %bitcast.30, f32[128,512]{1,0:T(8,128)S(1)} %get-tuple-element.26.a_ref, ...), custom_call_target="tpu_custom_call" | custom-call | tf_op jit(solution)/shard_map/pallas_call | solution.py:325
  34.2 1.9 %collective-permute-start.3 = (f32[256,256]{1,0:T(8,128)S(1)}, f32[256,256]{1,0:T(8,128)S(1)}, u32[]{:S(2)}, u32[]{:S(2)}) collective-permute-start(f32[256,256]{1,0:T(8,128)S(1)} %get-tuple-element.36), channel_id=1, source_target_pairs={{256,128},{0,1},{129,257},{385,386},{258,130},{2,3},{131,259},{387... | collective-permute-start | bytes 786440 | tf_op jit(solution)/shard_map/ppermute | solution.py:192
  36.1 3.9 %collective-permute-start.4 = (f32[256,256]{1,0:T(8,128)S(1)}, f32[256,256]{1,0:T(8,128)S(1)}, u32[]{:S(2)}, u32[]{:S(2)}) collective-permute-start(f32[256,256]{1,0:T(8,128)S(1)} %get-tuple-element.37), channel_id=1, source_target_pairs={{384,256},{128,0},{1,129},{257,385},{386,258},{130,2},{3,131},{259... | collective-permute-start | bytes 786440 | tf_op jit(solution)/shard_map/ppermute | solution.py:193
  40.0 0.0 copy-done.2
  40.0 0.3 fusion.3
  40.3 0.2 convolution_multiply_fusion.around_ref
  40.6 1.8 %collective-permute-done.3.got_odd = f32[256,256]{1,0:T(8,128)S(1)} collective-permute-done((f32[256,256]{1,0:T(8,128)S(1)}, f32[256,256]{1,0:T(8,128)S(1)}, u32[]{:S(2)}, u32[]{:S(2)}) %collective-permute-start.3) | collective-permute-done | bytes 262176 | tf_op jit(solution)/shard_map/ppermute | solution.py:192
  42.4 1.9 %collective-permute-done.4.got_even = f32[256,256]{1,0:T(8,128)S(1)} collective-permute-done((f32[256,256]{1,0:T(8,128)S(1)}, f32[256,256]{1,0:T(8,128)S(1)}, u32[]{:S(2)}, u32[]{:S(2)}) %collective-permute-start.4) | collective-permute-done | bytes 262176 | tf_op jit(solution)/shard_map/ppermute | solution.py:193
  44.4 1.2 shard_map.39
  45.6 16.9 %all_to_all.33 = f32[4,128,512]{2,1,0:T(8,128)S(1)} all-to-all(f32[4,128,512]{2,1,0:T(8,128)S(1)} %get-tuple-element.40), channel_id=1, replica_groups=mesh['yl'=4,'x'=4,'c'=2,'yh'=2,'z'=8] {'x'}, dimensions={0} | all-to-all | bytes 2097152 | tf_op jit(solution)/shard_map/all_to_all | solution.py:358
  62.5 1.9 %collective-permute-start.5 = (f32[512,512]{1,0:T(8,128)S(1)}, f32[512,512]{1,0:T(8,128)S(1)}, u32[]{:S(2)}, u32[]{:S(2)}) collective-permute-start(f32[512,512]{1,0:T(8,128)S(1)} %bitcast.25), channel_id=1, source_target_pairs={{0,16},{16,0},{1,17},{17,1},{2,18},{18,2},{3,19},{19,3},{4,20},{20... | collective-permute-start | bytes 3145736 | tf_op jit(solution)/shard_map/ppermute | solution.py:360
  64.4 0.7 shard_map.40
  65.1 2.0 %collective-permute-done.5.far_ref = f32[512,512]{1,0:T(8,128)S(1)} collective-permute-done((f32[512,512]{1,0:T(8,128)S(1)}, f32[512,512]{1,0:T(8,128)S(1)}, u32[]{:S(2)}, u32[]{:S(2)}) %collective-permute-start.5) | collective-permute-done | bytes 1048608 | tf_op jit(solution)/shard_map/ppermute | solution.py:360
  67.0 0.7 shard_map.41
  67.7 37.5 %all_to_all.34 = f32[64,1,2176]{2,1,0:T(1,128)S(1)} all-to-all(f32[64,1,2176]{2,1,0:T(1,128)S(1)} %bitcast.32), channel_id=1, replica_groups=mesh['yl'=4,'x'=4,'c'=2,'yh'=2,'z'=8] {'yh','yl','z'}, dimensions={0} | all-to-all | bytes 1114112 | tf_op jit(solution)/shard_map/all_to_all | solution.py:369
  105.2 0.1 shard_map.42
  105.3 25.0 %all_to_all.35 = f32[64,1,2176]{2,1,0:T(1,128)S(1)} all-to-all(f32[64,1,2176]{2,1,0:T(1,128)S(1)} %bitcast.34), channel_id=1, replica_groups=mesh['yl'=4,'x'=4,'c'=2,'yh'=2,'z'=8] {'yh','yl','z'}, dimensions={0} | all-to-all | bytes 1114112 | tf_op jit(solution)/shard_map/all_to_all | solution.py:369
  130.3 0.7 shard_map.43
  130.9 11.5 %all_to_all.36 = f32[4,32,512]{2,1,0:T(8,128)S(1)} all-to-all(f32[4,32,512]{2,1,0:T(8,128)S(1)} %bitcast.35), channel_id=1, replica_groups=mesh['yl'=4,'x'=4,'c'=2,'yh'=2,'z'=8] {'yl'}, dimensions={0} | all-to-all | bytes 524288 | tf_op jit(solution)/shard_map/all_to_all | solution.py:383
  142.4 0.7 copy.8
  (2 shorter events, 0.1 us)
Async XLA Ops:
  0.0 15.3 %copy-start = (f32[8,256,256]{2,1,0:T(8,128)S(1)}, f32[8,256,256]{2,1,0:T(8,128)}, u32[]{:S(2)}) copy-start(f32[8,256,256]{2,1,0:T(8,128)} %param.3) | copy-start | bytes 6291460
  0.0 1.1 copy-start.1
  1.9 15.4 %all-to-all-start = ((f32[4,32,512]{2,1,0:T(8,128)}), f32[4,32,512]{2,1,0:T(8,128)S(1)}, u32[]{:S(2)}, u32[]{:S(2)}) async-start(f32[4,32,512]{2,1,0:T(8,128)} %spread.1), calls=%async_computation | async-start | bytes 524288 | tf_op jit(solution)/shard_map/all_to_all | solution.py:346
  12.8 2.6 %collective-permute-start.2 = (f32[256,256]{1,0:T(8,128)}, f32[256,256]{1,0:T(8,128)}, u32[]{:S(2)}, u32[]{:S(2)}) collective-permute-start(f32[256,256]{1,0:T(8,128)} %slice_bitcast_fusion), channel_id=1, source_target_pairs={{0,1},{385,386},{2,3},{387,388},{4,5},{389,390},{6,7},{391,8},{392... | collective-permute-start | bytes 786440 | tf_op jit(solution)/shard_map/ppermute | solution.py:51
  17.3 22.7 %copy-start.2 = (f32[256,256]{1,0:T(8,128)S(1)}, f32[256,256]{1,0:T(8,128)}, u32[]{:S(2)}) copy-start(f32[256,256]{1,0:T(8,128)} %bitcast_select_fusion) | copy-start | bytes 786436
  18.5 12.0 %collective-permute-start = (f32[256,256]{1,0:T(8,128)S(1)}, f32[256,256]{1,0:T(8,128)S(1)}, u32[]{:S(2)}, u32[]{:S(2)}) collective-permute-start(f32[256,256]{1,0:T(8,128)S(1)} %get-tuple-element.27), channel_id=1, source_target_pairs={{256,128},{0,1},{129,257},{385,386},{258,130},{2,3},{131,259},{387... | collective-permute-start | bytes 786440 | tf_op jit(solution)/shard_map/ppermute | solution.py:192
  21.6 10.8 %collective-permute-start.1 = (f32[256,256]{1,0:T(8,128)S(1)}, f32[256,256]{1,0:T(8,128)S(1)}, u32[]{:S(2)}, u32[]{:S(2)}) collective-permute-start(f32[256,256]{1,0:T(8,128)S(1)} %get-tuple-element.28), channel_id=1, source_target_pairs={{384,256},{128,0},{1,129},{257,385},{386,258},{130,2},{3,131},{259... | collective-permute-start | bytes 786440 | tf_op jit(solution)/shard_map/ppermute | solution.py:193
  34.2 8.3 %collective-permute-start.3 = (f32[256,256]{1,0:T(8,128)S(1)}, f32[256,256]{1,0:T(8,128)S(1)}, u32[]{:S(2)}, u32[]{:S(2)}) collective-permute-start(f32[256,256]{1,0:T(8,128)S(1)} %get-tuple-element.36), channel_id=1, source_target_pairs={{256,128},{0,1},{129,257},{385,386},{258,130},{2,3},{131,259},{387... | collective-permute-start | bytes 786440 | tf_op jit(solution)/shard_map/ppermute | solution.py:192
  36.1 8.3 %collective-permute-start.4 = (f32[256,256]{1,0:T(8,128)S(1)}, f32[256,256]{1,0:T(8,128)S(1)}, u32[]{:S(2)}, u32[]{:S(2)}) collective-permute-start(f32[256,256]{1,0:T(8,128)S(1)} %get-tuple-element.37), channel_id=1, source_target_pairs={{384,256},{128,0},{1,129},{257,385},{386,258},{130,2},{3,131},{259... | collective-permute-start | bytes 786440 | tf_op jit(solution)/shard_map/ppermute | solution.py:193
  62.5 4.5 %collective-permute-start.5 = (f32[512,512]{1,0:T(8,128)S(1)}, f32[512,512]{1,0:T(8,128)S(1)}, u32[]{:S(2)}, u32[]{:S(2)}) collective-permute-start(f32[512,512]{1,0:T(8,128)S(1)} %bitcast.25), channel_id=1, source_target_pairs={{0,16},{16,0},{1,17},{17,1},{2,18},{18,2},{3,19},{19,3},{4,20},{20... | collective-permute-start | bytes 3145736 | tf_op jit(solution)/shard_map/ppermute | solution.py:360
